TPU v7x, 128 devices: a whole 4x4x4 slice. The times are simulated.
128 devices in a mesh: mem: 2 (over core), state: 64 (over y, x, z).
Axes of the slice: x: 4, y: 4, z: 4, core: 2. Of those that a mesh axis runs over, the one named last changes fastest.
Arguments:
- background_ensemble: bfloat16 [80, 4194304], P('mem', 'state'), may hold values from -6 to 6
- measured_segment_index: int32 [2, 256], replicated, may hold values from 0 to 127
- measured_place_within_segment: int32 [2, 256], replicated, may hold values from 0 to 32767
- measured_readings: float32 [2, 256], replicated, may hold values from -6 to 6
- measured_noise_spread: float32 [2, 256], replicated, may hold values from 0.25 to 4
- measured_damping_weight: float32 [2, 256], replicated, may hold values from 0.3 to 1
- measured_cutoff_extent: int32 [2, 256], replicated, may hold values from 1 to 1024
Outputs:
- analysis: bfloat16 [80, 4194304], P('mem', 'state')
Inputs may be any that keep to these rules, and one draw needn't show every extreme that they name: measured_segment_index numbers the blocks of 32768 state values in the order of the state dimension. measured_place_within_segment is a position inside the owner's block.
All inputs are finite; a program needn't handle non-finite values.
Results may differ from a plain program's by a relative error of at most 0.0051.
Values may be sent and summed in bfloat16 or wider, within the bound.
No kernel may reach another device: no remote copies, remote signals or barrier semaphores. Data moves between devices by JAX's collectives and lax.ppermute only.
A program may use at most 64 MiB of HBM per device.

v0:
```python
import jax
import jax.numpy as jnp
from jax import lax
from jax.sharding import Mesh
from jax.sharding import PartitionSpec as P

ENSEMBLE_COUNT = 80
SD = 32768
B = 2
LB = 128
BLK = 4096
STATE = ("state_0", "state_1", "state_2")


def split_up(array, dim, size):
    dims = array.shape
    blocks = array.reshape(*dims[:dim], size, dims[dim] // size, *dims[dim + 1 :])
    return jnp.moveaxis(blocks, dim, 0)


def sum_at_owner(array, axis, dim):
    blocks = split_up(array, dim, lax.axis_size(axis))
    arrived = lax.all_to_all(blocks, axis, split_axis=0, concat_axis=0, tiled=True)
    return arrived.sum(axis=0)


def summed_rows(array, axes, dim):
    far, near = axes
    own = sum_at_owner(split_up(array, dim, lax.axis_size(far)), near, dim + 1)
    return jnp.sum(lax.all_to_all(own, far, 0, 0, tiled=True), axis=0)


def filled_up(lines, size):
    spare = -lines.shape[0] % size
    if not spare:
        return lines
    return jnp.concatenate([lines, jnp.zeros((spare, *lines.shape[1:]), lines.dtype)])


def sent_to_all(array, axis):
    size = lax.axis_size(axis)
    return lax.all_to_all(
        jnp.broadcast_to(array[None], (size, *array.shape)), axis, 0, 0, tiled=True
    )


def joined_along(blocks, dim):
    blocks = jnp.moveaxis(blocks, 0, dim)
    dims = blocks.shape
    return blocks.reshape(*dims[:dim], dims[dim] * dims[dim + 1], *dims[dim + 2 :])


def gather_axes(array, axes, dim):
    far, near = axes
    blocks = sent_to_all(sent_to_all(array, far), near)
    return joined_along(blocks.swapaxes(0, 1).reshape(-1, *array.shape), dim)


def total_of(array, axes):
    lines = array.reshape(-1)
    own = summed_rows(filled_up(lines, lax.axis_size(axes[0]) * lax.axis_size(axes[1])), axes, 0)
    whole = gather_axes(own, axes, 0)
    return whole[: len(lines)].reshape(array.shape)


def observe_stats(prior_ens, values, variances):
    centre = jnp.mean(prior_ens, axis=0)
    anomaly = prior_ens - centre
    prior_var = jnp.sum(anomaly * anomaly, axis=0) / (ENSEMBLE_COUNT - 1) + 1e-06
    post_var = 1.0 / (1.0 / prior_var + 1.0 / variances)
    post_mean = post_var * (centre / prior_var + values / variances)
    shrink = jnp.sqrt(post_var / prior_var)
    increment = (post_mean - centre + (shrink - 1.0) * anomaly).astype(jnp.bfloat16)
    scaling = 1.0 / ((ENSEMBLE_COUNT - 1) * prior_var)
    return (increment, anomaly.astype(jnp.bfloat16), scaling)


def taper_weights(columns, obs_index, taper_row, reach_row):
    distance = jnp.abs(columns[:, None] // LB - obs_index[None, :] // LB).astype(jnp.float32)
    return taper_row[None, :] * jnp.maximum(
        0.0, 1.0 - distance / (reach_row[None, :].astype(jnp.float32) + 1.0)
    )


def update_block(
    block_values, columns, obs_index, taper_row, reach_row, increment, anomaly, scaling
):
    values = block_values.astype(jnp.float32)
    centred = (values - jnp.mean(values, axis=0)).astype(jnp.bfloat16)
    covariance = lax.dot_general(
        centred, anomaly, (((0,), (0,)), ((), ())), preferred_element_type=jnp.float32
    )
    gain_matrix = (
        taper_weights(columns, obs_index, taper_row, reach_row) * covariance * scaling[None, :]
    ).astype(jnp.bfloat16)
    change = lax.dot_general(
        increment, gain_matrix, (((1,), (1,)), ((), ())), preferred_element_type=jnp.float32
    )
    return (values + change).astype(jnp.bfloat16)


def collect_prior(realization_vectors, owner_row, local_row, my_block, col_offset):
    picked = jnp.take(realization_vectors, col_offset + local_row, axis=1).astype(jnp.float32)
    return jnp.where((owner_row == my_block)[None, :], picked, 0.0)


def apply_batch(
    realization_vectors, column_base, obs_index, taper_row, reach_row, increment, anomaly, scaling
):

    def advance(block_no, buffer):
        start_col = block_no * BLK
        block_values = lax.dynamic_slice_in_dim(buffer, start_col, BLK, 1)
        columns = column_base + start_col + jnp.arange(BLK, dtype=jnp.int32)
        renewed = update_block(
            block_values, columns, obs_index, taper_row, reach_row, increment, anomaly, scaling
        )
        return lax.dynamic_update_slice_in_dim(buffer, renewed, start_col, 1)

    return lax.fori_loop(0, realization_vectors.shape[1] // BLK, advance, realization_vectors)


def on_device(
    background_ensemble,
    measured_segment_index,
    measured_place_within_segment,
    measured_readings,
    measured_noise_spread,
    measured_damping_weight,
    measured_cutoff_extent,
):
    pieces = lax.axis_size("mem")
    member_row = lax.axis_index("mem")
    slab_index = lax.axis_index(STATE)
    my_block = slab_index * pieces + member_row
    realization_vectors = lax.all_to_all(
        background_ensemble, "mem", split_axis=1, concat_axis=0, tiled=True
    )
    column_base = my_block * SD
    col_offset = 0
    for batch_no in range(B):
        if batch_no == 0:
            prior_ens = total_of(
                collect_prior(
                    realization_vectors,
                    measured_segment_index[0],
                    measured_place_within_segment[0],
                    my_block,
                    col_offset,
                ),
                ("mem", ("state_0", "state_1", "state_2")),
            )
        else:
            prior_ens = total_of(
                collect_prior(
                    realization_vectors,
                    measured_segment_index[batch_no],
                    measured_place_within_segment[batch_no],
                    my_block,
                    col_offset,
                ),
                ("mem", ("state_0", "state_1", "state_2")),
            )
        obs_index = measured_segment_index[batch_no] * SD + measured_place_within_segment[batch_no]
        increment, anomaly, scaling = observe_stats(
            prior_ens, measured_readings[batch_no], measured_noise_spread[batch_no]
        )
        realization_vectors = apply_batch(
            realization_vectors,
            column_base,
            obs_index,
            measured_damping_weight[batch_no],
            measured_cutoff_extent[batch_no],
            increment,
            anomaly,
            scaling,
        )
    return lax.all_to_all(realization_vectors, "mem", split_axis=0, concat_axis=1, tiled=True)


def solution(mesh):
    torus = Mesh(
        mesh.devices.reshape(mesh.shape["mem"], 4, 4, 4), ("mem", "state_0", "state_1", "state_2")
    )
    in_specs = (P("mem", STATE), P(), P(), P(), P(), P(), P())
    out_specs = P("mem", STATE)
    return jax.shard_map(
        on_device, mesh=torus, in_specs=in_specs, out_specs=out_specs, check_vma=False
    )
```

profile of v0, /device:TPU:9, one launch (start us, length us, event | category | flops | bytes accessed | tf_op | source)
XLA Modules:
  0.0 209.1 jit_solution(6932354710521923166)
XLA Ops:
  0.0 5.2 %copy.47 = bf16[5,2,8,32768]{3,2,0,1:T(8,128)(2,1)} copy(bf16[5,2,8,32768]{3,2,1,0:T(8,128)(2,1)} %bitcast.89) | data formatting | bytes 10485760 | tf_op jit(solution)/shard_map/all_to_all | solution.py:136
  5.2 6.8 %all-to-all-start = ((bf16[40,2,32768]{2,0,1:T(8,128)(2,1)}), bf16[40,2,32768]{2,0,1:T(8,128)(2,1)}, u32[]{:S(2)}, u32[]{:S(2)}) async-start(bf16[40,2,32768]{2,0,1:T(8,128)(2,1)} %bitcast.87), calls=%async_computation | async-start | bytes 10485760 | tf_op jit(solution)/shard_map/all_to_all | solution.py:136
  12.1 4.8 %all-to-all-done = bf16[40,2,32768]{2,0,1:T(8,128)(2,1)} async-done(((bf16[40,2,32768]{2,0,1:T(8,128)(2,1)}), bf16[40,2,32768]{2,0,1:T(8,128)(2,1)}, u32[]{:S(2)}, u32[]{:S(2)}) %all-to-all-start) | async-done | bytes 5242912 | tf_op jit(solution)/shard_map/all_to_all | solution.py:136
  16.9 9.5 %copy.31 = bf16[80,32768]{0,1:T(8,128)(2,1)} copy(bf16[80,32768]{1,0:T(8,128)(2,1)} %bitcast.9) | data formatting | bytes 10485760 | tf_op jit(solution)/shard_map/all_to_all | solution.py:136
  26.4 5.2 %gather_fusion = bf16[256,80]{1,0:T(8,128)(2,1)S(1)} fusion(bf16[80,32768]{0,1:T(8,128)(2,1)} %copy.31, s32[1024]{0:T(1024)S(1)} %pad_clamp_fusion.1), kind=kCustom, calls=%fused_computation.clone | custom fusion | bytes 82944 | tf_op jit(solution)/shard_map/jit(_take)/gather | solution.py:103
  32.7 10.9 %all-to-all-start.1 = ((f32[64,2,160]{2,1,0:T(2,128)}), f32[64,2,160]{2,1,0:T(2,128)S(1)}, u32[]{:S(2)}, u32[]{:S(2)}) async-start(f32[64,2,160]{2,1,0:T(2,128)} %copy.33), calls=%async_computation.1 | async-start | bytes 262144 | tf_op jit(solution)/shard_map/all_to_all | solution.py:23
  43.6 7.9 %all-to-all-done.1 = f32[64,2,160]{2,1,0:T(2,128)S(1)} async-done(((f32[64,2,160]{2,1,0:T(2,128)}), f32[64,2,160]{2,1,0:T(2,128)S(1)}, u32[]{:S(2)}, u32[]{:S(2)}) %all-to-all-start.1) | async-done | bytes 81952 | tf_op jit(solution)/shard_map/all_to_all | solution.py:23
  51.6 5.0 %all_to_all.88 = f32[2,1,160]{2,1,0:T(1,128)S(1)} all-to-all(f32[2,1,160]{2,1,0:T(1,128)S(1)} %all_to_all.65), channel_id=1, replica_groups=mesh['mem'=2,'state_0'=4,'state_1'=4,'state_2'=4] {'mem'}, dimensions={0} | all-to-all | bytes 2560 | tf_op jit(solution)/shard_map/all_to_all | solution.py:30
  56.7 3.7 %all_to_all.89 = f32[2,1,160]{2,1,0:T(1,128)S(1)} all-to-all(f32[2,1,160]{2,1,0:T(1,128)S(1)} %broadcast_in_dim.94), channel_id=1, replica_groups=mesh['mem'=2,'state_0'=4,'state_1'=4,'state_2'=4] {'mem'}, dimensions={0} | all-to-all | bytes 2560 | tf_op jit(solution)/shard_map/all_to_all | solution.py:42
  61.1 5.6 %all-to-all-start.4 = ((f32[64,2,160]{2,1,0:T(2,128)}), f32[64,2,160]{2,1,0:T(2,128)S(1)}, u32[]{:S(2)}, u32[]{:S(2)}) async-start(f32[64,2,160]{2,1,0:T(2,128)} %broadcast_in_dim.96), calls=%async_computation.4 | async-start | bytes 262144 | tf_op jit(solution)/shard_map/all_to_all | solution.py:42
  66.7 7.9 %all-to-all-done.4 = f32[64,2,160]{2,1,0:T(2,128)S(1)} async-done(((f32[64,2,160]{2,1,0:T(2,128)}), f32[64,2,160]{2,1,0:T(2,128)S(1)}, u32[]{:S(2)}, u32[]{:S(2)}) %all-to-all-start.4) | async-done | bytes 81952 | tf_op jit(solution)/shard_map/all_to_all | solution.py:42
  74.9 33.8 %while.32 = (s32[]{:T(128)}, bf16[80,32768]{1,0:T(8,128)(2,1)}, f32[1,256]{1,0:T(1,128)S(1)}, s32[]{:T(128)}, s32[1,256]{1,0:T(1,128)S(1)}, /*index=5*/s32[256]{...) while((s32[]{:T(128)}, bf16[80,32768]{1,0:T(8,128)(2,1)}, ...), condition=%wide.region_6.8_spmd, body=%wide.region_4.7_spmd.sunk | while | flops 348720640 | bytes 3467987 | solution.py:120
  88.9 2.9 %fusion.48 = bf16[80,32768]{1,0:T(8,128)(2,1)} fusion(bf16[80,32768]{1,0:T(8,128)(2,1)} %get-tuple-element.801, s32[]{:T(128)S(6)} %select_n.138, bf16[80,256]{1,0:T(8,128)(2,1)S(1)} %get-tuple-element.825, bf16[80,4096]{1,0:T(8,128)(2,1)S(1)} %get-tuple-element.770, bf16[80,256]{1,0:T(8,128)(2,1)S(1)} %get-tuple-element.823, ...), kind=kOutput, calls=%fused_computation.8.clone.1 | convolution fusion | flops 347996160 | bytes 2084868 | tf_op jit(solution)/shard_map/while/body/eval_jaxpr/dot_general | solution.py:96
  108.7 9.5 %copy.35 = bf16[80,32768]{0,1:T(8,128)(2,1)} copy(bf16[80,32768]{1,0:T(8,128)(2,1)} %get-tuple-element.831) | data formatting | bytes 10485760 | tf_op jit(solution)/shard_map/while | solution.py:120
  118.2 5.2 %gather_fusion.1 = bf16[256,80]{1,0:T(8,128)(2,1)S(1)} fusion(bf16[80,32768]{0,1:T(8,128)(2,1)} %copy.35, s32[1024]{0:T(1024)S(1)} %pad_clamp_fusion), kind=kCustom, calls=%fused_computation.1.clone | custom fusion | bytes 82944 | tf_op jit(solution)/shard_map/jit(_take)/gather | solution.py:103
  123.8 13.5 %all_to_all.90 = f32[64,2,160]{2,1,0:T(2,128)S(1)} all-to-all(f32[64,2,160]{2,1,0:T(2,128)S(1)} %copy.37), channel_id=1, replica_groups=mesh['mem'=2,'state_0'=4,'state_1'=4,'state_2'=4] {'state_0','state_1','..., dimensions={0} | all-to-all | bytes 163840 | tf_op jit(solution)/shard_map/all_to_all | solution.py:23
  137.4 6.3 %all_to_all.91 = f32[2,1,160]{2,1,0:T(1,128)S(1)} all-to-all(f32[2,1,160]{2,1,0:T(1,128)S(1)} %all_to_all.70), channel_id=1, replica_groups=mesh['mem'=2,'state_0'=4,'state_1'=4,'state_2'=4] {'mem'}, dimensions={0} | all-to-all | bytes 2560 | tf_op jit(solution)/shard_map/all_to_all | solution.py:30
  143.7 3.7 %all_to_all.92 = f32[2,1,160]{2,1,0:T(1,128)S(1)} all-to-all(f32[2,1,160]{2,1,0:T(1,128)S(1)} %broadcast_in_dim.99), channel_id=1, replica_groups=mesh['mem'=2,'state_0'=4,'state_1'=4,'state_2'=4] {'mem'}, dimensions={0} | all-to-all | bytes 2560 | tf_op jit(solution)/shard_map/all_to_all | solution.py:42
  148.1 5.6 %all-to-all-start.8 = ((f32[64,2,160]{2,1,0:T(2,128)}), f32[64,2,160]{2,1,0:T(2,128)S(1)}, u32[]{:S(2)}, u32[]{:S(2)}) async-start(f32[64,2,160]{2,1,0:T(2,128)} %broadcast_in_dim.101), calls=%async_computation.8 | async-start | bytes 262144 | tf_op jit(solution)/shard_map/all_to_all | solution.py:42
  153.7 7.9 %all-to-all-done.8 = f32[64,2,160]{2,1,0:T(2,128)S(1)} async-done(((f32[64,2,160]{2,1,0:T(2,128)}), f32[64,2,160]{2,1,0:T(2,128)S(1)}, u32[]{:S(2)}, u32[]{:S(2)}) %all-to-all-start.8) | async-done | bytes 81952 | tf_op jit(solution)/shard_map/all_to_all | solution.py:42
  161.8 33.8 %while.33 = (s32[]{:T(128)}, bf16[80,32768]{1,0:T(8,128)(2,1)}, f32[1,256]{1,0:T(1,128)S(1)}, s32[]{:T(128)}, s32[1,256]{1,0:T(1,128)S(1)}, /*index=5*/s32[256]{...) while((s32[]{:T(128)}, bf16[80,32768]{1,0:T(8,128)(2,1)}, ...), condition=%wide.region_13.15_spmd, body=%wide.region_11.14_spmd.sunk | while | flops 348720640 | bytes 3467987 | solution.py:120
  175.9 2.9 %fusion.52 = bf16[80,32768]{1,0:T(8,128)(2,1)} fusion(bf16[80,32768]{1,0:T(8,128)(2,1)} %get-tuple-element.846, s32[]{:T(128)S(6)} %select_n.141, bf16[80,256]{1,0:T(8,128)(2,1)S(1)} %get-tuple-element.870, bf16[80,4096]{1,0:T(8,128)(2,1)S(1)} %get-tuple-element.783, bf16[80,256]{1,0:T(8,128)(2,1)S(1)} %get-tuple-element.868, ...), kind=kOutput, calls=%fused_computation.38.clone.1 | convolution fusion | flops 347996160 | bytes 2084868 | tf_op jit(solution)/shard_map/while/body/eval_jaxpr/dot_general | solution.py:96
  192.7 2.9 %fusion.52 = bf16[80,32768]{1,0:T(8,128)(2,1)} fusion(bf16[80,32768]{1,0:T(8,128)(2,1)} %get-tuple-element.846, s32[]{:T(128)S(6)} %select_n.141, bf16[80,256]{1,0:T(8,128)(2,1)S(1)} %get-tuple-element.870, bf16[80,4096]{1,0:T(8,128)(2,1)S(1)} %get-tuple-element.783, bf16[80,256]{1,0:T(8,128)(2,1)S(1)} %get-tuple-element.868, ...), kind=kOutput, calls=%fused_computation.38.clone.1 | convolution fusion | flops 347996160 | bytes 2084868 | tf_op jit(solution)/shard_map/while/body/eval_jaxpr/dot_general | solution.py:96
  195.7 10.7 %all_to_all.93 = bf16[2,40,32768]{2,1,0:T(8,128)(2,1)S(1)} all-to-all(bf16[2,40,32768]{2,1,0:T(8,128)(2,1)} %bitcast.29), channel_id=1, replica_groups=mesh['mem'=2,'state_0'=4,'state_1'=4,'state_2'=4] {'mem'}, dimensions={0} | all-to-all | bytes 10485760 | tf_op jit(solution)/shard_map/all_to_all | solution.py:178
  (169 shorter events, 64.7 us)
Async XLA Ops:
  5.2 6.8 %copy-start = (s32[2,256]{1,0:T(2,128)S(1)}, s32[2,256]{1,0:T(2,128)}, u32[]{:S(2)}) copy-start(s32[2,256]{1,0:T(2,128)} %param.14) | copy-start | bytes 6148
  5.2 6.8 %copy-start.4 = (s32[2,256]{1,0:T(2,128)S(1)}, s32[2,256]{1,0:T(2,128)}, u32[]{:S(2)}) copy-start(s32[2,256]{1,0:T(2,128)} %param.19) | copy-start | bytes 6148
  5.2 6.8 %copy-start.5 = (s32[2,256]{1,0:T(2,128)S(1)}, s32[2,256]{1,0:T(2,128)}, u32[]{:S(2)}) copy-start(s32[2,256]{1,0:T(2,128)} %param.15) | copy-start | bytes 6148
  5.2 11.7 %all-to-all-start = ((bf16[40,2,32768]{2,0,1:T(8,128)(2,1)}), bf16[40,2,32768]{2,0,1:T(8,128)(2,1)}, u32[]{:S(2)}, u32[]{:S(2)}) async-start(bf16[40,2,32768]{2,0,1:T(8,128)(2,1)} %bitcast.87), calls=%async_computation | async-start | bytes 10485760 | tf_op jit(solution)/shard_map/all_to_all | solution.py:136
  16.9 26.7 %copy-start.1 = (f32[2,256]{1,0:T(2,128)S(1)}, f32[2,256]{1,0:T(2,128)}, u32[]{:S(2)}) copy-start(f32[2,256]{1,0:T(2,128)} %param.18) | copy-start | bytes 6148
  16.9 58.0 %copy-start.2 = (f32[2,256]{1,0:T(2,128)S(1)}, f32[2,256]{1,0:T(2,128)}, u32[]{:S(2)}) copy-start(f32[2,256]{1,0:T(2,128)} %param.16) | copy-start | bytes 6148
  16.9 58.0 %copy-start.3 = (f32[2,256]{1,0:T(2,128)S(1)}, f32[2,256]{1,0:T(2,128)}, u32[]{:S(2)}) copy-start(f32[2,256]{1,0:T(2,128)} %param.17) | copy-start | bytes 6148
  32.7 18.8 %all-to-all-start.1 = ((f32[64,2,160]{2,1,0:T(2,128)}), f32[64,2,160]{2,1,0:T(2,128)S(1)}, u32[]{:S(2)}, u32[]{:S(2)}) async-start(f32[64,2,160]{2,1,0:T(2,128)} %copy.33), calls=%async_computation.1 | async-start | bytes 262144 | tf_op jit(solution)/shard_map/all_to_all | solution.py:23
  61.1 13.5 %all-to-all-start.4 = ((f32[64,2,160]{2,1,0:T(2,128)}), f32[64,2,160]{2,1,0:T(2,128)S(1)}, u32[]{:S(2)}, u32[]{:S(2)}) async-start(f32[64,2,160]{2,1,0:T(2,128)} %broadcast_in_dim.96), calls=%async_computation.4 | async-start | bytes 262144 | tf_op jit(solution)/shard_map/all_to_all | solution.py:42
  148.1 13.5 %all-to-all-start.8 = ((f32[64,2,160]{2,1,0:T(2,128)}), f32[64,2,160]{2,1,0:T(2,128)S(1)}, u32[]{:S(2)}, u32[]{:S(2)}) async-start(f32[64,2,160]{2,1,0:T(2,128)} %broadcast_in_dim.101), calls=%async_computation.8 | async-start | bytes 262144 | tf_op jit(solution)/shard_map/all_to_all | solution.py:42
where the time goes:
time: 213 us; the launch traced here: 209 us
  matrix products  46.8 us (22%)
  blocking collectives  42.8 us (20%)
  local copies, waits for them, and re-layouts  40.2 us (19%)
  starting transfers between devices  28.8 us (14%)
  waiting for transfers between devices  28.5 us (13%)
  other arithmetic  21.1 us (10%)
    dot_general x16, matrix products, update_block(): lax.dot_general(increment, gain_matrix, (((1,), (1,)), ((), ())), preferr...  46.8 us
    reduce_sum x16, other arithmetic, update_block(): centred = (values - jnp.mean(values, axis=0)).astype(jnp.bfloat16)  19.4 us
    all_to_all x2, waiting for transfers between devices, sent_to_all(): lax.all_to_all(jnp.broadcast_to(array[None], (size, *array.shape)), axis,...  15.8 us
    all_to_all x2, local copies, waits for them, and re-layouts, on_device(): lax.all_to_all(background_ensemble, 'mem', split_axis=1, concat_axis=0, t...  14.7 us
    all_to_all x1, blocking collectives, sum_at_owner(): lax.all_to_all(blocks, axis, split_axis=0, concat_axis=0, tiled=True)  13.5 us
    all_to_all x2, blocking collectives, summed_rows(): return jnp.sum(lax.all_to_all(own, far, 0, 0, tiled=True), axis=0)  11.3 us
    all_to_all x2, starting transfers between devices, sent_to_all(): lax.all_to_all(jnp.broadcast_to(array[None], (size, *array.shape)), axis,...  11.2 us
    all_to_all x1, starting transfers between devices, sum_at_owner(): lax.all_to_all(blocks, axis, split_axis=0, concat_axis=0, tiled=True)  10.9 us
  transfers between devices with their start and end apart: 4, of which 4 were waited for; matrix products, arithmetic and copies ran while one was open for 0% of the time, Pallas kernels for 0%

commit v1 on v0

v1 whole, which is shorter than its diff:
```python
import functools

import jax
import jax.numpy as jnp
from jax import lax
from jax.experimental import pallas as pl
from jax.experimental.pallas import tpu as pltpu
from jax.sharding import PartitionSpec as P

MEMBERS = 80
HALF = 40
SD = 32768
K = 256
B = 2
LB = 128
CHIP = 2 * SD
CHIPS = 64
SEG_BLOCKS = SD // LB
CHUNK = 2048
STEPS = SD // CHUNK
CHUNK_BLOCKS = CHUNK // LB
F32 = jnp.float32
BF16 = jnp.bfloat16
NT = (((1,), (1,)), ((), ()))
VMEM_LIMIT = 56 * 1024 * 1024


def dot(a, b):
    return jnp.dot(a, b, preferred_element_type=F32)


def dot_nt(a, b):
    return lax.dot_general(a, b, NT, preferred_element_type=F32)


def pick_kernel(rel_ref, x_ref, o_ref, xv, acc, owned, sems):
    parts = 4
    width = CHIP // parts
    copies = [
        pltpu.make_async_copy(
            x_ref.at[:, pl.ds(p * width, width)], xv.at[:, pl.ds(p * width, width)], sems.at[p]
        )
        for p in range(parts)
    ]
    for copy in copies:
        copy.start()
    acc[...] = jnp.zeros_like(acc)

    def scan(k, n):
        owned[n] = k
        return n + (rel_ref[k] >= 0).astype(jnp.int32)

    n = lax.fori_loop(0, B * K, scan, jnp.int32(0), unroll=8)
    for j in range(4):
        owned[n + j] = B * K
    for copy in copies:
        copy.wait()
    lane = lax.broadcasted_iota(jnp.int32, (HALF, LB), 1)

    def extract(i, _):
        for j in range(4):
            k = owned[4 * i + j]
            at = rel_ref[k]
            start = pl.multiple_of((at // LB) * LB, LB)
            tile = xv[:, pl.ds(start, LB)].astype(F32)
            turned = pltpu.roll(tile, (k - at) & (LB - 1), 1)
            pltpu.store(acc.at[k // LB], turned, mask=lane == (k & (LB - 1)))
        return 0

    lax.fori_loop(0, (n + 3) // 4, extract, 0)
    for g in range(B * K // LB):
        o_ref[:, g * LB : (g + 1) * LB] = acc[g].astype(BF16)


def pick(rel, x):
    return pl.pallas_call(
        pick_kernel,
        grid_spec=pltpu.PrefetchScalarGridSpec(
            num_scalar_prefetch=1,
            grid=(1,),
            in_specs=[pl.BlockSpec(memory_space=pl.ANY)],
            out_specs=pl.BlockSpec((HALF, B * K), lambda i, s: (0, 0)),
            scratch_shapes=[
                pltpu.VMEM((HALF, CHIP), BF16),
                pltpu.VMEM((B * K // LB + 1, HALF, LB), F32),
                pltpu.SMEM((B * K + 8,), jnp.int32),
                pltpu.SemaphoreType.DMA((4,)),
            ],
        ),
        out_shape=jax.ShapeDtypeStruct((HALF, B * K), BF16),
        compiler_params=pltpu.CompilerParams(vmem_limit_bytes=VMEM_LIMIT),
        cost_estimate=pl.CostEstimate(flops=0, bytes_accessed=2 * HALF * CHIP, transcendentals=0),
        name="pick",
    )(rel, x)


def observe_stats(prior, values, variances):
    centre = jnp.sum(prior, axis=0, keepdims=True) / MEMBERS
    anomaly = prior - centre
    prior_var = jnp.sum(anomaly * anomaly, axis=0, keepdims=True) / (MEMBERS - 1) + 1e-06
    post_var = 1.0 / (1.0 / prior_var + 1.0 / variances)
    post_mean = post_var * (centre / prior_var + values / variances)
    shrink = jnp.sqrt(post_var / prior_var)
    increment = (post_mean - centre + (shrink - 1.0) * anomaly).astype(BF16)
    scaled = anomaly * (1.0 / ((MEMBERS - 1) * prior_var))
    high = scaled.astype(BF16)
    low = (scaled - high.astype(F32)).astype(BF16)
    return increment, high, low


def iota(shape, dim):
    return lax.broadcasted_iota(jnp.int32, shape, dim)


def update_kernel(
    sp_ref, row_ref, col_ref, prior_ref, x_ref, own_ref, away_ref, cov_l, chg_l, cols, count
):
    step = pl.program_id(0)
    first = sp_ref[1].astype(F32)

    @pl.when(step == 0)
    def _():
        row = lambda r: row_ref[r : r + 1, :]
        eye = (iota((K, K), 0) == iota((K, K), 1)).astype(F32).astype(BF16)
        upper = (iota((K, K), 0) <= iota((K, K), 1)).astype(F32).astype(BF16)
        member_eye = (iota((MEMBERS, LB), 0) == iota((MEMBERS, LB), 1)).astype(F32).astype(BF16)
        prior0 = prior_ref[:, :K].astype(F32)
        stats0 = observe_stats(prior0, row(6), row(8))
        prior1b = prior_ref[:, K:]
        lhs = jnp.concatenate([dot_nt(eye, stats0[1]), dot_nt(eye, stats0[2])], 1).astype(BF16)
        cov = dot(lhs, jnp.concatenate([prior1b, prior1b], 0))
        distance = jnp.abs(row(1) - col_ref[:, 0:1])
        weight = col_ref[:, 2:3] * jnp.maximum(0.0, 1.0 - distance / col_ref[:, 1:2])
        gain = (weight * cov).astype(BF16)
        prior1 = (prior1b.astype(F32) + dot(stats0[0], gain)).astype(BF16).astype(F32)
        stats1 = observe_stats(prior1, row(7), row(9))
        most = jnp.int32(0)
        for b, (increment, high, low) in enumerate((stats0, stats1)):
            place, reach, damping = row(b), row(2 + b), row(4 + b)
            last = first + (SEG_BLOCKS - 1)
            gap = jnp.maximum(jnp.maximum(first - place, place - last), 0.0)
            felt = (gap < reach).astype(F32)
            rank = dot(jnp.broadcast_to(felt, (8, K)).astype(BF16), upper)[0:1]
            slot = jnp.where(felt > 0.0, rank - 1.0, -1.0)
            chosen = slot == iota((K, K), 0).astype(F32)
            most = jnp.maximum(most, jnp.sum(felt).astype(jnp.int32))
            pickm = chosen.astype(F32).astype(BF16)
            cov_l[b] = jnp.concatenate([dot_nt(pickm, high), dot_nt(pickm, low)], 1).astype(BF16)
            chg_l[b, :, 0:K] = dot_nt(increment, pickm).astype(BF16)
            chg_l[b, :, K : K + LB] = member_eye
            for c, value in enumerate((place, reach, damping)):
                column = jnp.sum(jnp.where(chosen, value, 0.0), axis=1, keepdims=True)
                if c == 1:
                    column = jnp.maximum(column, 1.0)
                cols[b, c] = jnp.broadcast_to(column, (K, LB))
        count[0] = most

    def weights(b, kc):
        block = (first + (step * CHUNK_BLOCKS).astype(F32)) + iota((kc, LB), 1).astype(F32)
        distance = jnp.abs(block - cols[b, 0, :kc])
        return cols[b, 2, :kc] * jnp.maximum(0.0, 1.0 - distance / cols[b, 1, :kc])

    def gains(b, kc, x, w, pair):
        cov = dot(cov_l[b, :kc], jnp.concatenate([x, x], 0))
        parts = [
            cov[:, h * LB : (h + 1) * LB]
            * jnp.broadcast_to(w[:, 2 * pair + h : 2 * pair + h + 1], (kc, LB))
            for h in range(2)
        ]
        return jnp.concatenate(parts, 1).astype(BF16)

    def advance(kc):
        w = [weights(b, kc) for b in range(B)]
        for pair in range(CHUNK // 256):
            x = x_ref[:, pair * 256 : (pair + 1) * 256]
            for b in range(B):
                g = gains(b, kc, x, w[b], pair)
                if kc == LB:
                    lhs = jnp.concatenate([chg_l[b, :, 0:LB], chg_l[b, :, K : K + LB]], 1)
                    spare = jnp.zeros((LB - MEMBERS, 256), BF16)
                    after = dot(lhs, jnp.concatenate([g, x, spare], 0))
                else:
                    after = dot(chg_l[b, :, 0:K], g) + x.astype(F32)
                if b == 0:
                    x = after.astype(BF16)
            own_ref[:, pair * 256 : (pair + 1) * 256] = after[:HALF].astype(BF16)
            away_ref[:, pair * 256 : (pair + 1) * 256] = after[HALF:].astype(BF16)

    @pl.when(count[0] <= LB)
    def _():
        advance(LB)

    @pl.when(count[0] > LB)
    def _():
        advance(K)


def update(sp, rows, cols, prior, x):
    return pl.pallas_call(
        update_kernel,
        grid_spec=pltpu.PrefetchScalarGridSpec(
            num_scalar_prefetch=1,
            grid=(STEPS,),
            in_specs=[
                pl.BlockSpec((16, K), lambda i, s: (0, 0)),
                pl.BlockSpec((K, 8), lambda i, s: (0, 0)),
                pl.BlockSpec((MEMBERS, B * K), lambda i, s: (0, 0)),
                pl.BlockSpec((MEMBERS, CHUNK), lambda i, s: (0, i)),
            ],
            out_specs=[
                pl.BlockSpec((HALF, CHUNK), lambda i, s: (0, s[0] * STEPS + i)),
                pl.BlockSpec((HALF, CHUNK), lambda i, s: (0, i)),
            ],
            scratch_shapes=[
                pltpu.VMEM((B, K, 2 * MEMBERS), BF16),
                pltpu.VMEM((B, MEMBERS, K + LB), BF16),
                pltpu.VMEM((B, 3, K, LB), F32),
                pltpu.SMEM((1,), jnp.int32),
            ],
        ),
        out_shape=[
            jax.ShapeDtypeStruct((HALF, CHIP), BF16),
            jax.ShapeDtypeStruct((HALF, SD), BF16),
        ],
        compiler_params=pltpu.CompilerParams(vmem_limit_bytes=VMEM_LIMIT),
        cost_estimate=pl.CostEstimate(
            flops=10_000_000_000, bytes_accessed=4 * MEMBERS * SD, transcendentals=0
        ),
        name="update",
    )(sp, rows, cols, prior, x)


def fill_kernel(sp_ref, got_ref, out_hbm, out_ref):
    out_ref[...] = got_ref[...]


def fill(sp, got, out):
    width = 8192
    return pl.pallas_call(
        fill_kernel,
        grid_spec=pltpu.PrefetchScalarGridSpec(
            num_scalar_prefetch=1,
            grid=(SD // width,),
            in_specs=[
                pl.BlockSpec((HALF, width), lambda i, s: (0, i)),
                pl.BlockSpec(memory_space=pl.ANY),
            ],
            out_specs=pl.BlockSpec((HALF, width), lambda i, s: (0, (1 - s[0]) * (SD // width) + i)),
        ),
        out_shape=jax.ShapeDtypeStruct((HALF, CHIP), BF16),
        input_output_aliases={2: 0},
        compiler_params=pltpu.CompilerParams(vmem_limit_bytes=VMEM_LIMIT),
        name="fill",
    )(sp, got, out)


def shifted(array, by):
    pairs = [(i, (i + by) % CHIPS) for i in range(CHIPS)]
    return lax.ppermute(array, "state", pairs)


def swapped(array):
    return lax.ppermute(array, "mem", [(0, 1), (1, 0)])


def on_device(x, segment, place, readings, spread, damping, extent):
    core = lax.axis_index("mem")
    chip = lax.axis_index("state")
    index = segment * SD + place
    rel = index.reshape(-1) - chip * CHIP
    rel = jnp.where((rel >= 0) & (rel < CHIP), rel, -1)
    rel = jnp.concatenate([rel, jnp.zeros((8,), jnp.int32)])
    block = (index // LB).astype(F32)
    reach = extent.astype(F32) + 1.0
    rows = jnp.concatenate([block, reach, damping, readings, spread, jnp.zeros((6, K), F32)], 0)
    cols = jnp.concatenate(
        [block[0][:, None], reach[0][:, None], damping[0][:, None], jnp.zeros((K, 5), F32)], 1
    )
    sp = jnp.stack([core, (chip * 2 + core) * SEG_BLOCKS]).astype(jnp.int32)

    picked = pick(rel, x)
    sent = lax.dynamic_slice_in_dim(x, (1 - core) * SD, SD, 1)
    kept = lax.dynamic_slice_in_dim(x, core * SD, SD, 1)
    whole = jnp.concatenate([kept, swapped(sent)], 0)
    near = picked + shifted(picked, 1) + shifted(picked, -1)
    far = near + shifted(near, 3) + shifted(near, -3)
    prior = jnp.concatenate([far, swapped(far)], 0)
    own, away = update(sp, rows, cols, prior, whole)
    return fill(sp, swapped(away), own)


def solution(mesh):
    in_specs = (P("mem", "state"), P(), P(), P(), P(), P(), P())
    return jax.shard_map(
        on_device, mesh=mesh, in_specs=in_specs, out_specs=P("mem", "state"), check_vma=False
    )
```

time: 213 us -> 127 us (0.60)
  the two profiles are of different devices: /device:TPU:9 before, /device:TPU:1 now
where the time goes in v1:
time: 127 us; the launch traced here: 126 us
  Pallas kernels  77.9 us (61%)
  waiting for transfers between devices  17.9 us (14%)
  starting transfers between devices  15.5 us (12%)
  local copies, waits for them, and re-layouts  8.58 us (7%)
  other arithmetic  6.46 us (5%)
    pallas_call x1, Pallas kernels, update(): pl.pallas_call(update_kernel, grid_spec=pltpu.PrefetchScalarGridSpec(num_...  69.3 us
    ppermute x4, waiting for transfers between devices, shifted(): return lax.ppermute(array, 'state', pairs)  12.8 us
    ppermute x4, starting transfers between devices, shifted(): return lax.ppermute(array, 'state', pairs)  11.3 us
    ppermute x3, waiting for transfers between devices, swapped(): return lax.ppermute(array, 'mem', [(0, 1), (1, 0)])  5.11 us
    pallas_call x1, Pallas kernels, fill(): pl.pallas_call(fill_kernel, grid_spec=pltpu.PrefetchScalarGridSpec(num_sc...  4.66 us
    dynamic_slice x1, local copies, waits for them, and re-layouts, on_device(): kept = lax.dynamic_slice_in_dim(x, core * SD, SD, 1)  4.38 us
    concatenate x1, other arithmetic, on_device(): whole = jnp.concatenate([kept, swapped(sent)], 0)  4.37 us
    ppermute x3, starting transfers between devices, swapped(): return lax.ppermute(array, 'mem', [(0, 1), (1, 0)])  4.17 us
  transfers between devices with their start and end apart: 7, of which 5 were waited for; matrix products, arithmetic and copies ran while one was open for 4% of the time, Pallas kernels for 3%

profile of v1, /device:TPU:1, one launch (start us, length us, event | category | flops | bytes accessed | tf_op | source)
XLA Modules:
  0.0 126.5 jit_solution(15365327798628465530)
XLA Ops:
  0.0 4.4 %constant_dynamic-slice_fusion.1 = (bf16[40,32768]{1,0:T(8,128)(2,1)S(1)}, bf16[40,32768]{1,0:T(8,128)(2,1)}) fusion(bf16[40,65536]{1,0:T(8,128)(2,1)} %x_ref.1, s32[]{:T(128)S(6)} %select_n.17, s32[]{:T(128)S(6)} %select_n.18), kind=kLoop, calls=%fused_computation.19 | loop fusion | bytes 10485768 | tf_op jit(solution)/shard_map/dynamic_slice | solution.py:283
  4.4 1.5 %collective-permute-start.5 = (bf16[40,32768]{1,0:T(8,128)(2,1)}, bf16[40,32768]{1,0:T(8,128)(2,1)}, u32[]{:S(2)}, u32[]{:S(2)}) collective-permute-start(bf16[40,32768]{1,0:T(8,128)(2,1)} %get-tuple-element.10), channel_id=1, source_target_pairs={{0,64},{64,0},{1,65},{65,1},{2,66},{66,2},{3,67},{67,3},{4,68},{68... | collective-permute-start | bytes 7864328 | tf_op jit(solution)/shard_map/ppermute | solution.py:263
  5.9 0.6 concatenate.17.rel_ref
  6.5 3.9 %pick.1 = bf16[40,512]{1,0:T(8,128)(2,1)} custom-call(s32[520]{0:T(1024)} %concatenate.17.rel_ref, bf16[40,65536]{1,0:T(8,128)(2,1)} %x_ref.1), custom_call_target="tpu_custom_call" | custom-call | bytes 5242880 | tf_op jit(solution)/shard_map/pick/pallas_call | solution.py:76
  10.4 8.6 %collective-permute-start.1 = (bf16[40,512]{1,0:T(8,128)(2,1)}, bf16[40,512]{1,0:T(8,128)(2,1)S(1)}, u32[]{:S(2)}, u32[]{:S(2)}) collective-permute-start(bf16[40,512]{1,0:T(8,128)(2,1)} %pick.1), channel_id=1, source_target_pairs={{0,63},{1,0},{2,1},{3,2},{4,3},{5,4},{6,5},{7,6},{8,7},{9,8},{10,9... | collective-permute-start | bytes 122888 | tf_op jit(solution)/shard_map/ppermute | solution.py:259
  19.1 0.1 pad.8.clone
  19.2 1.3 %collective-permute-done.1 = bf16[40,512]{1,0:T(8,128)(2,1)S(1)} collective-permute-done((bf16[40,512]{1,0:T(8,128)(2,1)}, bf16[40,512]{1,0:T(8,128)(2,1)S(1)}, u32[]{:S(2)}, u32[]{:S(2)}) %collective-permute-start.1) | collective-permute-done | bytes 40992 | tf_op jit(solution)/shard_map/ppermute | solution.py:259
  20.4 7.1 %collective-permute-done = bf16[40,512]{1,0:T(8,128)(2,1)S(1)} collective-permute-done((bf16[40,512]{1,0:T(8,128)(2,1)}, bf16[40,512]{1,0:T(8,128)(2,1)S(1)}, u32[]{:S(2)}, u32[]{:S(2)}) %collective-permute-start) | collective-permute-done | bytes 40992 | tf_op jit(solution)/shard_map/ppermute | solution.py:259
  27.5 0.8 add_add_fusion.1
  28.3 0.1 collective-permute-start.3
  28.4 2.7 %collective-permute-start.2 = (bf16[40,512]{1,0:T(8,128)(2,1)S(1)}, bf16[40,512]{1,0:T(8,128)(2,1)S(1)}, u32[]{:S(2)}, u32[]{:S(2)}) collective-permute-start(bf16[40,512]{1,0:T(8,128)(2,1)S(1)} %add_add_fusion.1), channel_id=1, source_target_pairs={{0,3},{1,4},{2,5},{3,6},{4,7},{5,8},{6,9},{7,10},{8,11},{9,12},{10... | collective-permute-start | bytes 122888 | tf_op jit(solution)/shard_map/ppermute | solution.py:259
  31.1 0.1 maximum_maximum_fusion
  31.1 1.3 %collective-permute-done.3 = bf16[40,512]{1,0:T(8,128)(2,1)S(1)} collective-permute-done((bf16[40,512]{1,0:T(8,128)(2,1)S(1)}, bf16[40,512]{1,0:T(8,128)(2,1)S(1)}, u32[]{:S(2)}, u32[]{:S(2)}) %collective-permute-start.3) | collective-permute-done | bytes 40992 | tf_op jit(solution)/shard_map/ppermute | solution.py:259
  32.4 3.1 %collective-permute-done.2 = bf16[40,512]{1,0:T(8,128)(2,1)S(1)} collective-permute-done((bf16[40,512]{1,0:T(8,128)(2,1)S(1)}, bf16[40,512]{1,0:T(8,128)(2,1)S(1)}, u32[]{:S(2)}, u32[]{:S(2)}) %collective-permute-start.2) | collective-permute-done | bytes 40992 | tf_op jit(solution)/shard_map/ppermute | solution.py:259
  35.5 2.7 %collective-permute-start.4 = (bf16[40,512]{1,0:T(8,128)(2,1)S(1)}, bf16[40,512]{1,0:T(8,128)(2,1)S(1)}, u32[]{:S(2)}, u32[]{:S(2)}) collective-permute-start(bf16[40,512]{1,0:T(8,128)(2,1)S(1)} %add_add_fusion), channel_id=1, source_target_pairs={{0,64},{64,0},{1,65},{65,1},{2,66},{66,2},{3,67},{67,3},{4,68},{68... | collective-permute-start | bytes 122888 | tf_op jit(solution)/shard_map/ppermute | solution.py:263
  38.2 0.6 pad_add_fusion.sp_ref
  38.8 0.8 copy.12.col_ref
  39.6 1.2 concatenate.15.row_ref
  40.8 0.6 pad_maximum_fusion.1.prior_ref
  41.5 4.4 %pad_maximum_fusion.x_ref = bf16[80,32768]{1,0:T(8,128)(2,1)} fusion(bf16[40,32768]{1,0:T(8,128)(2,1)} %collective-permute-done.5, bf16[40,32768]{1,0:T(8,128)(2,1)S(1)} %get-tuple-element.9), kind=kLoop, calls=%fused_computation | loop fusion | flops 10485760 | bytes 10485760 | tf_op jit(solution)/shard_map/concatenate | solution.py:284
  45.8 69.3 %update.1 = (bf16[40,65536]{1,0:T(8,128)(2,1)}, bf16[40,32768]{1,0:T(8,128)(2,1)}) custom-call(s32[2]{0:T(128)} %pad_add_fusion.sp_ref, f32[16,256]{1,0:T(8,128)} %concatenate.15.row_ref, f32[256,8]{1,0:T(8,128)} %copy.12.col_ref, bf16[80,512]{1,0:T(8,128)(2,1)} %pad_maximum_fusion.1.prior_ref, bf16[80,32768]{1,0:T(8,128)(2,1)} %pad_maximum_fusion.x_ref), custom_call_target="tpu_custom_call" | custom-call | flops 10000000000 | bytes 10485760 | tf_op jit(solution)/shard_map/update/pallas_call | solution.py:199
  115.2 5.1 %collective-permute-done.6.got_ref = bf16[40,32768]{1,0:T(8,128)(2,1)S(1)} collective-permute-done((bf16[40,32768]{1,0:T(8,128)(2,1)}, bf16[40,32768]{1,0:T(8,128)(2,1)S(1)}, u32[]{:S(2)}, u32[]{:S(2)}) %collective-permute-start.6) | collective-permute-done | bytes 2621472 | tf_op jit(solution)/shard_map/ppermute | solution.py:263
  120.3 1.5 %copy-done = bf16[40,32768]{1,0:T(8,128)(2,1)} copy-done((bf16[40,32768]{1,0:T(8,128)(2,1)}, bf16[40,32768]{1,0:T(8,128)(2,1)S(1)}, u32[]{:S(2)}) %copy-start) | copy-done | bytes 2621464
  121.8 4.7 %fill.1 = bf16[40,65536]{1,0:T(8,128)(2,1)} custom-call(s32[2]{0:T(128)} %pad_add_fusion.sp_ref, bf16[40,32768]{1,0:T(8,128)(2,1)} %copy-done, bf16[40,65536]{1,0:T(8,128)(2,1)} %get-tuple-element.8.out_hbm), custom_call_target="tpu_custom_call", output_to_operand_aliasing={{}: (2, {})} | custom-call | tf_op jit(solution)/shard_map/fill/pallas_call | solution.py:239
  (26 shorter events, 0.1 us)
Async XLA Ops:
  0.0 5.9 %copy-start.2 = (s32[2,256]{1,0:T(2,128)S(1)}, s32[2,256]{1,0:T(2,128)}, u32[]{:S(2)}) copy-start(s32[2,256]{1,0:T(2,128)} %param.9) | copy-start | bytes 6148
  0.0 5.9 %copy-start.3 = (s32[2,256]{1,0:T(2,128)S(1)}, s32[2,256]{1,0:T(2,128)}, u32[]{:S(2)}) copy-start(s32[2,256]{1,0:T(2,128)} %param.8) | copy-start | bytes 6148
  4.4 14.6 %copy-start.6 = (s32[2,256]{1,0:T(2,128)S(1)}, s32[2,256]{1,0:T(2,128)}, u32[]{:S(2)}) copy-start(s32[2,256]{1,0:T(2,128)} %param.13) | copy-start | bytes 6148
  4.4 14.7 %copy-start.1 = (f32[2,256]{1,0:T(2,128)S(1)}, f32[2,256]{1,0:T(2,128)}, u32[]{:S(2)}) copy-start(f32[2,256]{1,0:T(2,128)} %param.12) | copy-start | bytes 6148
  4.4 35.2 %copy-start.4 = (f32[2,256]{1,0:T(2,128)S(1)}, f32[2,256]{1,0:T(2,128)}, u32[]{:S(2)}) copy-start(f32[2,256]{1,0:T(2,128)} %param.10) | copy-start | bytes 6148
  4.4 35.2 %copy-start.5 = (f32[2,256]{1,0:T(2,128)S(1)}, f32[2,256]{1,0:T(2,128)}, u32[]{:S(2)}) copy-start(f32[2,256]{1,0:T(2,128)} %param.11) | copy-start | bytes 6148
  4.4 37.1 %collective-permute-start.5 = (bf16[40,32768]{1,0:T(8,128)(2,1)}, bf16[40,32768]{1,0:T(8,128)(2,1)}, u32[]{:S(2)}, u32[]{:S(2)}) collective-permute-start(bf16[40,32768]{1,0:T(8,128)(2,1)} %get-tuple-element.10), channel_id=1, source_target_pairs={{0,64},{64,0},{1,65},{65,1},{2,66},{66,2},{3,67},{67,3},{4,68},{68... | collective-permute-start | bytes 7864328 | tf_op jit(solution)/shard_map/ppermute | solution.py:263
  10.4 10.0 %collective-permute-start.1 = (bf16[40,512]{1,0:T(8,128)(2,1)}, bf16[40,512]{1,0:T(8,128)(2,1)S(1)}, u32[]{:S(2)}, u32[]{:S(2)}) collective-permute-start(bf16[40,512]{1,0:T(8,128)(2,1)} %pick.1), channel_id=1, source_target_pairs={{0,63},{1,0},{2,1},{3,2},{4,3},{5,4},{6,5},{7,6},{8,7},{9,8},{10,9... | collective-permute-start | bytes 122888 | tf_op jit(solution)/shard_map/ppermute | solution.py:259
  19.0 8.5 %collective-permute-start = (bf16[40,512]{1,0:T(8,128)(2,1)}, bf16[40,512]{1,0:T(8,128)(2,1)S(1)}, u32[]{:S(2)}, u32[]{:S(2)}) collective-permute-start(bf16[40,512]{1,0:T(8,128)(2,1)} %pick.1), channel_id=1, source_target_pairs={{0,1},{1,2},{2,3},{3,4},{4,5},{5,6},{6,7},{7,8},{8,9},{9,10},{10,1... | collective-permute-start | bytes 122888 | tf_op jit(solution)/shard_map/ppermute | solution.py:259
  28.3 4.1 %collective-permute-start.3 = (bf16[40,512]{1,0:T(8,128)(2,1)S(1)}, bf16[40,512]{1,0:T(8,128)(2,1)S(1)}, u32[]{:S(2)}, u32[]{:S(2)}) collective-permute-start(bf16[40,512]{1,0:T(8,128)(2,1)S(1)} %add_add_fusion.1), channel_id=1, source_target_pairs={{0,61},{1,62},{2,63},{3,0},{4,1},{5,2},{6,3},{7,4},{8,5},{9,6},{10... | collective-permute-start | bytes 122888 | tf_op jit(solution)/shard_map/ppermute | solution.py:259
  28.4 7.1 %collective-permute-start.2 = (bf16[40,512]{1,0:T(8,128)(2,1)S(1)}, bf16[40,512]{1,0:T(8,128)(2,1)S(1)}, u32[]{:S(2)}, u32[]{:S(2)}) collective-permute-start(bf16[40,512]{1,0:T(8,128)(2,1)S(1)} %add_add_fusion.1), channel_id=1, source_target_pairs={{0,3},{1,4},{2,5},{3,6},{4,7},{5,8},{6,9},{7,10},{8,11},{9,12},{10... | collective-permute-start | bytes 122888 | tf_op jit(solution)/shard_map/ppermute | solution.py:259
  35.5 5.3 %collective-permute-start.4 = (bf16[40,512]{1,0:T(8,128)(2,1)S(1)}, bf16[40,512]{1,0:T(8,128)(2,1)S(1)}, u32[]{:S(2)}, u32[]{:S(2)}) collective-permute-start(bf16[40,512]{1,0:T(8,128)(2,1)S(1)} %add_add_fusion), channel_id=1, source_target_pairs={{0,64},{64,0},{1,65},{65,1},{2,66},{66,2},{3,67},{67,3},{4,68},{68... | collective-permute-start | bytes 122888 | tf_op jit(solution)/shard_map/ppermute | solution.py:263
  115.2 5.1 %collective-permute-start.6 = (bf16[40,32768]{1,0:T(8,128)(2,1)}, bf16[40,32768]{1,0:T(8,128)(2,1)S(1)}, u32[]{:S(2)}, u32[]{:S(2)}) collective-permute-start(bf16[40,32768]{1,0:T(8,128)(2,1)} %get-tuple-element.7), channel_id=1, source_target_pairs={{0,64},{64,0},{1,65},{65,1},{2,66},{66,2},{3,67},{67,3},{4,68},{68... | collective-permute-start | bytes 7864328 | tf_op jit(solution)/shard_map/ppermute | solution.py:263
  120.3 1.5 %copy-start = (bf16[40,32768]{1,0:T(8,128)(2,1)}, bf16[40,32768]{1,0:T(8,128)(2,1)S(1)}, u32[]{:S(2)}) copy-start(bf16[40,32768]{1,0:T(8,128)(2,1)S(1)} %collective-permute-done.6.got_ref) | copy-start | bytes 7864324

commit v2 on v1

v2 whole, which is shorter than its diff:
```python
import jax
import jax.numpy as jnp
from jax import lax
from jax.experimental import pallas as pl
from jax.experimental.pallas import tpu as pltpu
from jax.sharding import PartitionSpec as P

MEMBERS = 80
HALF = 40
SD = 32768
K = 256
B = 2
LB = 128
CHIP = 2 * SD
CHIPS = 64
SEG_BLOCKS = SD // LB
CHUNK = 2048
STEPS = SD // CHUNK
CHUNK_BLOCKS = CHUNK // LB
PARTS = (7, 6, 3)
GROUP = 4
EXTRA = 16
DEPTH = MEMBERS + EXTRA
F32 = jnp.float32
BF16 = jnp.bfloat16
I32 = jnp.int32
NT = (((1,), (1,)), ((), ()))
VMEM_LIMIT = 40 * 1024 * 1024


def dot(a, b):
    return jnp.dot(a, b, preferred_element_type=F32)


def dot_nt(a, b):
    return lax.dot_general(a, b, NT, preferred_element_type=F32)


def iota(shape, dim):
    return lax.broadcasted_iota(I32, shape, dim)


def ones_where(mask):
    return mask.astype(F32).astype(BF16)


def whole(shape):
    return pl.BlockSpec(shape, lambda i, *s: (0,) * len(shape))


def pick_kernel(sp_ref, seg_ref, place_ref, x_ref, o_ref, xv, acc, owned, sems):
    parts = 4
    width = CHIP // parts
    copies = [
        pltpu.make_async_copy(
            x_ref.at[:, pl.ds(p * width, width)], xv.at[:, pl.ds(p * width, width)], sems.at[p]
        )
        for p in range(parts)
    ]
    for copy in copies:
        copy.start()
    acc[...] = jnp.zeros_like(acc)
    chip = sp_ref[2]
    n = I32(0)
    for b in range(B):

        def scan(k, n, b=b):
            owned[n] = b * K + k
            return n + ((seg_ref[b, k] >> 1) == chip).astype(I32)

        n = lax.fori_loop(0, K, scan, n, unroll=16)
    for j in range(4):
        owned[n + j] = B * K
    for copy in copies:
        copy.wait()
    lane = iota((HALF, LB), 1)

    def extract(i, _):
        for j in range(4):
            k = owned[4 * i + j]
            b = jnp.minimum(k >> 8, B - 1)
            within = k & (K - 1)
            at = (seg_ref[b, within] & 1) * SD + place_ref[b, within]
            start = pl.multiple_of((at >> 7) * LB, LB)
            tile = xv[:, pl.ds(start, LB)].astype(F32)
            turned = pltpu.roll(tile, (k - at) & (LB - 1), 1)
            pltpu.store(acc.at[k >> 7], turned, mask=lane == (k & (LB - 1)))
        return 0

    lax.fori_loop(0, (n + 3) >> 2, extract, 0)
    for g in range(B * K // LB):
        o_ref[:, g * LB : (g + 1) * LB] = acc[g].astype(BF16)


def pick(sp, segment, place, x):
    return pl.pallas_call(
        pick_kernel,
        grid_spec=pltpu.PrefetchScalarGridSpec(
            num_scalar_prefetch=3,
            grid=(1,),
            in_specs=[pl.BlockSpec(memory_space=pl.ANY)],
            out_specs=whole((HALF, B * K)),
            scratch_shapes=[
                pltpu.VMEM((HALF, CHIP), BF16),
                pltpu.VMEM((B * K // LB + 1, HALF, LB), F32),
                pltpu.SMEM((B * K + 8,), I32),
                pltpu.SemaphoreType.DMA((4,)),
            ],
        ),
        out_shape=jax.ShapeDtypeStruct((HALF, B * K), BF16),
        compiler_params=pltpu.CompilerParams(vmem_limit_bytes=VMEM_LIMIT),
        cost_estimate=pl.CostEstimate(flops=0, bytes_accessed=2 * HALF * CHIP, transcendentals=0),
        name="pick",
    )(sp, segment, place, x)


def places_kernel(
    sp_ref, seg_ref, place_ref, damp_ref, ext_ref, pick_ref, cols_ref, w_ref, count_ref
):
    first = sp_ref[1].astype(F32)
    last = first + (SEG_BLOCKS - 1)
    blocks = (seg_ref[...] * SEG_BLOCKS + (place_ref[...] >> 7)).astype(F32)
    reaches = ext_ref[...].astype(F32) + 1.0
    diagonal = iota((K, K), 0) == iota((K, K), 1)
    upper = ones_where(iota((K, K), 0) <= iota((K, K), 1))
    slots = iota((K, K), 0).astype(F32)
    most = I32(0)

    def column(mask, row):
        return jnp.sum(jnp.where(mask, row, 0.0), axis=1, keepdims=True)

    for b in range(B):
        block, reach, damping = blocks[b : b + 1], reaches[b : b + 1], damp_ref[b : b + 1, :]
        gap = jnp.maximum(jnp.maximum(first - block, block - last), 0.0)
        felt = (gap < reach).astype(F32)
        rank = dot(jnp.broadcast_to(felt, (8, K)).astype(BF16), upper)[0:1]
        chosen = jnp.where(felt > 0.0, rank - 1.0, -1.0) == slots
        most = jnp.maximum(most, jnp.sum(felt).astype(I32))
        pick_ref[b] = ones_where(chosen)
        cols_ref[b, 0] = jnp.broadcast_to(column(chosen, block), (K, LB))
        cols_ref[b, 1] = jnp.broadcast_to(jnp.maximum(column(chosen, reach), 1.0), (K, LB))
        cols_ref[b, 2] = jnp.broadcast_to(column(chosen, damping), (K, LB))
    count_ref[0] = most
    distance = jnp.abs(blocks[1:2] - column(diagonal, blocks[0:1]))
    reach = column(diagonal, reaches[0:1])
    damping = column(diagonal, damp_ref[0:1, :])
    w_ref[...] = damping * jnp.maximum(0.0, 1.0 - distance / reach)


def places(sp, segment, place, damping, extent):
    return pl.pallas_call(
        places_kernel,
        grid_spec=pltpu.PrefetchScalarGridSpec(
            num_scalar_prefetch=1,
            grid=(1,),
            in_specs=[whole((B, K))] * 4,
            out_specs=[
                whole((B, K, K)),
                whole((B, 3, K, LB)),
                whole((K, K)),
                pl.BlockSpec(memory_space=pltpu.SMEM),
            ],
        ),
        out_shape=[
            jax.ShapeDtypeStruct((B, K, K), BF16),
            jax.ShapeDtypeStruct((B, 3, K, LB), F32),
            jax.ShapeDtypeStruct((K, K), F32),
            jax.ShapeDtypeStruct((1,), I32),
        ],
        compiler_params=pltpu.CompilerParams(vmem_limit_bytes=VMEM_LIMIT),
        cost_estimate=pl.CostEstimate(
            flops=1_000_000, bytes_accessed=2_000_000, transcendentals=0
        ),
        name="places",
    )(sp, segment, place, damping, extent)


def observe_stats(prior, values, variances):
    centre = jnp.sum(prior, axis=0, keepdims=True) / MEMBERS
    anomaly = prior - centre
    prior_var = jnp.sum(anomaly * anomaly, axis=0, keepdims=True) / (MEMBERS - 1) + 1e-06
    post_var = 1.0 / (1.0 / prior_var + 1.0 / variances)
    post_mean = post_var * (centre / prior_var + values / variances)
    shrink = jnp.sqrt(post_var / prior_var)
    increment = (post_mean - centre + (shrink - 1.0) * anomaly).astype(BF16)
    scaled = (anomaly * (1.0 / ((MEMBERS - 1) * prior_var))).astype(BF16)
    left = jnp.sum(scaled.astype(F32), axis=0, keepdims=True) * (-1.0 / EXTRA)
    return increment, jnp.concatenate([scaled, jnp.broadcast_to(left, (EXTRA, K)).astype(BF16)], 0)


def with_extra(x):
    return jnp.concatenate([x, x[:EXTRA]], 0)


def stats_kernel(mine_ref, other_ref, val_ref, var_ref, pick_ref, w_ref, cov_ref, chg_ref):
    def prior(b):
        at = slice(b * K, (b + 1) * K)
        return jnp.concatenate([mine_ref[:, at].astype(F32), other_ref[:, at].astype(F32)], 0)

    increment0, scaled0 = observe_stats(prior(0), val_ref[0:1, :], var_ref[0:1, :])
    before = prior(1)
    eye = ones_where(iota((K, K), 0) == iota((K, K), 1))
    cov = dot(dot_nt(eye, scaled0).astype(BF16), with_extra(before.astype(BF16)))
    gain = (w_ref[...] * cov).astype(BF16)
    after = (before + dot(increment0, gain)).astype(BF16).astype(F32)
    increment1, scaled1 = observe_stats(after, val_ref[1:2, :], var_ref[1:2, :])
    for b, (increment, scaled) in enumerate(((increment0, scaled0), (increment1, scaled1))):
        cov_ref[b] = dot_nt(pick_ref[b], scaled).astype(BF16)
        chg_ref[b] = dot_nt(increment, pick_ref[b]).astype(BF16)


def stats(mine, other, readings, spread, picks, w):
    return pl.pallas_call(
        stats_kernel,
        grid=(1,),
        in_specs=[
            whole((HALF, B * K)),
            whole((HALF, B * K)),
            whole((B, K)),
            whole((B, K)),
            whole((B, K, K)),
            whole((K, K)),
        ],
        out_specs=[whole((B, K, DEPTH)), whole((B, MEMBERS, K))],
        out_shape=[
            jax.ShapeDtypeStruct((B, K, DEPTH), BF16),
            jax.ShapeDtypeStruct((B, MEMBERS, K), BF16),
        ],
        compiler_params=pltpu.CompilerParams(vmem_limit_bytes=VMEM_LIMIT),
        name="stats",
    )(mine, other, readings, spread, picks, w)


def update_kernel(begin, sp_ref, count_ref, cov_ref, chg_ref, cols, mine_ref, other_ref, *rest):
    own_ref, away_ref = rest[-2:]
    step = pl.program_id(0) + begin
    first = sp_ref[1].astype(F32)

    def weights(b, kc):
        block = (first + (step * CHUNK_BLOCKS).astype(F32)) + iota((kc, LB), 1).astype(F32)
        distance = jnp.abs(block - cols[b, 0, :kc])
        return cols[b, 2, :kc] * jnp.maximum(0.0, 1.0 - distance / cols[b, 1, :kc])

    def advance(kc):
        w = [weights(b, kc) for b in range(B)]
        for group in range(CHUNK // (256 * GROUP)):
            pairs = range(group * GROUP, (group + 1) * GROUP)
            at = [slice(p * 256, (p + 1) * 256) for p in pairs]
            wide = [
                jnp.concatenate([mine_ref[:, a].astype(F32), other_ref[:, a].astype(F32)], 0)
                for a in at
            ]
            for b in range(B):
                cov = [dot(cov_ref[b, :kc], with_extra(x.astype(BF16))) for x in wide]
                gain = [
                    jnp.concatenate(
                        [
                            c[:, h * LB : (h + 1) * LB]
                            * jnp.broadcast_to(w[b][:, 2 * p + h : 2 * p + h + 1], (kc, LB))
                            for h in range(2)
                        ],
                        1,
                    ).astype(BF16)
                    for p, c in zip(pairs, cov)
                ]
                wide = [x + dot(chg_ref[b, :, :kc], g) for x, g in zip(wide, gain)]
                if b == 0:
                    wide = [x.astype(BF16).astype(F32) for x in wide]
            for a, x in zip(at, wide):
                own_ref[:, a] = x[:HALF].astype(BF16)
                away_ref[:, a] = x[HALF:].astype(BF16)

    n = count_ref[0]

    @pl.when(n <= 64)
    def _():
        advance(64)

    @pl.when((n > 64) & (n <= 128))
    def _():
        advance(128)

    @pl.when(n > 128)
    def _():
        advance(K)


def update(begin, steps, sp, count, cov, chg, cols, x, got, out):
    half = lambda i, s, c: (0, s[0] * STEPS + begin + i)
    in_specs = [
        whole((B, K, DEPTH)),
        whole((B, MEMBERS, K)),
        whole((B, 3, K, LB)),
        pl.BlockSpec((HALF, CHUNK), half),
        pl.BlockSpec((HALF, CHUNK), half),
    ]
    operands = [sp, count, cov, chg, cols, x, got]
    aliases = {}
    if out is not None:
        in_specs.append(pl.BlockSpec(memory_space=pl.ANY))
        operands.append(out)
        aliases = {len(operands) - 1: 0}
    return pl.pallas_call(
        lambda *refs: update_kernel(begin, *refs),
        grid_spec=pltpu.PrefetchScalarGridSpec(
            num_scalar_prefetch=2,
            grid=(steps,),
            in_specs=in_specs,
            out_specs=[
                pl.BlockSpec((HALF, CHUNK), half),
                pl.BlockSpec((HALF, CHUNK), lambda i, s, c: (0, i)),
            ],
        ),
        out_shape=[
            jax.ShapeDtypeStruct((HALF, CHIP), BF16),
            jax.ShapeDtypeStruct((HALF, steps * CHUNK), BF16),
        ],
        input_output_aliases=aliases,
        compiler_params=pltpu.CompilerParams(vmem_limit_bytes=VMEM_LIMIT),
        cost_estimate=pl.CostEstimate(
            flops=600_000_000 * steps,
            bytes_accessed=4 * MEMBERS * CHUNK * steps,
            transcendentals=0,
        ),
        name=f"update{begin}",
    )(*operands)


def fill_kernel(sp_ref, got_ref, out_hbm, out_ref):
    out_ref[...] = got_ref[...]


def fill(begin, steps, sp, got, out):
    return pl.pallas_call(
        fill_kernel,
        grid_spec=pltpu.PrefetchScalarGridSpec(
            num_scalar_prefetch=1,
            grid=(steps,),
            in_specs=[
                pl.BlockSpec((HALF, CHUNK), lambda i, s: (0, i)),
                pl.BlockSpec(memory_space=pl.ANY),
            ],
            out_specs=pl.BlockSpec(
                (HALF, CHUNK), lambda i, s: (0, (1 - s[0]) * STEPS + begin + i)
            ),
        ),
        out_shape=jax.ShapeDtypeStruct((HALF, CHIP), BF16),
        input_output_aliases={2: 0},
        compiler_params=pltpu.CompilerParams(vmem_limit_bytes=VMEM_LIMIT),
        name=f"fill{begin}",
    )(sp, got, out)


def shifted(array, by):
    pairs = [(i, (i + by) % CHIPS) for i in range(CHIPS)]
    return lax.ppermute(array, "state", pairs)


def swapped(array):
    return lax.ppermute(array, "mem", [(0, 1), (1, 0)])


def on_device(x, segment, place, readings, spread, damping, extent):
    core = lax.axis_index("mem")
    chip = lax.axis_index("state")
    sp = jnp.stack([core, (chip * 2 + core) * SEG_BLOCKS, chip]).astype(I32)

    picked = pick(sp, segment, place, x)
    x, picked = lax.optimization_barrier((x, picked))
    up, down = shifted(picked, 1), shifted(picked, -1)
    got = swapped(x)
    picks, cols, w, count = places(sp, segment, place, damping, extent)
    near = picked + up + down
    near, picks, cols, w, count = lax.optimization_barrier((near, picks, cols, w, count))
    far = near + shifted(near, 3) + shifted(near, -3)
    cov, chg = stats(far, swapped(far), readings, spread, picks, w)
    out = None
    away = []
    begin = 0
    for steps in PARTS:
        out, part = update(begin, steps, sp, count, cov, chg, cols, x, got, out)
        away.append((begin, steps, swapped(part)))
        begin += steps
    for begin, steps, part in away:
        out = fill(begin, steps, sp, part, out)
    return out


def solution(mesh):
    in_specs = (P("mem", "state"), P(), P(), P(), P(), P(), P())
    return jax.shard_map(
        on_device, mesh=mesh, in_specs=in_specs, out_specs=P("mem", "state"), check_vma=False
    )
```

time: 127 us -> 72.3 us (0.57)
  Pallas kernels: 77.9 us -> 41.4 us
  local copies, waits for them, and re-layouts: 8.58 us -> 1.38 us
  other arithmetic: 6.46 us -> 0.1 us
  waiting for transfers between devices: 17.9 us -> 12.1 us
  starting transfers between devices: 15.5 us -> 17.6 us
    pallas_call x1 -> x5, Pallas kernels: 69.3 us -> 30.2 us  [the longest x3 28 us: update(): pl.pallas_call(lambda *refs: update_kernel(begin, *refs), grid_spec=pltpu...]
    concatenate x3 -> x0, other arithmetic: 5.09 us -> none  [the longest x1 4.37 us: on_device(): whole = jnp.concatenate([kept, swapped(sent)], 0)]
    dynamic_slice x1 -> x0, local copies, waits for them, and re-layouts: 4.38 us -> none  [on_device(): kept = lax.dynamic_slice_in_dim(x, core * SD, SD, 1)]
    ppermute x3 -> x5, waiting for transfers between devices: 5.11 us -> 0.88 us  [swapped(): return lax.ppermute(array, 'mem', [(0, 1), (1, 0)])]
    pallas_call x1 -> x3, Pallas kernels: 4.66 us -> 7.99 us  [fill(): pl.pallas_call(fill_kernel, grid_spec=pltpu.PrefetchScalarGridSpec(num_sc...]
    concatenate x4 -> x0, local copies, waits for them, and re-layouts: 2.67 us -> none  [the longest x1 1.22 us: on_device(): jnp.concatenate([block, reach, damping, readings, spread, jnp.zeros((6, K...]
    ppermute x4, waiting for transfers between devices: 12.8 us -> 11.2 us  [shifted(): return lax.ppermute(array, 'state', pairs)]
    ppermute x3 -> x5, starting transfers between devices: 4.17 us -> 5.04 us  [swapped(): return lax.ppermute(array, 'mem', [(0, 1), (1, 0)])]
  transfers between devices with their start and end apart: 7 -> 9, of which waited for: 5 -> 4; matrix products, arithmetic and copies ran while one was open for 4% -> 0% of each run, Pallas kernels for 3% -> 34%
where the time goes in v2:
time: 72.3 us; the launch traced here: 72.7 us
  Pallas kernels  41.4 us (57%)
  starting transfers between devices  17.6 us (24%)
  waiting for transfers between devices  12.1 us (17%)
  local copies, waits for them, and re-layouts  1.38 us (2%)
    pallas_call x3, Pallas kernels, update(): pl.pallas_call(lambda *refs: update_kernel(begin, *refs), grid_spec=pltpu...  28 us
    ppermute x4, starting transfers between devices, shifted(): return lax.ppermute(array, 'state', pairs)  12.5 us
    ppermute x4, waiting for transfers between devices, shifted(): return lax.ppermute(array, 'state', pairs)  11.2 us
    pallas_call x3, Pallas kernels, fill(): pl.pallas_call(fill_kernel, grid_spec=pltpu.PrefetchScalarGridSpec(num_sc...  7.99 us
    ppermute x5, starting transfers between devices, swapped(): return lax.ppermute(array, 'mem', [(0, 1), (1, 0)])  5.04 us
    pallas_call x1, Pallas kernels, pick(): pl.pallas_call(pick_kernel, grid_spec=pltpu.PrefetchScalarGridSpec(num_sc...  3.23 us
    pallas_call x1, Pallas kernels, places(): pl.pallas_call(places_kernel, grid_spec=pltpu.PrefetchScalarGridSpec(num_...  1.48 us
  transfers between devices with their start and end apart: 9, of which 4 were waited for; matrix products, arithmetic and copies ran while one was open for 0% of the time, Pallas kernels for 34%

profile of v2, /device:TPU:1, one launch (start us, length us, event | category | flops | bytes accessed | tf_op | source)
XLA Modules:
  0.0 72.7 jit_solution(7647295370238875729)
XLA Ops:
  0.0 0.1 pad_add_fusion.sp_ref.refs_0_
  0.1 0.7 copy-done
  0.8 0.7 copy-done.1
  1.5 3.2 %pick.1 = bf16[40,512]{1,0:T(8,128)(2,1)S(1)} custom-call(s32[3]{0:T(128)S(1)} %pad_add_fusion.sp_ref.refs_0_, s32[2,256]{1,0:T(2,128)S(1)} %copy-done, s32[2,256]{1,0:T(2,128)S(1)} %copy-done.1, bf16[40,65536]{1,0:T(8,128)(2,1)} %refs_5_.2), custom_call_target="tpu_custom_call" | custom-call | bytes 5242880 | tf_op jit(solution)/shard_map/pick/pallas_call | solution.py:96
  4.7 1.4 %collective-permute-start.5 = (bf16[40,65536]{1,0:T(8,128)(2,1)}, bf16[40,65536]{1,0:T(8,128)(2,1)S(1)}, u32[]{:S(2)}, u32[]{:S(2)}) collective-permute-start(bf16[40,65536]{1,0:T(8,128)(2,1)} %refs_5_.2), channel_id=1, source_target_pairs={{0,64},{64,0},{1,65},{65,1},{2,66},{66,2},{3,67},{67,3},{4,68},{68... | collective-permute-start | bytes 15728648 | tf_op jit(solution)/shard_map/ppermute | solution.py:360
  6.1 9.8 %collective-permute-start.1 = (bf16[40,512]{1,0:T(8,128)(2,1)S(1)}, bf16[40,512]{1,0:T(8,128)(2,1)S(1)}, u32[]{:S(2)}, u32[]{:S(2)}) collective-permute-start(bf16[40,512]{1,0:T(8,128)(2,1)S(1)} %pick.1), channel_id=1, source_target_pairs={{0,63},{1,0},{2,1},{3,2},{4,3},{5,4},{6,5},{7,6},{8,7},{9,8},{10,9... | collective-permute-start | bytes 122888 | tf_op jit(solution)/shard_map/ppermute | solution.py:356
  15.9 1.5 %places.1 = (bf16[2,256,256]{2,1,0:T(8,128)(2,1)S(1)}, f32[2,3,256,128]{3,2,1,0:T(8,128)S(1)}, f32[256,256]{1,0:T(8,128)S(1)}, s32[1]{0:T(128)}) custom-call(s32[3]{0:T(128)S(1)} %pad_add_fusion.sp_ref.refs_0_, s32[2,256]{1,0:T(2,128)S(1)} %copy-done, s32[2,256]{1,0:T(2,128)S(1)} %copy-done.1, f32[2,256]{1,0:T(2,128)S(1)} %copy-done.4, s32[2,256]{1,0:T(2,128)S(1)} %copy-done.5), custom_call_target="tpu_custom_call" | custom-call | flops 1000000 | bytes 2000000 | tf_op jit(solution)/shard_map/places/pallas_call | solution.py:151
  17.4 6.8 %collective-permute-done = bf16[40,512]{1,0:T(8,128)(2,1)S(1)} collective-permute-done((bf16[40,512]{1,0:T(8,128)(2,1)S(1)}, bf16[40,512]{1,0:T(8,128)(2,1)S(1)}, u32[]{:S(2)}, u32[]{:S(2)}) %collective-permute-start) | collective-permute-done | bytes 40992 | tf_op jit(solution)/shard_map/ppermute | solution.py:356
  24.2 0.1 collective-permute-start.3
  24.3 2.7 %collective-permute-start.2 = (bf16[40,512]{1,0:T(8,128)(2,1)S(1)}, bf16[40,512]{1,0:T(8,128)(2,1)S(1)}, u32[]{:S(2)}, u32[]{:S(2)}) collective-permute-start(bf16[40,512]{1,0:T(8,128)(2,1)S(1)} %add_add_fusion.1), channel_id=1, source_target_pairs={{0,3},{1,4},{2,5},{3,6},{4,7},{5,8},{6,9},{7,10},{8,11},{9,12},{10... | collective-permute-start | bytes 122888 | tf_op jit(solution)/shard_map/ppermute | solution.py:356
  27.0 1.4 %collective-permute-done.3 = bf16[40,512]{1,0:T(8,128)(2,1)S(1)} collective-permute-done((bf16[40,512]{1,0:T(8,128)(2,1)S(1)}, bf16[40,512]{1,0:T(8,128)(2,1)S(1)}, u32[]{:S(2)}, u32[]{:S(2)}) %collective-permute-start.3) | collective-permute-done | bytes 40992 | tf_op jit(solution)/shard_map/ppermute | solution.py:356
  28.4 3.1 %collective-permute-done.2 = bf16[40,512]{1,0:T(8,128)(2,1)S(1)} collective-permute-done((bf16[40,512]{1,0:T(8,128)(2,1)S(1)}, bf16[40,512]{1,0:T(8,128)(2,1)S(1)}, u32[]{:S(2)}, u32[]{:S(2)}) %collective-permute-start.2) | collective-permute-done | bytes 40992 | tf_op jit(solution)/shard_map/ppermute | solution.py:356
  31.5 2.7 %collective-permute-start.4 = (bf16[40,512]{1,0:T(8,128)(2,1)S(1)}, bf16[40,512]{1,0:T(8,128)(2,1)S(1)}, u32[]{:S(2)}, u32[]{:S(2)}) collective-permute-start(bf16[40,512]{1,0:T(8,128)(2,1)S(1)} %add_add_fusion.mine_ref), channel_id=1, source_target_pairs={{0,64},{64,0},{1,65},{65,1},{2,66},{66,2},{3,67},{67,3},{4,68},{68... | collective-permute-start | bytes 122888 | tf_op jit(solution)/shard_map/ppermute | solution.py:360
  34.2 0.9 %collective-permute-done.4.other_ref = bf16[40,512]{1,0:T(8,128)(2,1)S(1)} collective-permute-done((bf16[40,512]{1,0:T(8,128)(2,1)S(1)}, bf16[40,512]{1,0:T(8,128)(2,1)S(1)}, u32[]{:S(2)}, u32[]{:S(2)}) %collective-permute-start.4) | collective-permute-done | bytes 40992 | tf_op jit(solution)/shard_map/ppermute | solution.py:360
  35.1 0.8 %stats.1 = (bf16[2,256,96]{2,1,0:T(8,128)(2,1)S(1)}, bf16[2,80,256]{2,1,0:T(8,128)(2,1)S(1)}) custom-call(bf16[40,512]{1,0:T(8,128)(2,1)S(1)} %add_add_fusion.mine_ref, bf16[40,512]{1,0:T(8,128)(2,1)S(1)} %collective-permute-done.4.other_ref, f32[2,256]{1,0:T(2,128)S(1)} %copy-done.2, f32[2,256]{1,0:T(2,128)S(1)} %copy-done.3, ...), custom_call_target="tpu_custom_call" | custom-call | tf_op jit(solution)/shard_map/stats/pallas_call | solution.py:213
  35.9 11.4 %update0.1 = (bf16[40,65536]{1,0:T(8,128)(2,1)}, bf16[40,14336]{1,0:T(8,128)(2,1)S(1)}) custom-call(s32[3]{0:T(128)S(1)} %pad_add_fusion.sp_ref.refs_0_, s32[1]{0:T(128)} %get-tuple-element.29.refs_1_, bf16[2,256,96]{2,1,0:T(8,128)(2,1)S(1)} %get-tuple-element.33.refs_2_, bf16[2,80,256]{2,1,0:T(8,128)(2,1)S(1)} %get-tuple-element.34.refs_3_, ...), custom_call_target="tpu_custom_call" | custom-call | flops 4200000000 | bytes 4587520 | tf_op jit(solution)/shard_map/update0/pallas_call | solution.py:303
  47.2 0.4 collective-permute-start.8
  47.6 10.1 %update7.1 = (bf16[40,65536]{1,0:T(8,128)(2,1)}, bf16[40,12288]{1,0:T(8,128)(2,1)S(1)}) custom-call(s32[3]{0:T(128)S(1)} %pad_add_fusion.sp_ref.refs_0_, s32[1]{0:T(128)} %get-tuple-element.29.refs_1_, bf16[2,256,96]{2,1,0:T(8,128)(2,1)S(1)} %get-tuple-element.33.refs_2_, ...), custom_call_target="tpu_custom_call", output_to_operand_aliasing={{0}: (7, {})} | custom-call | flops 3600000000 | bytes 3932160 | tf_op jit(solution)/shard_map/update7/pallas_call | solution.py:303
  57.7 0.2 collective-permute-start.7
  57.9 6.5 %update13.1 = (bf16[40,65536]{1,0:T(8,128)(2,1)}, bf16[40,6144]{1,0:T(8,128)(2,1)S(1)}) custom-call(s32[3]{0:T(128)S(1)} %pad_add_fusion.sp_ref.refs_0_, s32[1]{0:T(128)} %get-tuple-element.29.refs_1_, bf16[2,256,96]{2,1,0:T(8,128)(2,1)S(1)} %get-tuple-element.33.refs_2_, ...), custom_call_target="tpu_custom_call", output_to_operand_aliasing={{0}: (7, {})} | custom-call | flops 1800000000 | bytes 1966080 | tf_op jit(solution)/shard_map/update13/pallas_call | solution.py:303
  64.3 0.4 collective-permute-start.6
  64.7 3.3 %fill0.1.out_hbm = bf16[40,65536]{1,0:T(8,128)(2,1)} custom-call(s32[3]{0:T(128)S(1)} %pad_add_fusion.sp_ref.refs_0_, bf16[40,14336]{1,0:T(8,128)(2,1)S(1)} %collective-permute-done.8.got_ref, bf16[40,65536]{1,0:T(8,128)(2,1)} %get-tuple-element.42.out_hbm), custom_call_target="tpu_custom_call", output_to_operand_aliasing={{}: (2, {})} | custom-call | tf_op jit(solution)/shard_map/fill0/pallas_call | solution.py:334
  68.0 2.7 %fill7.1.out_hbm = bf16[40,65536]{1,0:T(8,128)(2,1)} custom-call(s32[3]{0:T(128)S(1)} %pad_add_fusion.sp_ref.refs_0_, bf16[40,12288]{1,0:T(8,128)(2,1)S(1)} %collective-permute-done.7.got_ref, bf16[40,65536]{1,0:T(8,128)(2,1)} %fill0.1.out_hbm), custom_call_target="tpu_custom_call", output_to_operand_aliasing={{}: (2, {})} | custom-call | tf_op jit(solution)/shard_map/fill7/pallas_call | solution.py:334
  70.7 2.0 %fill13.1 = bf16[40,65536]{1,0:T(8,128)(2,1)} custom-call(s32[3]{0:T(128)S(1)} %pad_add_fusion.sp_ref.refs_0_, bf16[40,6144]{1,0:T(8,128)(2,1)S(1)} %collective-permute-done.6.got_ref, bf16[40,65536]{1,0:T(8,128)(2,1)} %fill7.1.out_hbm), custom_call_target="tpu_custom_call", output_to_operand_aliasing={{}: (2, {})} | custom-call | tf_op jit(solution)/shard_map/fill13/pallas_call | solution.py:334
  (18 shorter events, 0.1 us)
Async XLA Ops:
  0.0 15.9 %copy-start.5 = (s32[2,256]{1,0:T(2,128)S(1)}, s32[2,256]{1,0:T(2,128)}, u32[]{:S(2)}) copy-start(s32[2,256]{1,0:T(2,128)} %ext_ref.1) | copy-start | bytes 6148
  0.0 15.9 %copy-start.4 = (f32[2,256]{1,0:T(2,128)S(1)}, f32[2,256]{1,0:T(2,128)}, u32[]{:S(2)}) copy-start(f32[2,256]{1,0:T(2,128)} %damp_ref.1) | copy-start | bytes 6148
  0.0 35.1 %copy-start.3 = (f32[2,256]{1,0:T(2,128)S(1)}, f32[2,256]{1,0:T(2,128)}, u32[]{:S(2)}) copy-start(f32[2,256]{1,0:T(2,128)} %var_ref.1) | copy-start | bytes 6148
  0.0 35.1 %copy-start.2 = (f32[2,256]{1,0:T(2,128)S(1)}, f32[2,256]{1,0:T(2,128)}, u32[]{:S(2)}) copy-start(f32[2,256]{1,0:T(2,128)} %val_ref.1) | copy-start | bytes 6148
  0.1 0.7 copy-start
  0.8 0.7 copy-start.1
  4.7 31.2 %collective-permute-start.5 = (bf16[40,65536]{1,0:T(8,128)(2,1)}, bf16[40,65536]{1,0:T(8,128)(2,1)S(1)}, u32[]{:S(2)}, u32[]{:S(2)}) collective-permute-start(bf16[40,65536]{1,0:T(8,128)(2,1)} %refs_5_.2), channel_id=1, source_target_pairs={{0,64},{64,0},{1,65},{65,1},{2,66},{66,2},{3,67},{67,3},{4,68},{68... | collective-permute-start | bytes 15728648 | tf_op jit(solution)/shard_map/ppermute | solution.py:360
  6.1 11.3 %collective-permute-start.1 = (bf16[40,512]{1,0:T(8,128)(2,1)S(1)}, bf16[40,512]{1,0:T(8,128)(2,1)S(1)}, u32[]{:S(2)}, u32[]{:S(2)}) collective-permute-start(bf16[40,512]{1,0:T(8,128)(2,1)S(1)} %pick.1), channel_id=1, source_target_pairs={{0,63},{1,0},{2,1},{3,2},{4,3},{5,4},{6,5},{7,6},{8,7},{9,8},{10,9... | collective-permute-start | bytes 122888 | tf_op jit(solution)/shard_map/ppermute | solution.py:356
  15.9 8.3 %collective-permute-start = (bf16[40,512]{1,0:T(8,128)(2,1)S(1)}, bf16[40,512]{1,0:T(8,128)(2,1)S(1)}, u32[]{:S(2)}, u32[]{:S(2)}) collective-permute-start(bf16[40,512]{1,0:T(8,128)(2,1)S(1)} %pick.1), channel_id=1, source_target_pairs={{0,1},{1,2},{2,3},{3,4},{4,5},{5,6},{6,7},{7,8},{8,9},{9,10},{10,1... | collective-permute-start | bytes 122888 | tf_op jit(solution)/shard_map/ppermute | solution.py:356
  24.2 4.1 %collective-permute-start.3 = (bf16[40,512]{1,0:T(8,128)(2,1)S(1)}, bf16[40,512]{1,0:T(8,128)(2,1)S(1)}, u32[]{:S(2)}, u32[]{:S(2)}) collective-permute-start(bf16[40,512]{1,0:T(8,128)(2,1)S(1)} %add_add_fusion.1), channel_id=1, source_target_pairs={{0,61},{1,62},{2,63},{3,0},{4,1},{5,2},{6,3},{7,4},{8,5},{9,6},{10... | collective-permute-start | bytes 122888 | tf_op jit(solution)/shard_map/ppermute | solution.py:356
  24.3 7.1 %collective-permute-start.2 = (bf16[40,512]{1,0:T(8,128)(2,1)S(1)}, bf16[40,512]{1,0:T(8,128)(2,1)S(1)}, u32[]{:S(2)}, u32[]{:S(2)}) collective-permute-start(bf16[40,512]{1,0:T(8,128)(2,1)S(1)} %add_add_fusion.1), channel_id=1, source_target_pairs={{0,3},{1,4},{2,5},{3,6},{4,7},{5,8},{6,9},{7,10},{8,11},{9,12},{10... | collective-permute-start | bytes 122888 | tf_op jit(solution)/shard_map/ppermute | solution.py:356
  31.5 3.6 %collective-permute-start.4 = (bf16[40,512]{1,0:T(8,128)(2,1)S(1)}, bf16[40,512]{1,0:T(8,128)(2,1)S(1)}, u32[]{:S(2)}, u32[]{:S(2)}) collective-permute-start(bf16[40,512]{1,0:T(8,128)(2,1)S(1)} %add_add_fusion.mine_ref), channel_id=1, source_target_pairs={{0,64},{64,0},{1,65},{65,1},{2,66},{66,2},{3,67},{67,3},{4,68},{68... | collective-permute-start | bytes 122888 | tf_op jit(solution)/shard_map/ppermute | solution.py:360
  47.2 17.5 %collective-permute-start.8 = (bf16[40,14336]{1,0:T(8,128)(2,1)S(1)}, bf16[40,14336]{1,0:T(8,128)(2,1)S(1)}, u32[]{:S(2)}, u32[]{:S(2)}) collective-permute-start(bf16[40,14336]{1,0:T(8,128)(2,1)S(1)} %get-tuple-element.41), channel_id=1, source_target_pairs={{0,64},{64,0},{1,65},{65,1},{2,66},{66,2},{3,67},{67,3},{4,68},{68... | collective-permute-start | bytes 3440648 | tf_op jit(solution)/shard_map/ppermute | solution.py:360
  57.7 10.3 %collective-permute-start.7 = (bf16[40,12288]{1,0:T(8,128)(2,1)S(1)}, bf16[40,12288]{1,0:T(8,128)(2,1)S(1)}, u32[]{:S(2)}, u32[]{:S(2)}) collective-permute-start(bf16[40,12288]{1,0:T(8,128)(2,1)S(1)} %get-tuple-element.40), channel_id=1, source_target_pairs={{0,64},{64,0},{1,65},{65,1},{2,66},{66,2},{3,67},{67,3},{4,68},{68... | collective-permute-start | bytes 2949128 | tf_op jit(solution)/shard_map/ppermute | solution.py:360
  64.3 6.4 %collective-permute-start.6 = (bf16[40,6144]{1,0:T(8,128)(2,1)S(1)}, bf16[40,6144]{1,0:T(8,128)(2,1)S(1)}, u32[]{:S(2)}, u32[]{:S(2)}) collective-permute-start(bf16[40,6144]{1,0:T(8,128)(2,1)S(1)} %get-tuple-element.39), channel_id=1, source_target_pairs={{0,64},{64,0},{1,65},{65,1},{2,66},{66,2},{3,67},{67,3},{4,68},{68... | collective-permute-start | bytes 1474568 | tf_op jit(solution)/shard_map/ppermute | solution.py:360

commit v3 on v2

--- a/solution.py
+++ b/solution.py
@@ -26,6 +26,7 @@
 I32 = jnp.int32
 NT = (((1,), (1,)), ((), ()))
 VMEM_LIMIT = 40 * 1024 * 1024
+PICK_LIMIT = 40 * 1024 * 1024
 
 
 def dot(a, b):
@@ -48,7 +49,7 @@
     return pl.BlockSpec(shape, lambda i, *s: (0,) * len(shape))
 
 
-def pick_kernel(sp_ref, seg_ref, place_ref, x_ref, o_ref, xv, acc, owned, sems):
+def pick_kernel(sp_ref, index_ref, x_ref, o_ref, xv, acc, owned, sems):
     parts = 4
     width = CHIP // parts
     copies = [
@@ -66,7 +67,7 @@
 
         def scan(k, n, b=b):
             owned[n] = b * K + k
-            return n + ((seg_ref[b, k] >> 1) == chip).astype(I32)
+            return n + ((index_ref[b, k] >> 16) == chip).astype(I32)
 
         n = lax.fori_loop(0, K, scan, n, unroll=16)
     for j in range(4):
@@ -80,7 +81,7 @@
             k = owned[4 * i + j]
             b = jnp.minimum(k >> 8, B - 1)
             within = k & (K - 1)
-            at = (seg_ref[b, within] & 1) * SD + place_ref[b, within]
+            at = index_ref[b, within] & (CHIP - 1)
             start = pl.multiple_of((at >> 7) * LB, LB)
             tile = xv[:, pl.ds(start, LB)].astype(F32)
             turned = pltpu.roll(tile, (k - at) & (LB - 1), 1)
@@ -92,11 +93,11 @@
         o_ref[:, g * LB : (g + 1) * LB] = acc[g].astype(BF16)
 
 
-def pick(sp, segment, place, x):
+def pick(sp, index, x):
     return pl.pallas_call(
         pick_kernel,
         grid_spec=pltpu.PrefetchScalarGridSpec(
-            num_scalar_prefetch=3,
+            num_scalar_prefetch=2,
             grid=(1,),
             in_specs=[pl.BlockSpec(memory_space=pl.ANY)],
             out_specs=whole((HALF, B * K)),
@@ -108,10 +109,10 @@
             ],
         ),
         out_shape=jax.ShapeDtypeStruct((HALF, B * K), BF16),
-        compiler_params=pltpu.CompilerParams(vmem_limit_bytes=VMEM_LIMIT),
+        compiler_params=pltpu.CompilerParams(vmem_limit_bytes=PICK_LIMIT),
         cost_estimate=pl.CostEstimate(flops=0, bytes_accessed=2 * HALF * CHIP, transcendentals=0),
         name="pick",
-    )(sp, segment, place, x)
+    )(sp, index, x)
 
 
 def places_kernel(
@@ -272,7 +273,11 @@
 
     n = count_ref[0]
 
-    @pl.when(n <= 64)
+    @pl.when(n <= 32)
+    def _():
+        advance(32)
+
+    @pl.when((n > 32) & (n <= 64))
     def _():
         advance(64)
 
@@ -287,10 +292,7 @@
 
 def update(begin, steps, sp, count, cov, chg, cols, x, got, out):
     half = lambda i, s, c: (0, s[0] * STEPS + begin + i)
-    in_specs = [
-        whole((B, K, DEPTH)),
-        whole((B, MEMBERS, K)),
-        whole((B, 3, K, LB)),
+    in_specs = [pl.BlockSpec(memory_space=pltpu.VMEM)] * 3 + [
         pl.BlockSpec((HALF, CHUNK), half),
         pl.BlockSpec((HALF, CHUNK), half),
     ]
@@ -326,34 +328,47 @@
     )(*operands)
 
 
-def fill_kernel(sp_ref, got_ref, out_hbm, out_ref):
-    out_ref[...] = got_ref[...]
-
-
-def fill(begin, steps, sp, got, out):
+def fill(begins, sp, parts, out):
+    def kernel(sp_ref, *refs):
+        out_ref, sems = refs[-2:]
+        base = (1 - sp_ref[0]) * SD
+        copies = []
+        for j, (begin, part) in enumerate(zip(begins, refs[: len(parts)])):
+            start = pl.multiple_of(base + begin * CHUNK, CHUNK)
+            to = out_ref.at[:, pl.ds(start, part.shape[1])]
+            copies.append(pltpu.make_async_copy(part, to, sems.at[j]))
+        for copy in copies:
+            copy.start()
+        for copy in copies:
+            copy.wait()
+
     return pl.pallas_call(
-        fill_kernel,
+        kernel,
         grid_spec=pltpu.PrefetchScalarGridSpec(
             num_scalar_prefetch=1,
-            grid=(steps,),
-            in_specs=[
-                pl.BlockSpec((HALF, CHUNK), lambda i, s: (0, i)),
-                pl.BlockSpec(memory_space=pl.ANY),
-            ],
-            out_specs=pl.BlockSpec(
-                (HALF, CHUNK), lambda i, s: (0, (1 - s[0]) * STEPS + begin + i)
-            ),
+            grid=(1,),
+            in_specs=[pl.BlockSpec(memory_space=pltpu.VMEM)] * len(parts)
+            + [pl.BlockSpec(memory_space=pl.ANY)],
+            out_specs=pl.BlockSpec(memory_space=pl.ANY),
+            scratch_shapes=[pltpu.SemaphoreType.DMA((len(parts),))],
         ),
         out_shape=jax.ShapeDtypeStruct((HALF, CHIP), BF16),
-        input_output_aliases={2: 0},
+        input_output_aliases={1 + len(parts): 0},
         compiler_params=pltpu.CompilerParams(vmem_limit_bytes=VMEM_LIMIT),
-        name=f"fill{begin}",
-    )(sp, got, out)
-
-
-def shifted(array, by):
-    pairs = [(i, (i + by) % CHIPS) for i in range(CHIPS)]
-    return lax.ppermute(array, "state", pairs)
+        name=f"fill{begins[0]}",
+    )(sp, *parts, out)
+
+
+def sent(array, target):
+    return lax.ppermute(array, "state", [(i, target(i)) for i in range(CHIPS)])
+
+
+def along_row(array, by):
+    return sent(array, lambda i: i // 4 * 4 + (i + by) % 4)
+
+
+def across_rows(array, by):
+    return sent(array, lambda i: (i + 4 * by) % CHIPS)
 
 
 def swapped(array):
@@ -365,24 +380,24 @@
     chip = lax.axis_index("state")
     sp = jnp.stack([core, (chip * 2 + core) * SEG_BLOCKS, chip]).astype(I32)
 
-    picked = pick(sp, segment, place, x)
+    picked = pick(sp, segment * SD + place, x)
     x, picked = lax.optimization_barrier((x, picked))
-    up, down = shifted(picked, 1), shifted(picked, -1)
+    two, one, three = (along_row(picked, by) for by in (2, 1, 3))
     got = swapped(x)
     picks, cols, w, count = places(sp, segment, place, damping, extent)
-    near = picked + up + down
+    near = picked + one + two + three
     near, picks, cols, w, count = lax.optimization_barrier((near, picks, cols, w, count))
-    far = near + shifted(near, 3) + shifted(near, -3)
+    far = near + across_rows(near, 1) + across_rows(near, -1)
     cov, chg = stats(far, swapped(far), readings, spread, picks, w)
     out = None
     away = []
     begin = 0
     for steps in PARTS:
         out, part = update(begin, steps, sp, count, cov, chg, cols, x, got, out)
-        away.append((begin, steps, swapped(part)))
+        away.append((begin, swapped(part)))
         begin += steps
-    for begin, steps, part in away:
-        out = fill(begin, steps, sp, part, out)
+    for some in (away[:-1], away[-1:]):
+        out = fill([begin for begin, _ in some], sp, [part for _, part in some], out)
     return out
 
 

time: 72.3 us -> 60.6 us (0.84)
  Pallas kernels: 41.4 us -> 34.8 us
  starting transfers between devices: 17.6 us -> 14.7 us
  waiting for transfers between devices: 12.1 us -> 9.78 us
  local copies, waits for them, and re-layouts: 1.38 us -> 0.02 us
  other arithmetic: 0.1 us -> 0.85 us
    pallas_call x3 -> x2, Pallas kernels: 7.99 us -> 3.22 us  [fill(): pl.pallas_call(kernel, grid_spec=pltpu.PrefetchScalarGridSpec(num_scalar_...]
    ppermute x4 -> x5, starting transfers between devices: 12.5 us -> 9.26 us  [sent(): return lax.ppermute(array, 'state', [(i, target(i)) for i in range(CHIPS)])]
    ppermute x4 -> x5, waiting for transfers between devices: 11.2 us -> 8.9 us  [sent(): return lax.ppermute(array, 'state', [(i, target(i)) for i in range(CHIPS)])]
    pallas_call x3, Pallas kernels: 28 us -> 26.2 us  [update(): pl.pallas_call(lambda *refs: update_kernel(begin, *refs), grid_spec=pltpu...]
    unnamed x12, local copies, waits for them, and re-layouts: 1.38 us -> 0.02 us
    add x2 -> x3, other arithmetic: 0.02 us -> 0.77 us  [the longest x1 0.75 us: on_device(): picked = pick(sp, segment * SD + place, x)]
  transfers between devices with their start and end apart: 9 -> 10, of which waited for: 4 -> 5; matrix products, arithmetic and copies ran while one was open for 0% -> 0% of each run, Pallas kernels for 34% -> 33%
where the time goes in v3:
time: 60.6 us; the launch traced here: 60.5 us
  Pallas kernels  34.8 us (57%)
  starting transfers between devices  14.7 us (24%)
  waiting for transfers between devices  9.78 us (16%)
  other arithmetic  0.85 us (1%)
    pallas_call x3, Pallas kernels, update(): pl.pallas_call(lambda *refs: update_kernel(begin, *refs), grid_spec=pltpu...  26.2 us
    ppermute x5, starting transfers between devices, sent(): return lax.ppermute(array, 'state', [(i, target(i)) for i in range(CHIPS)])  9.26 us
    ppermute x5, waiting for transfers between devices, sent(): return lax.ppermute(array, 'state', [(i, target(i)) for i in range(CHIPS)])  8.9 us
    ppermute x5, starting transfers between devices, swapped(): return lax.ppermute(array, 'mem', [(0, 1), (1, 0)])  5.44 us
    pallas_call x2, Pallas kernels, fill(): pl.pallas_call(kernel, grid_spec=pltpu.PrefetchScalarGridSpec(num_scalar_...  3.22 us
    pallas_call x1, Pallas kernels, pick(): pl.pallas_call(pick_kernel, grid_spec=pltpu.PrefetchScalarGridSpec(num_sc...  3.2 us
    pallas_call x1, Pallas kernels, places(): pl.pallas_call(places_kernel, grid_spec=pltpu.PrefetchScalarGridSpec(num_...  1.48 us
  transfers between devices with their start and end apart: 10, of which 5 were waited for; matrix products, arithmetic and copies ran while one was open for 0% of the time, Pallas kernels for 33%

profile of v3, /device:TPU:1, one launch (start us, length us, event | category | flops | bytes accessed | tf_op | source)
XLA Modules:
  0.0 60.5 jit_solution(1040301078342733186)
XLA Ops:
  0.0 0.7 %multiply_add_fusion.index_ref = s32[2,256]{1,0:T(2,128)S(1)} fusion(s32[2,256]{1,0:T(2,128)} %place_ref.1, s32[2,256]{1,0:T(2,128)} %seg_ref.1), kind=kLoop, calls=%fused_computation.2 | loop fusion | flops 1024 | bytes 6144 | tf_op jit(solution)/shard_map/add | solution.py:383
  0.8 0.1 pad_add_fusion.sp_ref.refs_0_
  0.9 3.2 %pick.1 = bf16[40,512]{1,0:T(8,128)(2,1)S(1)} custom-call(s32[3]{0:T(128)S(1)} %pad_add_fusion.sp_ref.refs_0_, s32[2,256]{1,0:T(2,128)S(1)} %multiply_add_fusion.index_ref, bf16[40,65536]{1,0:T(8,128)(2,1)} %refs_5_.2), custom_call_target="tpu_custom_call" | custom-call | bytes 5242880 | tf_op jit(solution)/shard_map/pick/pallas_call | solution.py:97
  4.1 1.5 %collective-permute-start.6 = (bf16[40,65536]{1,0:T(8,128)(2,1)}, bf16[40,65536]{1,0:T(8,128)(2,1)S(1)}, u32[]{:S(2)}, u32[]{:S(2)}) collective-permute-start(bf16[40,65536]{1,0:T(8,128)(2,1)} %refs_5_.2), channel_id=1, source_target_pairs={{0,64},{64,0},{1,65},{65,1},{2,66},{66,2},{3,67},{67,3},{4,68},{68... | collective-permute-start | bytes 15728648 | tf_op jit(solution)/shard_map/ppermute | solution.py:375
  5.5 4.0 %collective-permute-start.2 = (bf16[40,512]{1,0:T(8,128)(2,1)S(1)}, bf16[40,512]{1,0:T(8,128)(2,1)S(1)}, u32[]{:S(2)}, u32[]{:S(2)}) collective-permute-start(bf16[40,512]{1,0:T(8,128)(2,1)S(1)} %pick.1), channel_id=1, source_target_pairs={{0,3},{1,0},{2,1},{3,2},{4,7},{5,4},{6,5},{7,6},{8,11},{9,8},{10,9... | collective-permute-start | bytes 122888 | tf_op jit(solution)/shard_map/ppermute | solution.py:363
  9.5 0.0 collective-permute-start.1
  9.5 0.6 collective-permute-start
  10.1 1.5 %places.1 = (bf16[2,256,256]{2,1,0:T(8,128)(2,1)S(1)}, f32[2,3,256,128]{3,2,1,0:T(8,128)S(1)}, f32[256,256]{1,0:T(8,128)S(1)}, s32[1]{0:T(128)}) custom-call(s32[3]{0:T(128)S(1)} %pad_add_fusion.sp_ref.refs_0_, s32[2,256]{1,0:T(2,128)S(1)} %copy-done, s32[2,256]{1,0:T(2,128)S(1)} %copy-done.1, f32[2,256]{1,0:T(2,128)S(1)} %copy-done.4, s32[2,256]{1,0:T(2,128)S(1)} %copy-done.5), custom_call_target="tpu_custom_call" | custom-call | flops 1000000 | bytes 2000000 | tf_op jit(solution)/shard_map/places/pallas_call | solution.py:152
  11.6 2.3 %collective-permute-done.1 = bf16[40,512]{1,0:T(8,128)(2,1)S(1)} collective-permute-done((bf16[40,512]{1,0:T(8,128)(2,1)S(1)}, bf16[40,512]{1,0:T(8,128)(2,1)S(1)}, u32[]{:S(2)}, u32[]{:S(2)}) %collective-permute-start.1) | collective-permute-done | bytes 40992 | tf_op jit(solution)/shard_map/ppermute | solution.py:363
  14.0 0.4 collective-permute-done
  14.4 4.7 %collective-permute-start.4 = (bf16[40,512]{1,0:T(8,128)(2,1)S(1)}, bf16[40,512]{1,0:T(8,128)(2,1)S(1)}, u32[]{:S(2)}, u32[]{:S(2)}) collective-permute-start(bf16[40,512]{1,0:T(8,128)(2,1)S(1)} %add_add_fusion.1), channel_id=1, source_target_pairs={{0,60},{1,61},{2,62},{3,63},{4,0},{5,1},{6,2},{7,3},{8,4},{9,5},{1... | collective-permute-start | bytes 122888 | tf_op jit(solution)/shard_map/ppermute | solution.py:363
  19.1 1.1 %collective-permute-done.4 = bf16[40,512]{1,0:T(8,128)(2,1)S(1)} collective-permute-done((bf16[40,512]{1,0:T(8,128)(2,1)S(1)}, bf16[40,512]{1,0:T(8,128)(2,1)S(1)}, u32[]{:S(2)}, u32[]{:S(2)}) %collective-permute-start.4) | collective-permute-done | bytes 40992 | tf_op jit(solution)/shard_map/ppermute | solution.py:363
  20.2 5.1 %collective-permute-done.3 = bf16[40,512]{1,0:T(8,128)(2,1)S(1)} collective-permute-done((bf16[40,512]{1,0:T(8,128)(2,1)S(1)}, bf16[40,512]{1,0:T(8,128)(2,1)S(1)}, u32[]{:S(2)}, u32[]{:S(2)}) %collective-permute-start.3) | collective-permute-done | bytes 40992 | tf_op jit(solution)/shard_map/ppermute | solution.py:363
  25.2 3.1 %collective-permute-start.5 = (bf16[40,512]{1,0:T(8,128)(2,1)S(1)}, bf16[40,512]{1,0:T(8,128)(2,1)S(1)}, u32[]{:S(2)}, u32[]{:S(2)}) collective-permute-start(bf16[40,512]{1,0:T(8,128)(2,1)S(1)} %add_add_fusion.mine_ref), channel_id=1, source_target_pairs={{0,64},{64,0},{1,65},{65,1},{2,66},{66,2},{3,67},{67,3},{4,68},{68... | collective-permute-start | bytes 122888 | tf_op jit(solution)/shard_map/ppermute | solution.py:375
  28.4 0.9 %collective-permute-done.5.other_ref = bf16[40,512]{1,0:T(8,128)(2,1)S(1)} collective-permute-done((bf16[40,512]{1,0:T(8,128)(2,1)S(1)}, bf16[40,512]{1,0:T(8,128)(2,1)S(1)}, u32[]{:S(2)}, u32[]{:S(2)}) %collective-permute-start.5) | collective-permute-done | bytes 40992 | tf_op jit(solution)/shard_map/ppermute | solution.py:375
  29.2 0.8 %stats.1 = (bf16[2,256,96]{2,1,0:T(8,128)(2,1)S(1)}, bf16[2,80,256]{2,1,0:T(8,128)(2,1)S(1)}) custom-call(bf16[40,512]{1,0:T(8,128)(2,1)S(1)} %add_add_fusion.mine_ref, bf16[40,512]{1,0:T(8,128)(2,1)S(1)} %collective-permute-done.5.other_ref, f32[2,256]{1,0:T(2,128)S(1)} %copy-done.2, f32[2,256]{1,0:T(2,128)S(1)} %copy-done.3, ...), custom_call_target="tpu_custom_call" | custom-call | tf_op jit(solution)/shard_map/stats/pallas_call | solution.py:214
  30.0 10.6 %update0.1 = (bf16[40,65536]{1,0:T(8,128)(2,1)}, bf16[40,14336]{1,0:T(8,128)(2,1)S(1)}) custom-call(s32[3]{0:T(128)S(1)} %pad_add_fusion.sp_ref.refs_0_, s32[1]{0:T(128)} %get-tuple-element.29.refs_1_, bf16[2,256,96]{2,1,0:T(8,128)(2,1)S(1)} %get-tuple-element.33.refs_2_, bf16[2,80,256]{2,1,0:T(8,128)(2,1)S(1)} %get-tuple-element.34.refs_3_, ...), custom_call_target="tpu_custom_call" | custom-call | flops 4200000000 | bytes 4587520 | tf_op jit(solution)/shard_map/update0/pallas_call | solution.py:305
  40.6 0.4 collective-permute-start.8
  41.0 9.5 %update7.1 = (bf16[40,65536]{1,0:T(8,128)(2,1)}, bf16[40,12288]{1,0:T(8,128)(2,1)S(1)}) custom-call(s32[3]{0:T(128)S(1)} %pad_add_fusion.sp_ref.refs_0_, s32[1]{0:T(128)} %get-tuple-element.29.refs_1_, bf16[2,256,96]{2,1,0:T(8,128)(2,1)S(1)} %get-tuple-element.33.refs_2_, ...), custom_call_target="tpu_custom_call", output_to_operand_aliasing={{0}: (7, {})} | custom-call | flops 3600000000 | bytes 3932160 | tf_op jit(solution)/shard_map/update7/pallas_call | solution.py:305
  50.5 0.2 collective-permute-start.9
  50.7 6.1 %update13.1 = (bf16[40,65536]{1,0:T(8,128)(2,1)}, bf16[40,6144]{1,0:T(8,128)(2,1)S(1)}) custom-call(s32[3]{0:T(128)S(1)} %pad_add_fusion.sp_ref.refs_0_, s32[1]{0:T(128)} %get-tuple-element.29.refs_1_, bf16[2,256,96]{2,1,0:T(8,128)(2,1)S(1)} %get-tuple-element.33.refs_2_, ...), custom_call_target="tpu_custom_call", output_to_operand_aliasing={{0}: (7, {})} | custom-call | flops 1800000000 | bytes 1966080 | tf_op jit(solution)/shard_map/update13/pallas_call | solution.py:305
  56.7 0.4 collective-permute-start.7
  57.1 1.9 %fill0.1.refs_1_ = bf16[40,65536]{1,0:T(8,128)(2,1)} custom-call(s32[3]{0:T(128)S(1)} %pad_add_fusion.sp_ref.refs_0_, bf16[40,14336]{1,0:T(8,128)(2,1)S(1)} %collective-permute-done.8.refs_0_, bf16[40,12288]{1,0:T(8,128)(2,1)S(1)} %collective-permute-done.9.refs_1_, bf16[40,65536]{1,0:T(8,128)(2,1)} %get-tuple-element.42.refs_2_), custom_call_target="tpu_custom_call", output_to_operand_aliasing={{}: (3, {})} | custom-call | tf_op jit(solution)/shard_map/fill0/pallas_call | solution.py:345
  59.0 1.3 %fill13.1 = bf16[40,65536]{1,0:T(8,128)(2,1)} custom-call(s32[3]{0:T(128)S(1)} %pad_add_fusion.sp_ref.refs_0_, bf16[40,6144]{1,0:T(8,128)(2,1)S(1)} %collective-permute-done.7.refs_0_, bf16[40,65536]{1,0:T(8,128)(2,1)} %fill0.1.refs_1_), custom_call_target="tpu_custom_call", output_to_operand_aliasing={{}: (2, {})} | custom-call | tf_op jit(solution)/shard_map/fill13/pallas_call | solution.py:345
  (20 shorter events, 0.1 us)
Async XLA Ops:
  0.0 10.1 %copy-start.1 = (s32[2,256]{1,0:T(2,128)S(1)}, s32[2,256]{1,0:T(2,128)}, u32[]{:S(2)}) copy-start(s32[2,256]{1,0:T(2,128)} %place_ref.1) | copy-start | bytes 6148
  0.0 10.1 %copy-start = (s32[2,256]{1,0:T(2,128)S(1)}, s32[2,256]{1,0:T(2,128)}, u32[]{:S(2)}) copy-start(s32[2,256]{1,0:T(2,128)} %seg_ref.1) | copy-start | bytes 6148
  0.0 10.1 %copy-start.5 = (s32[2,256]{1,0:T(2,128)S(1)}, s32[2,256]{1,0:T(2,128)}, u32[]{:S(2)}) copy-start(s32[2,256]{1,0:T(2,128)} %ext_ref.1) | copy-start | bytes 6148
  0.0 10.1 %copy-start.4 = (f32[2,256]{1,0:T(2,128)S(1)}, f32[2,256]{1,0:T(2,128)}, u32[]{:S(2)}) copy-start(f32[2,256]{1,0:T(2,128)} %damp_ref.1) | copy-start | bytes 6148
  0.0 29.2 %copy-start.3 = (f32[2,256]{1,0:T(2,128)S(1)}, f32[2,256]{1,0:T(2,128)}, u32[]{:S(2)}) copy-start(f32[2,256]{1,0:T(2,128)} %var_ref.1) | copy-start | bytes 6148
  0.0 29.2 %copy-start.2 = (f32[2,256]{1,0:T(2,128)S(1)}, f32[2,256]{1,0:T(2,128)}, u32[]{:S(2)}) copy-start(f32[2,256]{1,0:T(2,128)} %val_ref.1) | copy-start | bytes 6148
  4.1 25.9 %collective-permute-start.6 = (bf16[40,65536]{1,0:T(8,128)(2,1)}, bf16[40,65536]{1,0:T(8,128)(2,1)S(1)}, u32[]{:S(2)}, u32[]{:S(2)}) collective-permute-start(bf16[40,65536]{1,0:T(8,128)(2,1)} %refs_5_.2), channel_id=1, source_target_pairs={{0,64},{64,0},{1,65},{65,1},{2,66},{66,2},{3,67},{67,3},{4,68},{68... | collective-permute-start | bytes 15728648 | tf_op jit(solution)/shard_map/ppermute | solution.py:375
  5.5 6.1 %collective-permute-start.2 = (bf16[40,512]{1,0:T(8,128)(2,1)S(1)}, bf16[40,512]{1,0:T(8,128)(2,1)S(1)}, u32[]{:S(2)}, u32[]{:S(2)}) collective-permute-start(bf16[40,512]{1,0:T(8,128)(2,1)S(1)} %pick.1), channel_id=1, source_target_pairs={{0,3},{1,0},{2,1},{3,2},{4,7},{5,4},{6,5},{7,6},{8,11},{9,8},{10,9... | collective-permute-start | bytes 122888 | tf_op jit(solution)/shard_map/ppermute | solution.py:363
  9.5 4.5 %collective-permute-start.1 = (bf16[40,512]{1,0:T(8,128)(2,1)S(1)}, bf16[40,512]{1,0:T(8,128)(2,1)S(1)}, u32[]{:S(2)}, u32[]{:S(2)}) collective-permute-start(bf16[40,512]{1,0:T(8,128)(2,1)S(1)} %pick.1), channel_id=1, source_target_pairs={{0,2},{1,3},{2,0},{3,1},{4,6},{5,7},{6,4},{7,5},{8,10},{9,11},{10,... | collective-permute-start | bytes 122888 | tf_op jit(solution)/shard_map/ppermute | solution.py:363
  9.5 4.8 %collective-permute-start = (bf16[40,512]{1,0:T(8,128)(2,1)S(1)}, bf16[40,512]{1,0:T(8,128)(2,1)S(1)}, u32[]{:S(2)}, u32[]{:S(2)}) collective-permute-start(bf16[40,512]{1,0:T(8,128)(2,1)S(1)} %pick.1), channel_id=1, source_target_pairs={{0,1},{1,2},{2,3},{3,0},{4,5},{5,6},{6,7},{7,4},{8,9},{9,10},{10,1... | collective-permute-start | bytes 122888 | tf_op jit(solution)/shard_map/ppermute | solution.py:363
  14.4 5.8 %collective-permute-start.4 = (bf16[40,512]{1,0:T(8,128)(2,1)S(1)}, bf16[40,512]{1,0:T(8,128)(2,1)S(1)}, u32[]{:S(2)}, u32[]{:S(2)}) collective-permute-start(bf16[40,512]{1,0:T(8,128)(2,1)S(1)} %add_add_fusion.1), channel_id=1, source_target_pairs={{0,60},{1,61},{2,62},{3,63},{4,0},{5,1},{6,2},{7,3},{8,4},{9,5},{1... | collective-permute-start | bytes 122888 | tf_op jit(solution)/shard_map/ppermute | solution.py:363
  19.1 6.2 %collective-permute-start.3 = (bf16[40,512]{1,0:T(8,128)(2,1)S(1)}, bf16[40,512]{1,0:T(8,128)(2,1)S(1)}, u32[]{:S(2)}, u32[]{:S(2)}) collective-permute-start(bf16[40,512]{1,0:T(8,128)(2,1)S(1)} %add_add_fusion.1), channel_id=1, source_target_pairs={{0,4},{1,5},{2,6},{3,7},{4,8},{5,9},{6,10},{7,11},{8,12},{9,13},{1... | collective-permute-start | bytes 122888 | tf_op jit(solution)/shard_map/ppermute | solution.py:363
  25.2 4.0 %collective-permute-start.5 = (bf16[40,512]{1,0:T(8,128)(2,1)S(1)}, bf16[40,512]{1,0:T(8,128)(2,1)S(1)}, u32[]{:S(2)}, u32[]{:S(2)}) collective-permute-start(bf16[40,512]{1,0:T(8,128)(2,1)S(1)} %add_add_fusion.mine_ref), channel_id=1, source_target_pairs={{0,64},{64,0},{1,65},{65,1},{2,66},{66,2},{3,67},{67,3},{4,68},{68... | collective-permute-start | bytes 122888 | tf_op jit(solution)/shard_map/ppermute | solution.py:375
  40.6 16.4 %collective-permute-start.8 = (bf16[40,14336]{1,0:T(8,128)(2,1)S(1)}, bf16[40,14336]{1,0:T(8,128)(2,1)S(1)}, u32[]{:S(2)}, u32[]{:S(2)}) collective-permute-start(bf16[40,14336]{1,0:T(8,128)(2,1)S(1)} %get-tuple-element.40), channel_id=1, source_target_pairs={{0,64},{64,0},{1,65},{65,1},{2,66},{66,2},{3,67},{67,3},{4,68},{68... | collective-permute-start | bytes 3440648 | tf_op jit(solution)/shard_map/ppermute | solution.py:375
  50.5 6.6 %collective-permute-start.9 = (bf16[40,12288]{1,0:T(8,128)(2,1)S(1)}, bf16[40,12288]{1,0:T(8,128)(2,1)S(1)}, u32[]{:S(2)}, u32[]{:S(2)}) collective-permute-start(bf16[40,12288]{1,0:T(8,128)(2,1)S(1)} %get-tuple-element.41), channel_id=1, source_target_pairs={{0,64},{64,0},{1,65},{65,1},{2,66},{66,2},{3,67},{67,3},{4,68},{68... | collective-permute-start | bytes 2949128 | tf_op jit(solution)/shard_map/ppermute | solution.py:375
  56.7 2.3 %collective-permute-start.7 = (bf16[40,6144]{1,0:T(8,128)(2,1)S(1)}, bf16[40,6144]{1,0:T(8,128)(2,1)S(1)}, u32[]{:S(2)}, u32[]{:S(2)}) collective-permute-start(bf16[40,6144]{1,0:T(8,128)(2,1)S(1)} %get-tuple-element.39), channel_id=1, source_target_pairs={{0,64},{64,0},{1,65},{65,1},{2,66},{66,2},{3,67},{67,3},{4,68},{68... | collective-permute-start | bytes 1474568 | tf_op jit(solution)/shard_map/ppermute | solution.py:375

commit v4 on v3

--- a/solution.py
+++ b/solution.py
@@ -17,8 +17,9 @@
 CHUNK = 2048
 STEPS = SD // CHUNK
 CHUNK_BLOCKS = CHUNK // LB
-PARTS = (7, 6, 3)
+PARTS = (11, 5)
 GROUP = 4
+FLIGHT = 16
 EXTRA = 16
 DEPTH = MEMBERS + EXTRA
 F32 = jnp.float32
@@ -70,15 +71,15 @@
             return n + ((index_ref[b, k] >> 16) == chip).astype(I32)
 
         n = lax.fori_loop(0, K, scan, n, unroll=16)
-    for j in range(4):
+    for j in range(FLIGHT):
         owned[n + j] = B * K
     for copy in copies:
         copy.wait()
     lane = iota((HALF, LB), 1)
 
     def extract(i, _):
-        for j in range(4):
-            k = owned[4 * i + j]
+        for j in range(FLIGHT):
+            k = owned[FLIGHT * i + j]
             b = jnp.minimum(k >> 8, B - 1)
             within = k & (K - 1)
             at = index_ref[b, within] & (CHIP - 1)
@@ -88,7 +89,7 @@
             pltpu.store(acc.at[k >> 7], turned, mask=lane == (k & (LB - 1)))
         return 0
 
-    lax.fori_loop(0, (n + 3) >> 2, extract, 0)
+    lax.fori_loop(0, (n + FLIGHT - 1) // FLIGHT, extract, 0)
     for g in range(B * K // LB):
         o_ref[:, g * LB : (g + 1) * LB] = acc[g].astype(BF16)
 
@@ -104,7 +105,7 @@
             scratch_shapes=[
                 pltpu.VMEM((HALF, CHIP), BF16),
                 pltpu.VMEM((B * K // LB + 1, HALF, LB), F32),
-                pltpu.SMEM((B * K + 8,), I32),
+                pltpu.SMEM((B * K + FLIGHT,), I32),
                 pltpu.SemaphoreType.DMA((4,)),
             ],
         ),
@@ -232,9 +233,15 @@
     )(mine, other, readings, spread, picks, w)
 
 
+def moved(base, a):
+    return pl.ds(pl.multiple_of(base + a.start, 256), 256)
+
+
 def update_kernel(begin, sp_ref, count_ref, cov_ref, chg_ref, cols, mine_ref, other_ref, *rest):
     own_ref, away_ref = rest[-2:]
     step = pl.program_id(0) + begin
+    there = sp_ref[0] * SD + step * CHUNK
+    back = pl.program_id(0) * CHUNK
     first = sp_ref[1].astype(F32)
 
     def weights(b, kc):
@@ -248,7 +255,9 @@
             pairs = range(group * GROUP, (group + 1) * GROUP)
             at = [slice(p * 256, (p + 1) * 256) for p in pairs]
             wide = [
-                jnp.concatenate([mine_ref[:, a].astype(F32), other_ref[:, a].astype(F32)], 0)
+                jnp.concatenate(
+                    [mine_ref[:, a].astype(F32), other_ref[:, moved(there, a)].astype(F32)], 0
+                )
                 for a in at
             ]
             for b in range(B):
@@ -269,7 +278,7 @@
                     wide = [x.astype(BF16).astype(F32) for x in wide]
             for a, x in zip(at, wide):
                 own_ref[:, a] = x[:HALF].astype(BF16)
-                away_ref[:, a] = x[HALF:].astype(BF16)
+                away_ref[:, moved(back, a)] = x[HALF:].astype(BF16)
 
     n = count_ref[0]
 
@@ -294,7 +303,7 @@
     half = lambda i, s, c: (0, s[0] * STEPS + begin + i)
     in_specs = [pl.BlockSpec(memory_space=pltpu.VMEM)] * 3 + [
         pl.BlockSpec((HALF, CHUNK), half),
-        pl.BlockSpec((HALF, CHUNK), half),
+        pl.BlockSpec(memory_space=pltpu.VMEM),
     ]
     operands = [sp, count, cov, chg, cols, x, got]
     aliases = {}
@@ -310,7 +319,7 @@
             in_specs=in_specs,
             out_specs=[
                 pl.BlockSpec((HALF, CHUNK), half),
-                pl.BlockSpec((HALF, CHUNK), lambda i, s, c: (0, i)),
+                pl.BlockSpec(memory_space=pltpu.VMEM),
             ],
         ),
         out_shape=[
@@ -360,7 +369,8 @@
 
 
 def sent(array, target):
-    return lax.ppermute(array, "state", [(i, target(i)) for i in range(CHIPS)])
+    pairs = [(i, target(i)) for i in range(CHIPS)]
+    return lax.ppermute(array, "state", [(i, j) for i, j in pairs if 0 <= j < CHIPS])
 
 
 def along_row(array, by):
@@ -368,7 +378,7 @@
 
 
 def across_rows(array, by):
-    return sent(array, lambda i: (i + 4 * by) % CHIPS)
+    return sent(array, lambda i: i + 4 * by)
 
 
 def swapped(array):

time: 60.6 us -> 57.2 us (0.944)
  the two profiles are of different devices: /device:TPU:1 before, /device:TPU:9 now
where the time goes in v4:
time: 57.2 us; the launch traced here: 56.7 us
  Pallas kernels  32.1 us (56%)
  starting transfers between devices  14.7 us (26%)
  waiting for transfers between devices  8.83 us (15%)
  other arithmetic  0.85 us (1%)
    pallas_call x2, Pallas kernels, update(): pl.pallas_call(lambda *refs: update_kernel(begin, *refs), grid_spec=pltpu...  23.4 us
    ppermute x5, starting transfers between devices, sent(): lax.ppermute(array, 'state', [(i, j) for i, j in pairs if 0 <= j < CHIPS])  10.3 us
    ppermute x5, waiting for transfers between devices, sent(): lax.ppermute(array, 'state', [(i, j) for i, j in pairs if 0 <= j < CHIPS])  7.56 us
    ppermute x4, starting transfers between devices, swapped(): return lax.ppermute(array, 'mem', [(0, 1), (1, 0)])  4.38 us
    pallas_call x1, Pallas kernels, pick(): pl.pallas_call(pick_kernel, grid_spec=pltpu.PrefetchScalarGridSpec(num_sc...  3.29 us
    pallas_call x2, Pallas kernels, fill(): pl.pallas_call(kernel, grid_spec=pltpu.PrefetchScalarGridSpec(num_scalar_...  3.21 us
    pallas_call x1, Pallas kernels, places(): pl.pallas_call(places_kernel, grid_spec=pltpu.PrefetchScalarGridSpec(num_...  1.48 us
    ppermute x4, waiting for transfers between devices, swapped(): return lax.ppermute(array, 'mem', [(0, 1), (1, 0)])  1.27 us
  transfers between devices with their start and end apart: 9, of which 5 were waited for; matrix products, arithmetic and copies ran while one was open for 0% of the time, Pallas kernels for 22%

profile of v4, /device:TPU:9, one launch (start us, length us, event | category | flops | bytes accessed | tf_op | source)
XLA Modules:
  0.0 56.7 jit_solution(7363985620888450979)
XLA Ops:
  0.0 0.7 %multiply_add_fusion.index_ref = s32[2,256]{1,0:T(2,128)S(1)} fusion(s32[2,256]{1,0:T(2,128)} %place_ref.1, s32[2,256]{1,0:T(2,128)} %seg_ref.1), kind=kLoop, calls=%fused_computation.2 | loop fusion | flops 1024 | bytes 6144 | tf_op jit(solution)/shard_map/add | solution.py:393
  0.8 0.1 pad_add_fusion.sp_ref.refs_0_
  0.9 3.3 %pick.1 = bf16[40,512]{1,0:T(8,128)(2,1)S(1)} custom-call(s32[3]{0:T(128)S(1)} %pad_add_fusion.sp_ref.refs_0_, s32[2,256]{1,0:T(2,128)S(1)} %multiply_add_fusion.index_ref, bf16[40,65536]{1,0:T(8,128)(2,1)} %refs_5_.1), custom_call_target="tpu_custom_call" | custom-call | bytes 5242880 | tf_op jit(solution)/shard_map/pick/pallas_call | solution.py:98
  4.2 0.8 %collective-permute-start.6 = (bf16[40,65536]{1,0:T(8,128)(2,1)}, bf16[40,65536]{1,0:T(8,128)(2,1)S(1)}, u32[]{:S(2)}, u32[]{:S(2)}) collective-permute-start(bf16[40,65536]{1,0:T(8,128)(2,1)} %refs_5_.1), channel_id=1, source_target_pairs={{0,64},{64,0},{1,65},{65,1},{2,66},{66,2},{3,67},{67,3},{4,68},{68... | collective-permute-start | bytes 15728648 | tf_op jit(solution)/shard_map/ppermute | solution.py:385
  4.9 3.8 %collective-permute-start.2 = (bf16[40,512]{1,0:T(8,128)(2,1)S(1)}, bf16[40,512]{1,0:T(8,128)(2,1)S(1)}, u32[]{:S(2)}, u32[]{:S(2)}) collective-permute-start(bf16[40,512]{1,0:T(8,128)(2,1)S(1)} %pick.1), channel_id=1, source_target_pairs={{0,3},{1,0},{2,1},{3,2},{4,7},{5,4},{6,5},{7,6},{8,11},{9,8},{10,9... | collective-permute-start | bytes 122888 | tf_op jit(solution)/shard_map/ppermute | solution.py:373
  8.7 0.0 collective-permute-start.1
  8.7 0.7 %collective-permute-start = (bf16[40,512]{1,0:T(8,128)(2,1)S(1)}, bf16[40,512]{1,0:T(8,128)(2,1)S(1)}, u32[]{:S(2)}, u32[]{:S(2)}) collective-permute-start(bf16[40,512]{1,0:T(8,128)(2,1)S(1)} %pick.1), channel_id=1, source_target_pairs={{0,1},{1,2},{2,3},{3,0},{4,5},{5,6},{6,7},{7,4},{8,9},{9,10},{10,1... | collective-permute-start | bytes 122888 | tf_op jit(solution)/shard_map/ppermute | solution.py:373
  9.4 1.5 %places.1 = (bf16[2,256,256]{2,1,0:T(8,128)(2,1)S(1)}, f32[2,3,256,128]{3,2,1,0:T(8,128)S(1)}, f32[256,256]{1,0:T(8,128)S(1)}, s32[1]{0:T(128)}) custom-call(s32[3]{0:T(128)S(1)} %pad_add_fusion.sp_ref.refs_0_, s32[2,256]{1,0:T(2,128)S(1)} %copy-done, s32[2,256]{1,0:T(2,128)S(1)} %copy-done.1, f32[2,256]{1,0:T(2,128)S(1)} %copy-done.4, s32[2,256]{1,0:T(2,128)S(1)} %copy-done.5), custom_call_target="tpu_custom_call" | custom-call | flops 1000000 | bytes 2000000 | tf_op jit(solution)/shard_map/places/pallas_call | solution.py:153
  10.9 0.0 collective-permute-done.2
  10.9 2.2 %collective-permute-done.1 = bf16[40,512]{1,0:T(8,128)(2,1)S(1)} collective-permute-done((bf16[40,512]{1,0:T(8,128)(2,1)S(1)}, bf16[40,512]{1,0:T(8,128)(2,1)S(1)}, u32[]{:S(2)}, u32[]{:S(2)}) %collective-permute-start.1) | collective-permute-done | bytes 40992 | tf_op jit(solution)/shard_map/ppermute | solution.py:373
  13.1 0.4 collective-permute-done
  13.5 4.0 %collective-permute-start.4 = (bf16[40,512]{1,0:T(8,128)(2,1)S(1)}, bf16[40,512]{1,0:T(8,128)(2,1)S(1)}, u32[]{:S(2)}, u32[]{:S(2)}) collective-permute-start(bf16[40,512]{1,0:T(8,128)(2,1)S(1)} %add_add_fusion.1), channel_id=1, source_target_pairs={{4,0},{5,1},{6,2},{7,3},{8,4},{9,5},{10,6},{11,7},{12,8},{13,9},{1... | collective-permute-start | bytes 122888 | tf_op jit(solution)/shard_map/ppermute | solution.py:373
  17.5 1.9 %collective-permute-start.3 = (bf16[40,512]{1,0:T(8,128)(2,1)S(1)}, bf16[40,512]{1,0:T(8,128)(2,1)S(1)}, u32[]{:S(2)}, u32[]{:S(2)}) collective-permute-start(bf16[40,512]{1,0:T(8,128)(2,1)S(1)} %add_add_fusion.1), channel_id=1, source_target_pairs={{0,4},{1,5},{2,6},{3,7},{4,8},{5,9},{6,10},{7,11},{8,12},{9,13},{1... | collective-permute-start | bytes 122888 | tf_op jit(solution)/shard_map/ppermute | solution.py:373
  19.4 4.9 %collective-permute-done.3 = bf16[40,512]{1,0:T(8,128)(2,1)S(1)} collective-permute-done((bf16[40,512]{1,0:T(8,128)(2,1)S(1)}, bf16[40,512]{1,0:T(8,128)(2,1)S(1)}, u32[]{:S(2)}, u32[]{:S(2)}) %collective-permute-start.3) | collective-permute-done | bytes 40992 | tf_op jit(solution)/shard_map/ppermute | solution.py:373
  24.4 3.1 %collective-permute-start.5 = (bf16[40,512]{1,0:T(8,128)(2,1)S(1)}, bf16[40,512]{1,0:T(8,128)(2,1)S(1)}, u32[]{:S(2)}, u32[]{:S(2)}) collective-permute-start(bf16[40,512]{1,0:T(8,128)(2,1)S(1)} %add_add_fusion.mine_ref), channel_id=1, source_target_pairs={{0,64},{64,0},{1,65},{65,1},{2,66},{66,2},{3,67},{67,3},{4,68},{68... | collective-permute-start | bytes 122888 | tf_op jit(solution)/shard_map/ppermute | solution.py:385
  27.5 0.9 %collective-permute-done.5.other_ref = bf16[40,512]{1,0:T(8,128)(2,1)S(1)} collective-permute-done((bf16[40,512]{1,0:T(8,128)(2,1)S(1)}, bf16[40,512]{1,0:T(8,128)(2,1)S(1)}, u32[]{:S(2)}, u32[]{:S(2)}) %collective-permute-start.5) | collective-permute-done | bytes 40992 | tf_op jit(solution)/shard_map/ppermute | solution.py:385
  28.4 0.8 %stats.1 = (bf16[2,256,96]{2,1,0:T(8,128)(2,1)S(1)}, bf16[2,80,256]{2,1,0:T(8,128)(2,1)S(1)}) custom-call(bf16[40,512]{1,0:T(8,128)(2,1)S(1)} %add_add_fusion.mine_ref, bf16[40,512]{1,0:T(8,128)(2,1)S(1)} %collective-permute-done.5.other_ref, f32[2,256]{1,0:T(2,128)S(1)} %copy-done.2, f32[2,256]{1,0:T(2,128)S(1)} %copy-done.3, ...), custom_call_target="tpu_custom_call" | custom-call | tf_op jit(solution)/shard_map/stats/pallas_call | solution.py:215
  29.1 15.0 %update0.1 = (bf16[40,65536]{1,0:T(8,128)(2,1)}, bf16[40,22528]{1,0:T(8,128)(2,1)S(1)}) custom-call(s32[3]{0:T(128)S(1)} %pad_add_fusion.sp_ref.refs_0_, s32[1]{0:T(128)} %get-tuple-element.27.refs_1_, bf16[2,256,96]{2,1,0:T(8,128)(2,1)S(1)} %get-tuple-element.31.refs_2_, bf16[2,80,256]{2,1,0:T(8,128)(2,1)S(1)} %get-tuple-element.32.refs_3_, ...), custom_call_target="tpu_custom_call" | custom-call | flops 6600000000 | bytes 7208960 | tf_op jit(solution)/shard_map/update0/pallas_call | solution.py:314
  44.2 0.4 collective-permute-start.8
  44.5 8.4 %update11.1 = (bf16[40,65536]{1,0:T(8,128)(2,1)}, bf16[40,10240]{1,0:T(8,128)(2,1)S(1)}) custom-call(s32[3]{0:T(128)S(1)} %pad_add_fusion.sp_ref.refs_0_, s32[1]{0:T(128)} %get-tuple-element.27.refs_1_, bf16[2,256,96]{2,1,0:T(8,128)(2,1)S(1)} %get-tuple-element.31.refs_2_, ...), custom_call_target="tpu_custom_call", output_to_operand_aliasing={{0}: (7, {})} | custom-call | flops 3000000000 | bytes 3276800 | tf_op jit(solution)/shard_map/update11/pallas_call | solution.py:314
  52.9 0.2 collective-permute-start.7
  53.0 1.8 %fill0.1.refs_1_ = bf16[40,65536]{1,0:T(8,128)(2,1)} custom-call(s32[3]{0:T(128)S(1)} %pad_add_fusion.sp_ref.refs_0_, bf16[40,22528]{1,0:T(8,128)(2,1)S(1)} %collective-permute-done.8.refs_0_, bf16[40,65536]{1,0:T(8,128)(2,1)} %get-tuple-element.38.refs_1_), custom_call_target="tpu_custom_call", output_to_operand_aliasing={{}: (2, {})} | custom-call | tf_op jit(solution)/shard_map/fill0/pallas_call | solution.py:354
  54.8 0.4 collective-permute-done.7.refs_0_
  55.2 1.4 %fill11.1 = bf16[40,65536]{1,0:T(8,128)(2,1)} custom-call(s32[3]{0:T(128)S(1)} %pad_add_fusion.sp_ref.refs_0_, bf16[40,10240]{1,0:T(8,128)(2,1)S(1)} %collective-permute-done.7.refs_0_, bf16[40,65536]{1,0:T(8,128)(2,1)} %fill0.1.refs_1_), custom_call_target="tpu_custom_call", output_to_operand_aliasing={{}: (2, {})} | custom-call | tf_op jit(solution)/shard_map/fill11/pallas_call | solution.py:354
  (17 shorter events, 0.1 us)
Async XLA Ops:
  0.0 9.4 %copy-start.1 = (s32[2,256]{1,0:T(2,128)S(1)}, s32[2,256]{1,0:T(2,128)}, u32[]{:S(2)}) copy-start(s32[2,256]{1,0:T(2,128)} %place_ref.1) | copy-start | bytes 6148
  0.0 9.4 %copy-start = (s32[2,256]{1,0:T(2,128)S(1)}, s32[2,256]{1,0:T(2,128)}, u32[]{:S(2)}) copy-start(s32[2,256]{1,0:T(2,128)} %seg_ref.1) | copy-start | bytes 6148
  0.0 9.4 %copy-start.5 = (s32[2,256]{1,0:T(2,128)S(1)}, s32[2,256]{1,0:T(2,128)}, u32[]{:S(2)}) copy-start(s32[2,256]{1,0:T(2,128)} %ext_ref.1) | copy-start | bytes 6148
  0.0 9.4 %copy-start.4 = (f32[2,256]{1,0:T(2,128)S(1)}, f32[2,256]{1,0:T(2,128)}, u32[]{:S(2)}) copy-start(f32[2,256]{1,0:T(2,128)} %damp_ref.1) | copy-start | bytes 6148
  0.0 28.3 %copy-start.3 = (f32[2,256]{1,0:T(2,128)S(1)}, f32[2,256]{1,0:T(2,128)}, u32[]{:S(2)}) copy-start(f32[2,256]{1,0:T(2,128)} %var_ref.1) | copy-start | bytes 6148
  0.0 28.3 %copy-start.2 = (f32[2,256]{1,0:T(2,128)S(1)}, f32[2,256]{1,0:T(2,128)}, u32[]{:S(2)}) copy-start(f32[2,256]{1,0:T(2,128)} %val_ref.1) | copy-start | bytes 6148
  4.2 25.0 %collective-permute-start.6 = (bf16[40,65536]{1,0:T(8,128)(2,1)}, bf16[40,65536]{1,0:T(8,128)(2,1)S(1)}, u32[]{:S(2)}, u32[]{:S(2)}) collective-permute-start(bf16[40,65536]{1,0:T(8,128)(2,1)} %refs_5_.1), channel_id=1, source_target_pairs={{0,64},{64,0},{1,65},{65,1},{2,66},{66,2},{3,67},{67,3},{4,68},{68... | collective-permute-start | bytes 15728648 | tf_op jit(solution)/shard_map/ppermute | solution.py:385
  4.9 6.0 %collective-permute-start.2 = (bf16[40,512]{1,0:T(8,128)(2,1)S(1)}, bf16[40,512]{1,0:T(8,128)(2,1)S(1)}, u32[]{:S(2)}, u32[]{:S(2)}) collective-permute-start(bf16[40,512]{1,0:T(8,128)(2,1)S(1)} %pick.1), channel_id=1, source_target_pairs={{0,3},{1,0},{2,1},{3,2},{4,7},{5,4},{6,5},{7,6},{8,11},{9,8},{10,9... | collective-permute-start | bytes 122888 | tf_op jit(solution)/shard_map/ppermute | solution.py:373
  8.7 4.5 %collective-permute-start.1 = (bf16[40,512]{1,0:T(8,128)(2,1)S(1)}, bf16[40,512]{1,0:T(8,128)(2,1)S(1)}, u32[]{:S(2)}, u32[]{:S(2)}) collective-permute-start(bf16[40,512]{1,0:T(8,128)(2,1)S(1)} %pick.1), channel_id=1, source_target_pairs={{0,2},{1,3},{2,0},{3,1},{4,6},{5,7},{6,4},{7,5},{8,10},{9,11},{10,... | collective-permute-start | bytes 122888 | tf_op jit(solution)/shard_map/ppermute | solution.py:373
  8.7 4.8 %collective-permute-start = (bf16[40,512]{1,0:T(8,128)(2,1)S(1)}, bf16[40,512]{1,0:T(8,128)(2,1)S(1)}, u32[]{:S(2)}, u32[]{:S(2)}) collective-permute-start(bf16[40,512]{1,0:T(8,128)(2,1)S(1)} %pick.1), channel_id=1, source_target_pairs={{0,1},{1,2},{2,3},{3,0},{4,5},{5,6},{6,7},{7,4},{8,9},{9,10},{10,1... | collective-permute-start | bytes 122888 | tf_op jit(solution)/shard_map/ppermute | solution.py:373
  13.5 5.9 %collective-permute-start.4 = (bf16[40,512]{1,0:T(8,128)(2,1)S(1)}, bf16[40,512]{1,0:T(8,128)(2,1)S(1)}, u32[]{:S(2)}, u32[]{:S(2)}) collective-permute-start(bf16[40,512]{1,0:T(8,128)(2,1)S(1)} %add_add_fusion.1), channel_id=1, source_target_pairs={{4,0},{5,1},{6,2},{7,3},{8,4},{9,5},{10,6},{11,7},{12,8},{13,9},{1... | collective-permute-start | bytes 122888 | tf_op jit(solution)/shard_map/ppermute | solution.py:373
  17.5 6.9 %collective-permute-start.3 = (bf16[40,512]{1,0:T(8,128)(2,1)S(1)}, bf16[40,512]{1,0:T(8,128)(2,1)S(1)}, u32[]{:S(2)}, u32[]{:S(2)}) collective-permute-start(bf16[40,512]{1,0:T(8,128)(2,1)S(1)} %add_add_fusion.1), channel_id=1, source_target_pairs={{0,4},{1,5},{2,6},{3,7},{4,8},{5,9},{6,10},{7,11},{8,12},{9,13},{1... | collective-permute-start | bytes 122888 | tf_op jit(solution)/shard_map/ppermute | solution.py:373
  24.4 4.0 %collective-permute-start.5 = (bf16[40,512]{1,0:T(8,128)(2,1)S(1)}, bf16[40,512]{1,0:T(8,128)(2,1)S(1)}, u32[]{:S(2)}, u32[]{:S(2)}) collective-permute-start(bf16[40,512]{1,0:T(8,128)(2,1)S(1)} %add_add_fusion.mine_ref), channel_id=1, source_target_pairs={{0,64},{64,0},{1,65},{65,1},{2,66},{66,2},{3,67},{67,3},{4,68},{68... | collective-permute-start | bytes 122888 | tf_op jit(solution)/shard_map/ppermute | solution.py:385
  44.2 8.9 %collective-permute-start.8 = (bf16[40,22528]{1,0:T(8,128)(2,1)S(1)}, bf16[40,22528]{1,0:T(8,128)(2,1)S(1)}, u32[]{:S(2)}, u32[]{:S(2)}) collective-permute-start(bf16[40,22528]{1,0:T(8,128)(2,1)S(1)} %get-tuple-element.37), channel_id=1, source_target_pairs={{0,64},{64,0},{1,65},{65,1},{2,66},{66,2},{3,67},{67,3},{4,68},{68... | collective-permute-start | bytes 5406728 | tf_op jit(solution)/shard_map/ppermute | solution.py:385
  52.9 2.3 %collective-permute-start.7 = (bf16[40,10240]{1,0:T(8,128)(2,1)S(1)}, bf16[40,10240]{1,0:T(8,128)(2,1)S(1)}, u32[]{:S(2)}, u32[]{:S(2)}) collective-permute-start(bf16[40,10240]{1,0:T(8,128)(2,1)S(1)} %get-tuple-element.36), channel_id=1, source_target_pairs={{0,64},{64,0},{1,65},{65,1},{2,66},{66,2},{3,67},{67,3},{4,68},{68... | collective-permute-start | bytes 2457608 | tf_op jit(solution)/shard_map/ppermute | solution.py:385

commit v5 on v4

--- a/solution.py
+++ b/solution.py
@@ -14,11 +14,12 @@
 CHIP = 2 * SD
 CHIPS = 64
 SEG_BLOCKS = SD // LB
-CHUNK = 2048
+CHUNK = 4096
 STEPS = SD // CHUNK
 CHUNK_BLOCKS = CHUNK // LB
-PARTS = (11, 5)
-GROUP = 4
+PARTS = (6, 2)
+IN_FLIGHT = {32: 16, 64: 16, 128: 8, K: 4}
+PIECES = 4
 FLIGHT = 16
 EXTRA = 16
 DEPTH = MEMBERS + EXTRA
@@ -251,8 +252,8 @@
 
     def advance(kc):
         w = [weights(b, kc) for b in range(B)]
-        for group in range(CHUNK // (256 * GROUP)):
-            pairs = range(group * GROUP, (group + 1) * GROUP)
+        for start in range(0, CHUNK // 256, IN_FLIGHT[kc]):
+            pairs = range(start, start + IN_FLIGHT[kc])
             at = [slice(p * 256, (p + 1) * 256) for p in pairs]
             wide = [
                 jnp.concatenate(
@@ -343,9 +344,12 @@
         base = (1 - sp_ref[0]) * SD
         copies = []
         for j, (begin, part) in enumerate(zip(begins, refs[: len(parts)])):
-            start = pl.multiple_of(base + begin * CHUNK, CHUNK)
-            to = out_ref.at[:, pl.ds(start, part.shape[1])]
-            copies.append(pltpu.make_async_copy(part, to, sems.at[j]))
+            width = part.shape[1] // PIECES
+            for p in range(PIECES):
+                start = pl.multiple_of(base + begin * CHUNK + p * width, 1024)
+                to = out_ref.at[:, pl.ds(start, width)]
+                piece = part.at[:, pl.ds(p * width, width)]
+                copies.append(pltpu.make_async_copy(piece, to, sems.at[j * PIECES + p]))
         for copy in copies:
             copy.start()
         for copy in copies:
@@ -359,7 +363,7 @@
             in_specs=[pl.BlockSpec(memory_space=pltpu.VMEM)] * len(parts)
             + [pl.BlockSpec(memory_space=pl.ANY)],
             out_specs=pl.BlockSpec(memory_space=pl.ANY),
-            scratch_shapes=[pltpu.SemaphoreType.DMA((len(parts),))],
+            scratch_shapes=[pltpu.SemaphoreType.DMA((PIECES * len(parts),))],
         ),
         out_shape=jax.ShapeDtypeStruct((HALF, CHIP), BF16),
         input_output_aliases={1 + len(parts): 0},

time: 57.2 us -> 46.8 us (0.82)
  Pallas kernels: 32.1 us -> 21.9 us
    pallas_call x2, Pallas kernels: 23.4 us -> 13.1 us  [update(): pl.pallas_call(lambda *refs: update_kernel(begin, *refs), grid_spec=pltpu...]
  transfers between devices with their start and end apart: 9 -> 9, of which waited for: 5 -> 5; matrix products, arithmetic and copies ran while one was open for 0% -> 0% of each run, Pallas kernels for 22% -> 19%
where the time goes in v5:
time: 46.8 us; the launch traced here: 46.3 us
  Pallas kernels  21.9 us (47%)
  starting transfers between devices  14.7 us (31%)
  waiting for transfers between devices  8.51 us (18%)
  other arithmetic  0.85 us (2%)
    pallas_call x2, Pallas kernels, update(): pl.pallas_call(lambda *refs: update_kernel(begin, *refs), grid_spec=pltpu...  13.1 us
    ppermute x5, starting transfers between devices, sent(): lax.ppermute(array, 'state', [(i, j) for i, j in pairs if 0 <= j < CHIPS])  10.3 us
    ppermute x5, waiting for transfers between devices, sent(): lax.ppermute(array, 'state', [(i, j) for i, j in pairs if 0 <= j < CHIPS])  7.56 us
    ppermute x4, starting transfers between devices, swapped(): return lax.ppermute(array, 'mem', [(0, 1), (1, 0)])  4.42 us
    pallas_call x1, Pallas kernels, pick(): pl.pallas_call(pick_kernel, grid_spec=pltpu.PrefetchScalarGridSpec(num_sc...  3.29 us
    pallas_call x2, Pallas kernels, fill(): pl.pallas_call(kernel, grid_spec=pltpu.PrefetchScalarGridSpec(num_scalar_...  3.25 us
    pallas_call x1, Pallas kernels, places(): pl.pallas_call(places_kernel, grid_spec=pltpu.PrefetchScalarGridSpec(num_...  1.48 us
    ppermute x4, waiting for transfers between devices, swapped(): return lax.ppermute(array, 'mem', [(0, 1), (1, 0)])  0.95 us
  transfers between devices with their start and end apart: 9, of which 5 were waited for; matrix products, arithmetic and copies ran while one was open for 0% of the time, Pallas kernels for 19%

profile of v5, /device:TPU:9, one launch (start us, length us, event | category | flops | bytes accessed | tf_op | source)
XLA Modules:
  0.0 46.3 jit_solution(16611194455614189615)
XLA Ops:
  0.0 0.7 %multiply_add_fusion.index_ref = s32[2,256]{1,0:T(2,128)S(1)} fusion(s32[2,256]{1,0:T(2,128)} %place_ref.1, s32[2,256]{1,0:T(2,128)} %seg_ref.1), kind=kLoop, calls=%fused_computation.2 | loop fusion | flops 1024 | bytes 6144 | tf_op jit(solution)/shard_map/add | solution.py:397
  0.8 0.1 pad_add_fusion.sp_ref.refs_0_
  0.9 3.3 %pick.1 = bf16[40,512]{1,0:T(8,128)(2,1)S(1)} custom-call(s32[3]{0:T(128)S(1)} %pad_add_fusion.sp_ref.refs_0_, s32[2,256]{1,0:T(2,128)S(1)} %multiply_add_fusion.index_ref, bf16[40,65536]{1,0:T(8,128)(2,1)} %refs_5_.1), custom_call_target="tpu_custom_call" | custom-call | bytes 5242880 | tf_op jit(solution)/shard_map/pick/pallas_call | solution.py:99
  4.2 0.8 %collective-permute-start.6 = (bf16[40,65536]{1,0:T(8,128)(2,1)}, bf16[40,65536]{1,0:T(8,128)(2,1)S(1)}, u32[]{:S(2)}, u32[]{:S(2)}) collective-permute-start(bf16[40,65536]{1,0:T(8,128)(2,1)} %refs_5_.1), channel_id=1, source_target_pairs={{0,64},{64,0},{1,65},{65,1},{2,66},{66,2},{3,67},{67,3},{4,68},{68... | collective-permute-start | bytes 15728648 | tf_op jit(solution)/shard_map/ppermute | solution.py:389
  4.9 3.8 %collective-permute-start.2 = (bf16[40,512]{1,0:T(8,128)(2,1)S(1)}, bf16[40,512]{1,0:T(8,128)(2,1)S(1)}, u32[]{:S(2)}, u32[]{:S(2)}) collective-permute-start(bf16[40,512]{1,0:T(8,128)(2,1)S(1)} %pick.1), channel_id=1, source_target_pairs={{0,3},{1,0},{2,1},{3,2},{4,7},{5,4},{6,5},{7,6},{8,11},{9,8},{10,9... | collective-permute-start | bytes 122888 | tf_op jit(solution)/shard_map/ppermute | solution.py:377
  8.7 0.0 collective-permute-start.1
  8.7 0.7 %collective-permute-start = (bf16[40,512]{1,0:T(8,128)(2,1)S(1)}, bf16[40,512]{1,0:T(8,128)(2,1)S(1)}, u32[]{:S(2)}, u32[]{:S(2)}) collective-permute-start(bf16[40,512]{1,0:T(8,128)(2,1)S(1)} %pick.1), channel_id=1, source_target_pairs={{0,1},{1,2},{2,3},{3,0},{4,5},{5,6},{6,7},{7,4},{8,9},{9,10},{10,1... | collective-permute-start | bytes 122888 | tf_op jit(solution)/shard_map/ppermute | solution.py:377
  9.4 1.5 %places.1 = (bf16[2,256,256]{2,1,0:T(8,128)(2,1)S(1)}, f32[2,3,256,128]{3,2,1,0:T(8,128)S(1)}, f32[256,256]{1,0:T(8,128)S(1)}, s32[1]{0:T(128)}) custom-call(s32[3]{0:T(128)S(1)} %pad_add_fusion.sp_ref.refs_0_, s32[2,256]{1,0:T(2,128)S(1)} %copy-done, s32[2,256]{1,0:T(2,128)S(1)} %copy-done.1, f32[2,256]{1,0:T(2,128)S(1)} %copy-done.4, s32[2,256]{1,0:T(2,128)S(1)} %copy-done.5), custom_call_target="tpu_custom_call" | custom-call | flops 1000000 | bytes 2000000 | tf_op jit(solution)/shard_map/places/pallas_call | solution.py:154
  10.9 0.0 collective-permute-done.2
  10.9 2.2 %collective-permute-done.1 = bf16[40,512]{1,0:T(8,128)(2,1)S(1)} collective-permute-done((bf16[40,512]{1,0:T(8,128)(2,1)S(1)}, bf16[40,512]{1,0:T(8,128)(2,1)S(1)}, u32[]{:S(2)}, u32[]{:S(2)}) %collective-permute-start.1) | collective-permute-done | bytes 40992 | tf_op jit(solution)/shard_map/ppermute | solution.py:377
  13.1 0.4 collective-permute-done
  13.5 3.9 %collective-permute-start.4 = (bf16[40,512]{1,0:T(8,128)(2,1)S(1)}, bf16[40,512]{1,0:T(8,128)(2,1)S(1)}, u32[]{:S(2)}, u32[]{:S(2)}) collective-permute-start(bf16[40,512]{1,0:T(8,128)(2,1)S(1)} %add_add_fusion.1), channel_id=1, source_target_pairs={{4,0},{5,1},{6,2},{7,3},{8,4},{9,5},{10,6},{11,7},{12,8},{13,9},{1... | collective-permute-start | bytes 122888 | tf_op jit(solution)/shard_map/ppermute | solution.py:377
  17.5 1.9 %collective-permute-start.3 = (bf16[40,512]{1,0:T(8,128)(2,1)S(1)}, bf16[40,512]{1,0:T(8,128)(2,1)S(1)}, u32[]{:S(2)}, u32[]{:S(2)}) collective-permute-start(bf16[40,512]{1,0:T(8,128)(2,1)S(1)} %add_add_fusion.1), channel_id=1, source_target_pairs={{0,4},{1,5},{2,6},{3,7},{4,8},{5,9},{6,10},{7,11},{8,12},{9,13},{1... | collective-permute-start | bytes 122888 | tf_op jit(solution)/shard_map/ppermute | solution.py:377
  19.4 4.9 %collective-permute-done.3 = bf16[40,512]{1,0:T(8,128)(2,1)S(1)} collective-permute-done((bf16[40,512]{1,0:T(8,128)(2,1)S(1)}, bf16[40,512]{1,0:T(8,128)(2,1)S(1)}, u32[]{:S(2)}, u32[]{:S(2)}) %collective-permute-start.3) | collective-permute-done | bytes 40992 | tf_op jit(solution)/shard_map/ppermute | solution.py:377
  24.4 3.2 %collective-permute-start.5 = (bf16[40,512]{1,0:T(8,128)(2,1)S(1)}, bf16[40,512]{1,0:T(8,128)(2,1)S(1)}, u32[]{:S(2)}, u32[]{:S(2)}) collective-permute-start(bf16[40,512]{1,0:T(8,128)(2,1)S(1)} %add_add_fusion.mine_ref), channel_id=1, source_target_pairs={{0,64},{64,0},{1,65},{65,1},{2,66},{66,2},{3,67},{67,3},{4,68},{68... | collective-permute-start | bytes 122888 | tf_op jit(solution)/shard_map/ppermute | solution.py:389
  27.5 0.9 %collective-permute-done.5.other_ref = bf16[40,512]{1,0:T(8,128)(2,1)S(1)} collective-permute-done((bf16[40,512]{1,0:T(8,128)(2,1)S(1)}, bf16[40,512]{1,0:T(8,128)(2,1)S(1)}, u32[]{:S(2)}, u32[]{:S(2)}) %collective-permute-start.5) | collective-permute-done | bytes 40992 | tf_op jit(solution)/shard_map/ppermute | solution.py:389
  28.4 0.8 %stats.1 = (bf16[2,256,96]{2,1,0:T(8,128)(2,1)S(1)}, bf16[2,80,256]{2,1,0:T(8,128)(2,1)S(1)}) custom-call(bf16[40,512]{1,0:T(8,128)(2,1)S(1)} %add_add_fusion.mine_ref, bf16[40,512]{1,0:T(8,128)(2,1)S(1)} %collective-permute-done.5.other_ref, f32[2,256]{1,0:T(2,128)S(1)} %copy-done.2, f32[2,256]{1,0:T(2,128)S(1)} %copy-done.3, ...), custom_call_target="tpu_custom_call" | custom-call | tf_op jit(solution)/shard_map/stats/pallas_call | solution.py:216
  29.2 8.5 %update0.1 = (bf16[40,65536]{1,0:T(8,128)(2,1)}, bf16[40,24576]{1,0:T(8,128)(2,1)S(1)}) custom-call(s32[3]{0:T(128)S(1)} %pad_add_fusion.sp_ref.refs_0_, s32[1]{0:T(128)} %get-tuple-element.27.refs_1_, bf16[2,256,96]{2,1,0:T(8,128)(2,1)S(1)} %get-tuple-element.31.refs_2_, bf16[2,80,256]{2,1,0:T(8,128)(2,1)S(1)} %get-tuple-element.32.refs_3_, ...), custom_call_target="tpu_custom_call" | custom-call | flops 3600000000 | bytes 7864320 | tf_op jit(solution)/shard_map/update0/pallas_call | solution.py:315
  37.6 0.3 collective-permute-start.8
  38.0 4.6 %update6.1 = (bf16[40,65536]{1,0:T(8,128)(2,1)}, bf16[40,8192]{1,0:T(8,128)(2,1)S(1)}) custom-call(s32[3]{0:T(128)S(1)} %pad_add_fusion.sp_ref.refs_0_, s32[1]{0:T(128)} %get-tuple-element.27.refs_1_, bf16[2,256,96]{2,1,0:T(8,128)(2,1)S(1)} %get-tuple-element.31.refs_2_, ...), custom_call_target="tpu_custom_call", output_to_operand_aliasing={{0}: (7, {})} | custom-call | flops 1200000000 | bytes 2621440 | tf_op jit(solution)/shard_map/update6/pallas_call | solution.py:315
  42.6 0.2 collective-permute-start.7
  42.8 1.8 %fill0.1.refs_1_ = bf16[40,65536]{1,0:T(8,128)(2,1)} custom-call(s32[3]{0:T(128)S(1)} %pad_add_fusion.sp_ref.refs_0_, bf16[40,24576]{1,0:T(8,128)(2,1)S(1)} %collective-permute-done.8.refs_0_, bf16[40,65536]{1,0:T(8,128)(2,1)} %get-tuple-element.38.refs_1_), custom_call_target="tpu_custom_call", output_to_operand_aliasing={{}: (2, {})} | custom-call | tf_op jit(solution)/shard_map/fill0/pallas_call | solution.py:358
  44.6 0.1 collective-permute-done.7.refs_0_
  44.7 1.4 %fill6.1 = bf16[40,65536]{1,0:T(8,128)(2,1)} custom-call(s32[3]{0:T(128)S(1)} %pad_add_fusion.sp_ref.refs_0_, bf16[40,8192]{1,0:T(8,128)(2,1)S(1)} %collective-permute-done.7.refs_0_, bf16[40,65536]{1,0:T(8,128)(2,1)} %fill0.1.refs_1_), custom_call_target="tpu_custom_call", output_to_operand_aliasing={{}: (2, {})} | custom-call | tf_op jit(solution)/shard_map/fill6/pallas_call | solution.py:358
  (17 shorter events, 0.1 us)
Async XLA Ops:
  0.0 9.4 %copy-start.1 = (s32[2,256]{1,0:T(2,128)S(1)}, s32[2,256]{1,0:T(2,128)}, u32[]{:S(2)}) copy-start(s32[2,256]{1,0:T(2,128)} %place_ref.1) | copy-start | bytes 6148
  0.0 9.4 %copy-start = (s32[2,256]{1,0:T(2,128)S(1)}, s32[2,256]{1,0:T(2,128)}, u32[]{:S(2)}) copy-start(s32[2,256]{1,0:T(2,128)} %seg_ref.1) | copy-start | bytes 6148
  0.0 9.4 %copy-start.5 = (s32[2,256]{1,0:T(2,128)S(1)}, s32[2,256]{1,0:T(2,128)}, u32[]{:S(2)}) copy-start(s32[2,256]{1,0:T(2,128)} %ext_ref.1) | copy-start | bytes 6148
  0.0 9.4 %copy-start.4 = (f32[2,256]{1,0:T(2,128)S(1)}, f32[2,256]{1,0:T(2,128)}, u32[]{:S(2)}) copy-start(f32[2,256]{1,0:T(2,128)} %damp_ref.1) | copy-start | bytes 6148
  0.0 28.4 %copy-start.3 = (f32[2,256]{1,0:T(2,128)S(1)}, f32[2,256]{1,0:T(2,128)}, u32[]{:S(2)}) copy-start(f32[2,256]{1,0:T(2,128)} %var_ref.1) | copy-start | bytes 6148
  0.0 28.3 %copy-start.2 = (f32[2,256]{1,0:T(2,128)S(1)}, f32[2,256]{1,0:T(2,128)}, u32[]{:S(2)}) copy-start(f32[2,256]{1,0:T(2,128)} %val_ref.1) | copy-start | bytes 6148
  4.2 25.0 %collective-permute-start.6 = (bf16[40,65536]{1,0:T(8,128)(2,1)}, bf16[40,65536]{1,0:T(8,128)(2,1)S(1)}, u32[]{:S(2)}, u32[]{:S(2)}) collective-permute-start(bf16[40,65536]{1,0:T(8,128)(2,1)} %refs_5_.1), channel_id=1, source_target_pairs={{0,64},{64,0},{1,65},{65,1},{2,66},{66,2},{3,67},{67,3},{4,68},{68... | collective-permute-start | bytes 15728648 | tf_op jit(solution)/shard_map/ppermute | solution.py:389
  4.9 6.0 %collective-permute-start.2 = (bf16[40,512]{1,0:T(8,128)(2,1)S(1)}, bf16[40,512]{1,0:T(8,128)(2,1)S(1)}, u32[]{:S(2)}, u32[]{:S(2)}) collective-permute-start(bf16[40,512]{1,0:T(8,128)(2,1)S(1)} %pick.1), channel_id=1, source_target_pairs={{0,3},{1,0},{2,1},{3,2},{4,7},{5,4},{6,5},{7,6},{8,11},{9,8},{10,9... | collective-permute-start | bytes 122888 | tf_op jit(solution)/shard_map/ppermute | solution.py:377
  8.7 4.5 %collective-permute-start.1 = (bf16[40,512]{1,0:T(8,128)(2,1)S(1)}, bf16[40,512]{1,0:T(8,128)(2,1)S(1)}, u32[]{:S(2)}, u32[]{:S(2)}) collective-permute-start(bf16[40,512]{1,0:T(8,128)(2,1)S(1)} %pick.1), channel_id=1, source_target_pairs={{0,2},{1,3},{2,0},{3,1},{4,6},{5,7},{6,4},{7,5},{8,10},{9,11},{10,... | collective-permute-start | bytes 122888 | tf_op jit(solution)/shard_map/ppermute | solution.py:377
  8.7 4.8 %collective-permute-start = (bf16[40,512]{1,0:T(8,128)(2,1)S(1)}, bf16[40,512]{1,0:T(8,128)(2,1)S(1)}, u32[]{:S(2)}, u32[]{:S(2)}) collective-permute-start(bf16[40,512]{1,0:T(8,128)(2,1)S(1)} %pick.1), channel_id=1, source_target_pairs={{0,1},{1,2},{2,3},{3,0},{4,5},{5,6},{6,7},{7,4},{8,9},{9,10},{10,1... | collective-permute-start | bytes 122888 | tf_op jit(solution)/shard_map/ppermute | solution.py:377
  13.5 5.9 %collective-permute-start.4 = (bf16[40,512]{1,0:T(8,128)(2,1)S(1)}, bf16[40,512]{1,0:T(8,128)(2,1)S(1)}, u32[]{:S(2)}, u32[]{:S(2)}) collective-permute-start(bf16[40,512]{1,0:T(8,128)(2,1)S(1)} %add_add_fusion.1), channel_id=1, source_target_pairs={{4,0},{5,1},{6,2},{7,3},{8,4},{9,5},{10,6},{11,7},{12,8},{13,9},{1... | collective-permute-start | bytes 122888 | tf_op jit(solution)/shard_map/ppermute | solution.py:377
  17.5 6.9 %collective-permute-start.3 = (bf16[40,512]{1,0:T(8,128)(2,1)S(1)}, bf16[40,512]{1,0:T(8,128)(2,1)S(1)}, u32[]{:S(2)}, u32[]{:S(2)}) collective-permute-start(bf16[40,512]{1,0:T(8,128)(2,1)S(1)} %add_add_fusion.1), channel_id=1, source_target_pairs={{0,4},{1,5},{2,6},{3,7},{4,8},{5,9},{6,10},{7,11},{8,12},{9,13},{1... | collective-permute-start | bytes 122888 | tf_op jit(solution)/shard_map/ppermute | solution.py:377
  24.4 4.0 %collective-permute-start.5 = (bf16[40,512]{1,0:T(8,128)(2,1)S(1)}, bf16[40,512]{1,0:T(8,128)(2,1)S(1)}, u32[]{:S(2)}, u32[]{:S(2)}) collective-permute-start(bf16[40,512]{1,0:T(8,128)(2,1)S(1)} %add_add_fusion.mine_ref), channel_id=1, source_target_pairs={{0,64},{64,0},{1,65},{65,1},{2,66},{66,2},{3,67},{67,3},{4,68},{68... | collective-permute-start | bytes 122888 | tf_op jit(solution)/shard_map/ppermute | solution.py:389
  37.6 5.1 %collective-permute-start.8 = (bf16[40,24576]{1,0:T(8,128)(2,1)S(1)}, bf16[40,24576]{1,0:T(8,128)(2,1)S(1)}, u32[]{:S(2)}, u32[]{:S(2)}) collective-permute-start(bf16[40,24576]{1,0:T(8,128)(2,1)S(1)} %get-tuple-element.37), channel_id=1, source_target_pairs={{0,64},{64,0},{1,65},{65,1},{2,66},{66,2},{3,67},{67,3},{4,68},{68... | collective-permute-start | bytes 5898248 | tf_op jit(solution)/shard_map/ppermute | solution.py:389
  42.6 2.1 %collective-permute-start.7 = (bf16[40,8192]{1,0:T(8,128)(2,1)S(1)}, bf16[40,8192]{1,0:T(8,128)(2,1)S(1)}, u32[]{:S(2)}, u32[]{:S(2)}) collective-permute-start(bf16[40,8192]{1,0:T(8,128)(2,1)S(1)} %get-tuple-element.36), channel_id=1, source_target_pairs={{0,64},{64,0},{1,65},{65,1},{2,66},{66,2},{3,67},{67,3},{4,68},{68... | collective-permute-start | bytes 1966088 | tf_op jit(solution)/shard_map/ppermute | solution.py:389

commit v6 on v5

--- a/solution.py
+++ b/solution.py
@@ -235,7 +235,7 @@
 
 
 def moved(base, a):
-    return pl.ds(pl.multiple_of(base + a.start, 256), 256)
+    return pl.ds(pl.multiple_of(base + a, 256), 256)
 
 
 def update_kernel(begin, sp_ref, count_ref, cov_ref, chg_ref, cols, mine_ref, other_ref, *rest):
@@ -245,41 +245,53 @@
     back = pl.program_id(0) * CHUNK
     first = sp_ref[1].astype(F32)
 
-    def weights(b, kc):
-        block = (first + (step * CHUNK_BLOCKS).astype(F32)) + iota((kc, LB), 1).astype(F32)
+    def weights(b, kc, start):
+        block = (first + (step * CHUNK_BLOCKS + start).astype(F32)) + iota((kc, LB), 1).astype(F32)
         distance = jnp.abs(block - cols[b, 0, :kc])
         return cols[b, 2, :kc] * jnp.maximum(0.0, 1.0 - distance / cols[b, 1, :kc])
 
+    def advance_pairs(kc, start):
+        pairs = range(IN_FLIGHT[kc])
+        at = [pl.multiple_of((start + p) * 256, 256) for p in pairs]
+        w = [weights(b, kc, 2 * start) for b in range(B)]
+        wide = [
+            jnp.concatenate(
+                [
+                    mine_ref[:, pl.ds(a, 256)].astype(F32),
+                    other_ref[:, moved(there, a)].astype(F32),
+                ],
+                0,
+            )
+            for a in at
+        ]
+        for b in range(B):
+            cov = [dot(cov_ref[b, :kc], with_extra(x.astype(BF16))) for x in wide]
+            gain = [
+                jnp.concatenate(
+                    [
+                        c[:, h * LB : (h + 1) * LB]
+                        * jnp.broadcast_to(w[b][:, 2 * p + h : 2 * p + h + 1], (kc, LB))
+                        for h in range(2)
+                    ],
+                    1,
+                ).astype(BF16)
+                for p, c in zip(pairs, cov)
+            ]
+            wide = [x + dot(chg_ref[b, :, :kc], g) for x, g in zip(wide, gain)]
+            if b == 0:
+                wide = [x.astype(BF16).astype(F32) for x in wide]
+        for a, x in zip(at, wide):
+            own_ref[:, pl.ds(a, 256)] = x[:HALF].astype(BF16)
+            away_ref[:, moved(back, a)] = x[HALF:].astype(BF16)
+
     def advance(kc):
-        w = [weights(b, kc) for b in range(B)]
-        for start in range(0, CHUNK // 256, IN_FLIGHT[kc]):
-            pairs = range(start, start + IN_FLIGHT[kc])
-            at = [slice(p * 256, (p + 1) * 256) for p in pairs]
-            wide = [
-                jnp.concatenate(
-                    [mine_ref[:, a].astype(F32), other_ref[:, moved(there, a)].astype(F32)], 0
-                )
-                for a in at
-            ]
-            for b in range(B):
-                cov = [dot(cov_ref[b, :kc], with_extra(x.astype(BF16))) for x in wide]
-                gain = [
-                    jnp.concatenate(
-                        [
-                            c[:, h * LB : (h + 1) * LB]
-                            * jnp.broadcast_to(w[b][:, 2 * p + h : 2 * p + h + 1], (kc, LB))
-                            for h in range(2)
-                        ],
-                        1,
-                    ).astype(BF16)
-                    for p, c in zip(pairs, cov)
-                ]
-                wide = [x + dot(chg_ref[b, :, :kc], g) for x, g in zip(wide, gain)]
-                if b == 0:
-                    wide = [x.astype(BF16).astype(F32) for x in wide]
-            for a, x in zip(at, wide):
-                own_ref[:, a] = x[:HALF].astype(BF16)
-                away_ref[:, moved(back, a)] = x[HALF:].astype(BF16)
+        rounds = CHUNK // 256 // IN_FLIGHT[kc]
+
+        def body(i, _):
+            advance_pairs(kc, i * IN_FLIGHT[kc])
+            return 0
+
+        lax.fori_loop(0, rounds, body, 0)
 
     n = count_ref[0]
 
@@ -338,10 +350,10 @@
     )(*operands)
 
 
-def fill(begins, sp, parts, out):
-    def kernel(sp_ref, *refs):
+def fill(begins, parts, out):
+    def kernel(*refs):
         out_ref, sems = refs[-2:]
-        base = (1 - sp_ref[0]) * SD
+        base = (1 - lax.axis_index("mem")) * SD
         copies = []
         for j, (begin, part) in enumerate(zip(begins, refs[: len(parts)])):
             width = part.shape[1] // PIECES
@@ -357,19 +369,15 @@
 
     return pl.pallas_call(
         kernel,
-        grid_spec=pltpu.PrefetchScalarGridSpec(
-            num_scalar_prefetch=1,
-            grid=(1,),
-            in_specs=[pl.BlockSpec(memory_space=pltpu.VMEM)] * len(parts)
-            + [pl.BlockSpec(memory_space=pl.ANY)],
-            out_specs=pl.BlockSpec(memory_space=pl.ANY),
-            scratch_shapes=[pltpu.SemaphoreType.DMA((PIECES * len(parts),))],
-        ),
+        in_specs=[pl.BlockSpec(memory_space=pltpu.VMEM)] * len(parts)
+        + [pl.BlockSpec(memory_space=pl.ANY)],
+        out_specs=pl.BlockSpec(memory_space=pl.ANY),
+        scratch_shapes=[pltpu.SemaphoreType.DMA((PIECES * len(parts),))],
         out_shape=jax.ShapeDtypeStruct((HALF, CHIP), BF16),
-        input_output_aliases={1 + len(parts): 0},
+        input_output_aliases={len(parts): 0},
         compiler_params=pltpu.CompilerParams(vmem_limit_bytes=VMEM_LIMIT),
         name=f"fill{begins[0]}",
-    )(sp, *parts, out)
+    )(*parts, out)
 
 
 def sent(array, target):
@@ -377,12 +385,16 @@
     return lax.ppermute(array, "state", [(i, j) for i, j in pairs if 0 <= j < CHIPS])
 
 
-def along_row(array, by):
-    return sent(array, lambda i: i // 4 * 4 + (i + by) % 4)
-
-
-def across_rows(array, by):
-    return sent(array, lambda i: i + 4 * by)
+def along_row(array, bits):
+    return sent(array, lambda i: i ^ bits)
+
+
+def across_rows(array, first):
+    def partner(i):
+        row = i // 4
+        return i + 4 if row % 2 == first else i - 4
+
+    return sent(array, partner)
 
 
 def swapped(array):
@@ -396,12 +408,12 @@
 
     picked = pick(sp, segment * SD + place, x)
     x, picked = lax.optimization_barrier((x, picked))
-    two, one, three = (along_row(picked, by) for by in (2, 1, 3))
+    two, one, three = (along_row(picked, bits) for bits in (2, 1, 3))
     got = swapped(x)
     picks, cols, w, count = places(sp, segment, place, damping, extent)
     near = picked + one + two + three
     near, picks, cols, w, count = lax.optimization_barrier((near, picks, cols, w, count))
-    far = near + across_rows(near, 1) + across_rows(near, -1)
+    far = near + across_rows(near, 1) + across_rows(near, 0)
     cov, chg = stats(far, swapped(far), readings, spread, picks, w)
     out = None
     away = []
@@ -411,7 +423,7 @@
         away.append((begin, swapped(part)))
         begin += steps
     for some in (away[:-1], away[-1:]):
-        out = fill([begin for begin, _ in some], sp, [part for _, part in some], out)
+        out = fill([begin for begin, _ in some], [part for _, part in some], out)
     return out
 
 

time: 46.8 us -> 42.6 us (0.910)
  waiting for transfers between devices: 8.51 us -> 6.99 us
  starting transfers between devices: 14.7 us -> 13.6 us
  Pallas kernels: 21.9 us -> 20.8 us
    ppermute x5, waiting for transfers between devices: 7.56 us -> 5.5 us  [sent(): lax.ppermute(array, 'state', [(i, j) for i, j in pairs if 0 <= j < CHIPS])]
    pallas_call x2, Pallas kernels: 3.25 us -> 2.16 us  [fill(): pl.pallas_call(kernel, in_specs=[pl.BlockSpec(memory_space=pltpu.VMEM)] *...]
    ppermute x5, starting transfers between devices: 10.3 us -> 9.23 us  [sent(): lax.ppermute(array, 'state', [(i, j) for i, j in pairs if 0 <= j < CHIPS])]
    ppermute x4, waiting for transfers between devices: 0.95 us -> 1.5 us  [swapped(): return lax.ppermute(array, 'mem', [(0, 1), (1, 0)])]
  transfers between devices with their start and end apart: 9 -> 9, of which waited for: 5 -> 4; matrix products, arithmetic and copies ran while one was open for 0% -> 0% of each run, Pallas kernels for 19% -> 19%
where the time goes in v6:
time: 42.6 us; the launch traced here: 42.4 us
  Pallas kernels  20.8 us (49%)
  starting transfers between devices  13.6 us (32%)
  waiting for transfers between devices  6.99 us (16%)
  other arithmetic  0.85 us (2%)
    pallas_call x2, Pallas kernels, update(): pl.pallas_call(lambda *refs: update_kernel(begin, *refs), grid_spec=pltpu...  13.1 us
    ppermute x5, starting transfers between devices, sent(): lax.ppermute(array, 'state', [(i, j) for i, j in pairs if 0 <= j < CHIPS])  9.23 us
    ppermute x5, waiting for transfers between devices, sent(): lax.ppermute(array, 'state', [(i, j) for i, j in pairs if 0 <= j < CHIPS])  5.5 us
    ppermute x4, starting transfers between devices, swapped(): return lax.ppermute(array, 'mem', [(0, 1), (1, 0)])  4.34 us
    pallas_call x1, Pallas kernels, pick(): pl.pallas_call(pick_kernel, grid_spec=pltpu.PrefetchScalarGridSpec(num_sc...  3.29 us
    pallas_call x2, Pallas kernels, fill(): pl.pallas_call(kernel, in_specs=[pl.BlockSpec(memory_space=pltpu.VMEM)] *...  2.16 us
    ppermute x4, waiting for transfers between devices, swapped(): return lax.ppermute(array, 'mem', [(0, 1), (1, 0)])  1.5 us
    pallas_call x1, Pallas kernels, places(): pl.pallas_call(places_kernel, grid_spec=pltpu.PrefetchScalarGridSpec(num_...  1.48 us
  transfers between devices with their start and end apart: 9, of which 4 were waited for; matrix products, arithmetic and copies ran while one was open for 0% of the time, Pallas kernels for 19%

profile of v6, /device:TPU:9, one launch (start us, length us, event | category | flops | bytes accessed | tf_op | source)
XLA Modules:
  0.0 42.4 jit_solution(10038404701930721242)
XLA Ops:
  0.0 0.7 %multiply_add_fusion.index_ref = s32[2,256]{1,0:T(2,128)S(1)} fusion(s32[2,256]{1,0:T(2,128)} %place_ref.1, s32[2,256]{1,0:T(2,128)} %seg_ref.1), kind=kLoop, calls=%fused_computation.2 | loop fusion | flops 1024 | bytes 6144 | tf_op jit(solution)/shard_map/add | solution.py:409
  0.8 0.1 pad_add_fusion.sp_ref.refs_0_
  0.9 3.3 %pick.1 = bf16[40,512]{1,0:T(8,128)(2,1)S(1)} custom-call(s32[3]{0:T(128)S(1)} %pad_add_fusion.sp_ref.refs_0_, s32[2,256]{1,0:T(2,128)S(1)} %multiply_add_fusion.index_ref, bf16[40,65536]{1,0:T(8,128)(2,1)} %refs_5_.1), custom_call_target="tpu_custom_call" | custom-call | bytes 5242880 | tf_op jit(solution)/shard_map/pick/pallas_call | solution.py:99
  4.2 0.8 %collective-permute-start.6 = (bf16[40,65536]{1,0:T(8,128)(2,1)}, bf16[40,65536]{1,0:T(8,128)(2,1)S(1)}, u32[]{:S(2)}, u32[]{:S(2)}) collective-permute-start(bf16[40,65536]{1,0:T(8,128)(2,1)} %refs_5_.1), channel_id=1, source_target_pairs={{0,64},{64,0},{1,65},{65,1},{2,66},{66,2},{3,67},{67,3},{4,68},{68... | collective-permute-start | bytes 15728648 | tf_op jit(solution)/shard_map/ppermute | solution.py:401
  4.9 3.8 %collective-permute-start.2 = (bf16[40,512]{1,0:T(8,128)(2,1)S(1)}, bf16[40,512]{1,0:T(8,128)(2,1)S(1)}, u32[]{:S(2)}, u32[]{:S(2)}) collective-permute-start(bf16[40,512]{1,0:T(8,128)(2,1)S(1)} %pick.1), channel_id=1, source_target_pairs={{0,3},{1,2},{2,1},{3,0},{4,7},{5,6},{6,5},{7,4},{8,11},{9,10},{10,... | collective-permute-start | bytes 122888 | tf_op jit(solution)/shard_map/ppermute | solution.py:385
  8.7 0.0 collective-permute-start.1
  8.7 0.6 %collective-permute-start = (bf16[40,512]{1,0:T(8,128)(2,1)S(1)}, bf16[40,512]{1,0:T(8,128)(2,1)S(1)}, u32[]{:S(2)}, u32[]{:S(2)}) collective-permute-start(bf16[40,512]{1,0:T(8,128)(2,1)S(1)} %pick.1), channel_id=1, source_target_pairs={{0,1},{1,0},{2,3},{3,2},{4,5},{5,4},{6,7},{7,6},{8,9},{9,8},{10,11... | collective-permute-start | bytes 122888 | tf_op jit(solution)/shard_map/ppermute | solution.py:385
  9.3 1.5 %places.1 = (bf16[2,256,256]{2,1,0:T(8,128)(2,1)S(1)}, f32[2,3,256,128]{3,2,1,0:T(8,128)S(1)}, f32[256,256]{1,0:T(8,128)S(1)}, s32[1]{0:T(128)}) custom-call(s32[3]{0:T(128)S(1)} %pad_add_fusion.sp_ref.refs_0_, s32[2,256]{1,0:T(2,128)S(1)} %copy-done, s32[2,256]{1,0:T(2,128)S(1)} %copy-done.1, f32[2,256]{1,0:T(2,128)S(1)} %copy-done.4, s32[2,256]{1,0:T(2,128)S(1)} %copy-done.5), custom_call_target="tpu_custom_call" | custom-call | flops 1000000 | bytes 2000000 | tf_op jit(solution)/shard_map/places/pallas_call | solution.py:154
  10.8 0.0 collective-permute-done.2
  10.8 2.3 %collective-permute-done.1 = bf16[40,512]{1,0:T(8,128)(2,1)S(1)} collective-permute-done((bf16[40,512]{1,0:T(8,128)(2,1)S(1)}, bf16[40,512]{1,0:T(8,128)(2,1)S(1)}, u32[]{:S(2)}, u32[]{:S(2)}) %collective-permute-start.1) | collective-permute-done | bytes 40992 | tf_op jit(solution)/shard_map/ppermute | solution.py:385
  13.1 1.3 %collective-permute-start.4 = (bf16[40,512]{1,0:T(8,128)(2,1)S(1)}, bf16[40,512]{1,0:T(8,128)(2,1)S(1)}, u32[]{:S(2)}, u32[]{:S(2)}) collective-permute-start(bf16[40,512]{1,0:T(8,128)(2,1)S(1)} %add_add_fusion.1), channel_id=1, source_target_pairs={{0,4},{1,5},{2,6},{3,7},{4,0},{5,1},{6,2},{7,3},{8,12},{9,13},{10,... | collective-permute-start | bytes 122888 | tf_op jit(solution)/shard_map/ppermute | solution.py:385
  14.3 3.6 %collective-permute-start.3 = (bf16[40,512]{1,0:T(8,128)(2,1)S(1)}, bf16[40,512]{1,0:T(8,128)(2,1)S(1)}, u32[]{:S(2)}, u32[]{:S(2)}) collective-permute-start(bf16[40,512]{1,0:T(8,128)(2,1)S(1)} %add_add_fusion.1), channel_id=1, source_target_pairs={{4,8},{5,9},{6,10},{7,11},{8,4},{9,5},{10,6},{11,7},{12,16},{13,17... | collective-permute-start | bytes 122888 | tf_op jit(solution)/shard_map/ppermute | solution.py:385
  18.0 0.0 collective-permute-done.4
  18.0 3.2 %collective-permute-done.3 = bf16[40,512]{1,0:T(8,128)(2,1)S(1)} collective-permute-done((bf16[40,512]{1,0:T(8,128)(2,1)S(1)}, bf16[40,512]{1,0:T(8,128)(2,1)S(1)}, u32[]{:S(2)}, u32[]{:S(2)}) %collective-permute-start.3) | collective-permute-done | bytes 40992 | tf_op jit(solution)/shard_map/ppermute | solution.py:385
  21.2 3.1 %collective-permute-start.5 = (bf16[40,512]{1,0:T(8,128)(2,1)S(1)}, bf16[40,512]{1,0:T(8,128)(2,1)S(1)}, u32[]{:S(2)}, u32[]{:S(2)}) collective-permute-start(bf16[40,512]{1,0:T(8,128)(2,1)S(1)} %add_add_fusion.mine_ref), channel_id=1, source_target_pairs={{0,64},{64,0},{1,65},{65,1},{2,66},{66,2},{3,67},{67,3},{4,68},{68... | collective-permute-start | bytes 122888 | tf_op jit(solution)/shard_map/ppermute | solution.py:401
  24.3 0.9 %collective-permute-done.5.other_ref = bf16[40,512]{1,0:T(8,128)(2,1)S(1)} collective-permute-done((bf16[40,512]{1,0:T(8,128)(2,1)S(1)}, bf16[40,512]{1,0:T(8,128)(2,1)S(1)}, u32[]{:S(2)}, u32[]{:S(2)}) %collective-permute-start.5) | collective-permute-done | bytes 40992 | tf_op jit(solution)/shard_map/ppermute | solution.py:401
  25.2 0.8 %stats.1 = (bf16[2,256,96]{2,1,0:T(8,128)(2,1)S(1)}, bf16[2,80,256]{2,1,0:T(8,128)(2,1)S(1)}) custom-call(bf16[40,512]{1,0:T(8,128)(2,1)S(1)} %add_add_fusion.mine_ref, bf16[40,512]{1,0:T(8,128)(2,1)S(1)} %collective-permute-done.5.other_ref, f32[2,256]{1,0:T(2,128)S(1)} %copy-done.2, f32[2,256]{1,0:T(2,128)S(1)} %copy-done.3, ...), custom_call_target="tpu_custom_call" | custom-call | tf_op jit(solution)/shard_map/stats/pallas_call | solution.py:216
  25.9 8.5 %update0.1 = (bf16[40,65536]{1,0:T(8,128)(2,1)}, bf16[40,24576]{1,0:T(8,128)(2,1)S(1)}) custom-call(s32[3]{0:T(128)S(1)} %pad_add_fusion.sp_ref.refs_0_, s32[1]{0:T(128)} %get-tuple-element.27.refs_1_, bf16[2,256,96]{2,1,0:T(8,128)(2,1)S(1)} %get-tuple-element.31.refs_2_, bf16[2,80,256]{2,1,0:T(8,128)(2,1)S(1)} %get-tuple-element.32.refs_3_, ...), custom_call_target="tpu_custom_call" | custom-call | flops 3600000000 | bytes 7864320 | tf_op jit(solution)/shard_map/update0/pallas_call | solution.py:327
  34.4 0.3 collective-permute-start.8
  34.8 4.6 %update6.1 = (bf16[40,65536]{1,0:T(8,128)(2,1)}, bf16[40,8192]{1,0:T(8,128)(2,1)S(1)}) custom-call(s32[3]{0:T(128)S(1)} %pad_add_fusion.sp_ref.refs_0_, s32[1]{0:T(128)} %get-tuple-element.27.refs_1_, bf16[2,256,96]{2,1,0:T(8,128)(2,1)S(1)} %get-tuple-element.31.refs_2_, ...), custom_call_target="tpu_custom_call", output_to_operand_aliasing={{0}: (7, {})} | custom-call | flops 1200000000 | bytes 2621440 | tf_op jit(solution)/shard_map/update6/pallas_call | solution.py:327
  39.4 0.2 collective-permute-start.7
  39.6 1.3 %fill0.1.refs_1_ = bf16[40,65536]{1,0:T(8,128)(2,1)} custom-call(bf16[40,24576]{1,0:T(8,128)(2,1)S(1)} %collective-permute-done.8.refs_0_, bf16[40,65536]{1,0:T(8,128)(2,1)} %get-tuple-element.38.refs_1_), custom_call_target="tpu_custom_call", output_to_operand_aliasing={{}: (1, {})} | custom-call | tf_op jit(solution)/shard_map/fill0/pallas_call | solution.py:370
  40.9 0.6 %collective-permute-done.7.refs_0_ = bf16[40,8192]{1,0:T(8,128)(2,1)S(1)} collective-permute-done((bf16[40,8192]{1,0:T(8,128)(2,1)S(1)}, bf16[40,8192]{1,0:T(8,128)(2,1)S(1)}, u32[]{:S(2)}, u32[]{:S(2)}) %collective-permute-start.7) | collective-permute-done | bytes 655392 | tf_op jit(solution)/shard_map/ppermute | solution.py:401
  41.5 0.9 %fill6.1 = bf16[40,65536]{1,0:T(8,128)(2,1)} custom-call(bf16[40,8192]{1,0:T(8,128)(2,1)S(1)} %collective-permute-done.7.refs_0_, bf16[40,65536]{1,0:T(8,128)(2,1)} %fill0.1.refs_1_), custom_call_target="tpu_custom_call", output_to_operand_aliasing={{}: (1, {})} | custom-call | tf_op jit(solution)/shard_map/fill6/pallas_call | solution.py:370
  (17 shorter events, 0.1 us)
Async XLA Ops:
  0.0 9.3 %copy-start.1 = (s32[2,256]{1,0:T(2,128)S(1)}, s32[2,256]{1,0:T(2,128)}, u32[]{:S(2)}) copy-start(s32[2,256]{1,0:T(2,128)} %place_ref.1) | copy-start | bytes 6148
  0.0 9.3 %copy-start = (s32[2,256]{1,0:T(2,128)S(1)}, s32[2,256]{1,0:T(2,128)}, u32[]{:S(2)}) copy-start(s32[2,256]{1,0:T(2,128)} %seg_ref.1) | copy-start | bytes 6148
  0.0 9.3 %copy-start.5 = (s32[2,256]{1,0:T(2,128)S(1)}, s32[2,256]{1,0:T(2,128)}, u32[]{:S(2)}) copy-start(s32[2,256]{1,0:T(2,128)} %ext_ref.1) | copy-start | bytes 6148
  0.0 9.3 %copy-start.4 = (f32[2,256]{1,0:T(2,128)S(1)}, f32[2,256]{1,0:T(2,128)}, u32[]{:S(2)}) copy-start(f32[2,256]{1,0:T(2,128)} %damp_ref.1) | copy-start | bytes 6148
  0.0 25.1 %copy-start.3 = (f32[2,256]{1,0:T(2,128)S(1)}, f32[2,256]{1,0:T(2,128)}, u32[]{:S(2)}) copy-start(f32[2,256]{1,0:T(2,128)} %var_ref.1) | copy-start | bytes 6148
  0.0 25.1 %copy-start.2 = (f32[2,256]{1,0:T(2,128)S(1)}, f32[2,256]{1,0:T(2,128)}, u32[]{:S(2)}) copy-start(f32[2,256]{1,0:T(2,128)} %val_ref.1) | copy-start | bytes 6148
  4.2 21.8 %collective-permute-start.6 = (bf16[40,65536]{1,0:T(8,128)(2,1)}, bf16[40,65536]{1,0:T(8,128)(2,1)S(1)}, u32[]{:S(2)}, u32[]{:S(2)}) collective-permute-start(bf16[40,65536]{1,0:T(8,128)(2,1)} %refs_5_.1), channel_id=1, source_target_pairs={{0,64},{64,0},{1,65},{65,1},{2,66},{66,2},{3,67},{67,3},{4,68},{68... | collective-permute-start | bytes 15728648 | tf_op jit(solution)/shard_map/ppermute | solution.py:401
  4.9 5.8 %collective-permute-start.2 = (bf16[40,512]{1,0:T(8,128)(2,1)S(1)}, bf16[40,512]{1,0:T(8,128)(2,1)S(1)}, u32[]{:S(2)}, u32[]{:S(2)}) collective-permute-start(bf16[40,512]{1,0:T(8,128)(2,1)S(1)} %pick.1), channel_id=1, source_target_pairs={{0,3},{1,2},{2,1},{3,0},{4,7},{5,6},{6,5},{7,4},{8,11},{9,10},{10,... | collective-permute-start | bytes 122888 | tf_op jit(solution)/shard_map/ppermute | solution.py:385
  8.7 4.4 %collective-permute-start.1 = (bf16[40,512]{1,0:T(8,128)(2,1)S(1)}, bf16[40,512]{1,0:T(8,128)(2,1)S(1)}, u32[]{:S(2)}, u32[]{:S(2)}) collective-permute-start(bf16[40,512]{1,0:T(8,128)(2,1)S(1)} %pick.1), channel_id=1, source_target_pairs={{0,2},{1,3},{2,0},{3,1},{4,6},{5,7},{6,4},{7,5},{8,10},{9,11},{10,... | collective-permute-start | bytes 122888 | tf_op jit(solution)/shard_map/ppermute | solution.py:385
  8.7 4.4 %collective-permute-start = (bf16[40,512]{1,0:T(8,128)(2,1)S(1)}, bf16[40,512]{1,0:T(8,128)(2,1)S(1)}, u32[]{:S(2)}, u32[]{:S(2)}) collective-permute-start(bf16[40,512]{1,0:T(8,128)(2,1)S(1)} %pick.1), channel_id=1, source_target_pairs={{0,1},{1,0},{2,3},{3,2},{4,5},{5,4},{6,7},{7,6},{8,9},{9,8},{10,11... | collective-permute-start | bytes 122888 | tf_op jit(solution)/shard_map/ppermute | solution.py:385
  13.1 4.9 %collective-permute-start.4 = (bf16[40,512]{1,0:T(8,128)(2,1)S(1)}, bf16[40,512]{1,0:T(8,128)(2,1)S(1)}, u32[]{:S(2)}, u32[]{:S(2)}) collective-permute-start(bf16[40,512]{1,0:T(8,128)(2,1)S(1)} %add_add_fusion.1), channel_id=1, source_target_pairs={{0,4},{1,5},{2,6},{3,7},{4,0},{5,1},{6,2},{7,3},{8,12},{9,13},{10,... | collective-permute-start | bytes 122888 | tf_op jit(solution)/shard_map/ppermute | solution.py:385
  14.3 6.8 %collective-permute-start.3 = (bf16[40,512]{1,0:T(8,128)(2,1)S(1)}, bf16[40,512]{1,0:T(8,128)(2,1)S(1)}, u32[]{:S(2)}, u32[]{:S(2)}) collective-permute-start(bf16[40,512]{1,0:T(8,128)(2,1)S(1)} %add_add_fusion.1), channel_id=1, source_target_pairs={{4,8},{5,9},{6,10},{7,11},{8,4},{9,5},{10,6},{11,7},{12,16},{13,17... | collective-permute-start | bytes 122888 | tf_op jit(solution)/shard_map/ppermute | solution.py:385
  21.2 3.9 %collective-permute-start.5 = (bf16[40,512]{1,0:T(8,128)(2,1)S(1)}, bf16[40,512]{1,0:T(8,128)(2,1)S(1)}, u32[]{:S(2)}, u32[]{:S(2)}) collective-permute-start(bf16[40,512]{1,0:T(8,128)(2,1)S(1)} %add_add_fusion.mine_ref), channel_id=1, source_target_pairs={{0,64},{64,0},{1,65},{65,1},{2,66},{66,2},{3,67},{67,3},{4,68},{68... | collective-permute-start | bytes 122888 | tf_op jit(solution)/shard_map/ppermute | solution.py:401
  34.4 5.1 %collective-permute-start.8 = (bf16[40,24576]{1,0:T(8,128)(2,1)S(1)}, bf16[40,24576]{1,0:T(8,128)(2,1)S(1)}, u32[]{:S(2)}, u32[]{:S(2)}) collective-permute-start(bf16[40,24576]{1,0:T(8,128)(2,1)S(1)} %get-tuple-element.37), channel_id=1, source_target_pairs={{0,64},{64,0},{1,65},{65,1},{2,66},{66,2},{3,67},{67,3},{4,68},{68... | collective-permute-start | bytes 5898248 | tf_op jit(solution)/shard_map/ppermute | solution.py:401
  39.4 2.1 %collective-permute-start.7 = (bf16[40,8192]{1,0:T(8,128)(2,1)S(1)}, bf16[40,8192]{1,0:T(8,128)(2,1)S(1)}, u32[]{:S(2)}, u32[]{:S(2)}) collective-permute-start(bf16[40,8192]{1,0:T(8,128)(2,1)S(1)} %get-tuple-element.36), channel_id=1, source_target_pairs={{0,64},{64,0},{1,65},{65,1},{2,66},{66,2},{3,67},{67,3},{4,68},{68... | collective-permute-start | bytes 1966088 | tf_op jit(solution)/shard_map/ppermute | solution.py:401

commit v7 on v6

--- a/solution.py
+++ b/solution.py
@@ -14,11 +14,11 @@
 CHIP = 2 * SD
 CHIPS = 64
 SEG_BLOCKS = SD // LB
-CHUNK = 4096
+CHUNK = 8192
 STEPS = SD // CHUNK
 CHUNK_BLOCKS = CHUNK // LB
-PARTS = (6, 2)
-IN_FLIGHT = {32: 16, 64: 16, 128: 8, K: 4}
+PARTS = (3, 1)
+IN_FLIGHT = {32: 32, 64: 32, 128: 8, K: 4}
 PIECES = 4
 FLIGHT = 16
 EXTRA = 16
@@ -413,7 +413,7 @@
     picks, cols, w, count = places(sp, segment, place, damping, extent)
     near = picked + one + two + three
     near, picks, cols, w, count = lax.optimization_barrier((near, picks, cols, w, count))
-    far = near + across_rows(near, 1) + across_rows(near, 0)
+    far = near + across_rows(near, 0) + across_rows(near, 1)
     cov, chg = stats(far, swapped(far), readings, spread, picks, w)
     out = None
     away = []

time: 42.6 us -> 40.6 us (0.953); the launches traced: 42.4 us -> 39.9 us
  Pallas kernels: 20.8 us -> 19.5 us
  starting transfers between devices: 13.6 us -> 12.9 us
    pallas_call x2, Pallas kernels: 13.1 us -> 11.6 us  [update(): pl.pallas_call(lambda *refs: update_kernel(begin, *refs), grid_spec=pltpu...]
    ppermute x5, starting transfers between devices: 9.23 us -> 8.56 us  [sent(): lax.ppermute(array, 'state', [(i, j) for i, j in pairs if 0 <= j < CHIPS])]
    ppermute x5, waiting for transfers between devices: 5.5 us -> 5.06 us  [sent(): lax.ppermute(array, 'state', [(i, j) for i, j in pairs if 0 <= j < CHIPS])]
  transfers between devices with their start and end apart: 9 -> 9, of which waited for: 4 -> 5; matrix products, arithmetic and copies ran while one was open for 0% -> 0% of each run, Pallas kernels for 19% -> 20%
where the time goes in v7:
time: 40.6 us; the launch traced here: 39.9 us
  Pallas kernels  19.5 us (48%)
  starting transfers between devices  12.9 us (32%)
  waiting for transfers between devices  6.57 us (16%)
  other arithmetic  0.85 us (2%)
    pallas_call x2, Pallas kernels, update(): pl.pallas_call(lambda *refs: update_kernel(begin, *refs), grid_spec=pltpu...  11.6 us
    ppermute x5, starting transfers between devices, sent(): lax.ppermute(array, 'state', [(i, j) for i, j in pairs if 0 <= j < CHIPS])  8.56 us
    ppermute x5, waiting for transfers between devices, sent(): lax.ppermute(array, 'state', [(i, j) for i, j in pairs if 0 <= j < CHIPS])  5.06 us
    ppermute x4, starting transfers between devices, swapped(): return lax.ppermute(array, 'mem', [(0, 1), (1, 0)])  4.34 us
    pallas_call x1, Pallas kernels, pick(): pl.pallas_call(pick_kernel, grid_spec=pltpu.PrefetchScalarGridSpec(num_sc...  3.47 us
    pallas_call x2, Pallas kernels, fill(): pl.pallas_call(kernel, in_specs=[pl.BlockSpec(memory_space=pltpu.VMEM)] *...  2.16 us
    ppermute x4, waiting for transfers between devices, swapped(): return lax.ppermute(array, 'mem', [(0, 1), (1, 0)])  1.51 us
    pallas_call x1, Pallas kernels, places(): pl.pallas_call(places_kernel, grid_spec=pltpu.PrefetchScalarGridSpec(num_...  1.48 us
  transfers between devices with their start and end apart: 9, of which 5 were waited for; matrix products, arithmetic and copies ran while one was open for 0% of the time, Pallas kernels for 20%

profile of v7, /device:TPU:9, one launch (start us, length us, event | category | flops | bytes accessed | tf_op | source)
XLA Modules:
  0.0 39.9 jit_solution(15691975659382287641)
XLA Ops:
  0.0 0.7 %multiply_add_fusion.index_ref = s32[2,256]{1,0:T(2,128)S(1)} fusion(s32[2,256]{1,0:T(2,128)} %place_ref.1, s32[2,256]{1,0:T(2,128)} %seg_ref.1), kind=kLoop, calls=%fused_computation.2 | loop fusion | flops 1024 | bytes 6144 | tf_op jit(solution)/shard_map/add | solution.py:409
  0.8 0.1 pad_add_fusion.sp_ref.refs_0_
  0.9 3.5 %pick.1 = bf16[40,512]{1,0:T(8,128)(2,1)S(1)} custom-call(s32[3]{0:T(128)S(1)} %pad_add_fusion.sp_ref.refs_0_, s32[2,256]{1,0:T(2,128)S(1)} %multiply_add_fusion.index_ref, bf16[40,65536]{1,0:T(8,128)(2,1)} %refs_5_.1), custom_call_target="tpu_custom_call" | custom-call | bytes 5242880 | tf_op jit(solution)/shard_map/pick/pallas_call | solution.py:99
  4.4 0.8 %collective-permute-start.6 = (bf16[40,65536]{1,0:T(8,128)(2,1)}, bf16[40,65536]{1,0:T(8,128)(2,1)S(1)}, u32[]{:S(2)}, u32[]{:S(2)}) collective-permute-start(bf16[40,65536]{1,0:T(8,128)(2,1)} %refs_5_.1), channel_id=1, source_target_pairs={{0,64},{64,0},{1,65},{65,1},{2,66},{66,2},{3,67},{67,3},{4,68},{68... | collective-permute-start | bytes 15728648 | tf_op jit(solution)/shard_map/ppermute | solution.py:401
  5.1 3.6 %collective-permute-start.2 = (bf16[40,512]{1,0:T(8,128)(2,1)S(1)}, bf16[40,512]{1,0:T(8,128)(2,1)S(1)}, u32[]{:S(2)}, u32[]{:S(2)}) collective-permute-start(bf16[40,512]{1,0:T(8,128)(2,1)S(1)} %pick.1), channel_id=1, source_target_pairs={{0,3},{1,2},{2,1},{3,0},{4,7},{5,6},{6,5},{7,4},{8,11},{9,10},{10,... | collective-permute-start | bytes 122888 | tf_op jit(solution)/shard_map/ppermute | solution.py:385
  8.7 0.0 collective-permute-start.1
  8.7 0.5 %collective-permute-start = (bf16[40,512]{1,0:T(8,128)(2,1)S(1)}, bf16[40,512]{1,0:T(8,128)(2,1)S(1)}, u32[]{:S(2)}, u32[]{:S(2)}) collective-permute-start(bf16[40,512]{1,0:T(8,128)(2,1)S(1)} %pick.1), channel_id=1, source_target_pairs={{0,1},{1,0},{2,3},{3,2},{4,5},{5,4},{6,7},{7,6},{8,9},{9,8},{10,11... | collective-permute-start | bytes 122888 | tf_op jit(solution)/shard_map/ppermute | solution.py:385
  9.3 1.5 %places.1 = (bf16[2,256,256]{2,1,0:T(8,128)(2,1)S(1)}, f32[2,3,256,128]{3,2,1,0:T(8,128)S(1)}, f32[256,256]{1,0:T(8,128)S(1)}, s32[1]{0:T(128)}) custom-call(s32[3]{0:T(128)S(1)} %pad_add_fusion.sp_ref.refs_0_, s32[2,256]{1,0:T(2,128)S(1)} %copy-done, s32[2,256]{1,0:T(2,128)S(1)} %copy-done.1, f32[2,256]{1,0:T(2,128)S(1)} %copy-done.4, s32[2,256]{1,0:T(2,128)S(1)} %copy-done.5), custom_call_target="tpu_custom_call" | custom-call | flops 1000000 | bytes 2000000 | tf_op jit(solution)/shard_map/places/pallas_call | solution.py:154
  10.8 0.0 collective-permute-done.2
  10.8 2.3 %collective-permute-done.1 = bf16[40,512]{1,0:T(8,128)(2,1)S(1)} collective-permute-done((bf16[40,512]{1,0:T(8,128)(2,1)S(1)}, bf16[40,512]{1,0:T(8,128)(2,1)S(1)}, u32[]{:S(2)}, u32[]{:S(2)}) %collective-permute-start.1) | collective-permute-done | bytes 40992 | tf_op jit(solution)/shard_map/ppermute | solution.py:385
  13.1 4.3 %collective-permute-start.4 = (bf16[40,512]{1,0:T(8,128)(2,1)S(1)}, bf16[40,512]{1,0:T(8,128)(2,1)S(1)}, u32[]{:S(2)}, u32[]{:S(2)}) collective-permute-start(bf16[40,512]{1,0:T(8,128)(2,1)S(1)} %add_add_fusion.1), channel_id=1, source_target_pairs={{4,8},{5,9},{6,10},{7,11},{8,4},{9,5},{10,6},{11,7},{12,16},{13,17... | collective-permute-start | bytes 122888 | tf_op jit(solution)/shard_map/ppermute | solution.py:385
  17.3 0.1 collective-permute-start.3
  17.5 2.4 %collective-permute-done.4 = bf16[40,512]{1,0:T(8,128)(2,1)S(1)} collective-permute-done((bf16[40,512]{1,0:T(8,128)(2,1)S(1)}, bf16[40,512]{1,0:T(8,128)(2,1)S(1)}, u32[]{:S(2)}, u32[]{:S(2)}) %collective-permute-start.4) | collective-permute-done | bytes 40992 | tf_op jit(solution)/shard_map/ppermute | solution.py:385
  19.9 0.4 collective-permute-done.3
  20.3 3.1 %collective-permute-start.5 = (bf16[40,512]{1,0:T(8,128)(2,1)S(1)}, bf16[40,512]{1,0:T(8,128)(2,1)S(1)}, u32[]{:S(2)}, u32[]{:S(2)}) collective-permute-start(bf16[40,512]{1,0:T(8,128)(2,1)S(1)} %add_add_fusion.mine_ref), channel_id=1, source_target_pairs={{0,64},{64,0},{1,65},{65,1},{2,66},{66,2},{3,67},{67,3},{4,68},{68... | collective-permute-start | bytes 122888 | tf_op jit(solution)/shard_map/ppermute | solution.py:401
  23.4 0.9 %collective-permute-done.5.other_ref = bf16[40,512]{1,0:T(8,128)(2,1)S(1)} collective-permute-done((bf16[40,512]{1,0:T(8,128)(2,1)S(1)}, bf16[40,512]{1,0:T(8,128)(2,1)S(1)}, u32[]{:S(2)}, u32[]{:S(2)}) %collective-permute-start.5) | collective-permute-done | bytes 40992 | tf_op jit(solution)/shard_map/ppermute | solution.py:401
  24.2 0.8 %stats.1 = (bf16[2,256,96]{2,1,0:T(8,128)(2,1)S(1)}, bf16[2,80,256]{2,1,0:T(8,128)(2,1)S(1)}) custom-call(bf16[40,512]{1,0:T(8,128)(2,1)S(1)} %add_add_fusion.mine_ref, bf16[40,512]{1,0:T(8,128)(2,1)S(1)} %collective-permute-done.5.other_ref, f32[2,256]{1,0:T(2,128)S(1)} %copy-done.2, f32[2,256]{1,0:T(2,128)S(1)} %copy-done.3, ...), custom_call_target="tpu_custom_call" | custom-call | tf_op jit(solution)/shard_map/stats/pallas_call | solution.py:216
  25.0 7.1 %update0.1 = (bf16[40,65536]{1,0:T(8,128)(2,1)}, bf16[40,24576]{1,0:T(8,128)(2,1)S(1)}) custom-call(s32[3]{0:T(128)S(1)} %pad_add_fusion.sp_ref.refs_0_, s32[1]{0:T(128)} %get-tuple-element.27.refs_1_, bf16[2,256,96]{2,1,0:T(8,128)(2,1)S(1)} %get-tuple-element.31.refs_2_, bf16[2,80,256]{2,1,0:T(8,128)(2,1)S(1)} %get-tuple-element.32.refs_3_, ...), custom_call_target="tpu_custom_call" | custom-call | flops 1800000000 | bytes 7864320 | tf_op jit(solution)/shard_map/update0/pallas_call | solution.py:327
  32.2 0.4 collective-permute-start.8
  32.5 4.4 %update3.1 = (bf16[40,65536]{1,0:T(8,128)(2,1)}, bf16[40,8192]{1,0:T(8,128)(2,1)S(1)}) custom-call(s32[3]{0:T(128)S(1)} %pad_add_fusion.sp_ref.refs_0_, s32[1]{0:T(128)} %get-tuple-element.27.refs_1_, bf16[2,256,96]{2,1,0:T(8,128)(2,1)S(1)} %get-tuple-element.31.refs_2_, ...), custom_call_target="tpu_custom_call", output_to_operand_aliasing={{0}: (7, {})} | custom-call | flops 600000000 | bytes 2621440 | tf_op jit(solution)/shard_map/update3/pallas_call | solution.py:327
  36.9 0.2 collective-permute-start.7
  37.1 1.3 %fill0.1.refs_1_ = bf16[40,65536]{1,0:T(8,128)(2,1)} custom-call(bf16[40,24576]{1,0:T(8,128)(2,1)S(1)} %collective-permute-done.8.refs_0_, bf16[40,65536]{1,0:T(8,128)(2,1)} %get-tuple-element.38.refs_1_), custom_call_target="tpu_custom_call", output_to_operand_aliasing={{}: (1, {})} | custom-call | tf_op jit(solution)/shard_map/fill0/pallas_call | solution.py:370
  38.4 0.6 %collective-permute-done.7.refs_0_ = bf16[40,8192]{1,0:T(8,128)(2,1)S(1)} collective-permute-done((bf16[40,8192]{1,0:T(8,128)(2,1)S(1)}, bf16[40,8192]{1,0:T(8,128)(2,1)S(1)}, u32[]{:S(2)}, u32[]{:S(2)}) %collective-permute-start.7) | collective-permute-done | bytes 655392 | tf_op jit(solution)/shard_map/ppermute | solution.py:401
  39.0 0.9 %fill3.1 = bf16[40,65536]{1,0:T(8,128)(2,1)} custom-call(bf16[40,8192]{1,0:T(8,128)(2,1)S(1)} %collective-permute-done.7.refs_0_, bf16[40,65536]{1,0:T(8,128)(2,1)} %fill0.1.refs_1_), custom_call_target="tpu_custom_call", output_to_operand_aliasing={{}: (1, {})} | custom-call | tf_op jit(solution)/shard_map/fill3/pallas_call | solution.py:370
  (17 shorter events, 0.1 us)
Async XLA Ops:
  0.0 9.3 %copy-start.1 = (s32[2,256]{1,0:T(2,128)S(1)}, s32[2,256]{1,0:T(2,128)}, u32[]{:S(2)}) copy-start(s32[2,256]{1,0:T(2,128)} %place_ref.1) | copy-start | bytes 6148
  0.0 9.3 %copy-start = (s32[2,256]{1,0:T(2,128)S(1)}, s32[2,256]{1,0:T(2,128)}, u32[]{:S(2)}) copy-start(s32[2,256]{1,0:T(2,128)} %seg_ref.1) | copy-start | bytes 6148
  0.0 9.3 %copy-start.5 = (s32[2,256]{1,0:T(2,128)S(1)}, s32[2,256]{1,0:T(2,128)}, u32[]{:S(2)}) copy-start(s32[2,256]{1,0:T(2,128)} %ext_ref.1) | copy-start | bytes 6148
  0.0 9.3 %copy-start.4 = (f32[2,256]{1,0:T(2,128)S(1)}, f32[2,256]{1,0:T(2,128)}, u32[]{:S(2)}) copy-start(f32[2,256]{1,0:T(2,128)} %damp_ref.1) | copy-start | bytes 6148
  0.0 24.2 %copy-start.3 = (f32[2,256]{1,0:T(2,128)S(1)}, f32[2,256]{1,0:T(2,128)}, u32[]{:S(2)}) copy-start(f32[2,256]{1,0:T(2,128)} %var_ref.1) | copy-start | bytes 6148
  0.0 24.2 %copy-start.2 = (f32[2,256]{1,0:T(2,128)S(1)}, f32[2,256]{1,0:T(2,128)}, u32[]{:S(2)}) copy-start(f32[2,256]{1,0:T(2,128)} %val_ref.1) | copy-start | bytes 6148
  4.4 20.7 %collective-permute-start.6 = (bf16[40,65536]{1,0:T(8,128)(2,1)}, bf16[40,65536]{1,0:T(8,128)(2,1)S(1)}, u32[]{:S(2)}, u32[]{:S(2)}) collective-permute-start(bf16[40,65536]{1,0:T(8,128)(2,1)} %refs_5_.1), channel_id=1, source_target_pairs={{0,64},{64,0},{1,65},{65,1},{2,66},{66,2},{3,67},{67,3},{4,68},{68... | collective-permute-start | bytes 15728648 | tf_op jit(solution)/shard_map/ppermute | solution.py:401
  5.1 5.7 %collective-permute-start.2 = (bf16[40,512]{1,0:T(8,128)(2,1)S(1)}, bf16[40,512]{1,0:T(8,128)(2,1)S(1)}, u32[]{:S(2)}, u32[]{:S(2)}) collective-permute-start(bf16[40,512]{1,0:T(8,128)(2,1)S(1)} %pick.1), channel_id=1, source_target_pairs={{0,3},{1,2},{2,1},{3,0},{4,7},{5,6},{6,5},{7,4},{8,11},{9,10},{10,... | collective-permute-start | bytes 122888 | tf_op jit(solution)/shard_map/ppermute | solution.py:385
  8.7 4.4 %collective-permute-start.1 = (bf16[40,512]{1,0:T(8,128)(2,1)S(1)}, bf16[40,512]{1,0:T(8,128)(2,1)S(1)}, u32[]{:S(2)}, u32[]{:S(2)}) collective-permute-start(bf16[40,512]{1,0:T(8,128)(2,1)S(1)} %pick.1), channel_id=1, source_target_pairs={{0,2},{1,3},{2,0},{3,1},{4,6},{5,7},{6,4},{7,5},{8,10},{9,11},{10,... | collective-permute-start | bytes 122888 | tf_op jit(solution)/shard_map/ppermute | solution.py:385
  8.7 4.3 %collective-permute-start = (bf16[40,512]{1,0:T(8,128)(2,1)S(1)}, bf16[40,512]{1,0:T(8,128)(2,1)S(1)}, u32[]{:S(2)}, u32[]{:S(2)}) collective-permute-start(bf16[40,512]{1,0:T(8,128)(2,1)S(1)} %pick.1), channel_id=1, source_target_pairs={{0,1},{1,0},{2,3},{3,2},{4,5},{5,4},{6,7},{7,6},{8,9},{9,8},{10,11... | collective-permute-start | bytes 122888 | tf_op jit(solution)/shard_map/ppermute | solution.py:385
  13.1 6.9 %collective-permute-start.4 = (bf16[40,512]{1,0:T(8,128)(2,1)S(1)}, bf16[40,512]{1,0:T(8,128)(2,1)S(1)}, u32[]{:S(2)}, u32[]{:S(2)}) collective-permute-start(bf16[40,512]{1,0:T(8,128)(2,1)S(1)} %add_add_fusion.1), channel_id=1, source_target_pairs={{4,8},{5,9},{6,10},{7,11},{8,4},{9,5},{10,6},{11,7},{12,16},{13,17... | collective-permute-start | bytes 122888 | tf_op jit(solution)/shard_map/ppermute | solution.py:385
  17.3 2.9 %collective-permute-start.3 = (bf16[40,512]{1,0:T(8,128)(2,1)S(1)}, bf16[40,512]{1,0:T(8,128)(2,1)S(1)}, u32[]{:S(2)}, u32[]{:S(2)}) collective-permute-start(bf16[40,512]{1,0:T(8,128)(2,1)S(1)} %add_add_fusion.1), channel_id=1, source_target_pairs={{0,4},{1,5},{2,6},{3,7},{4,0},{5,1},{6,2},{7,3},{8,12},{9,13},{10,... | collective-permute-start | bytes 122888 | tf_op jit(solution)/shard_map/ppermute | solution.py:385
  20.3 3.9 %collective-permute-start.5 = (bf16[40,512]{1,0:T(8,128)(2,1)S(1)}, bf16[40,512]{1,0:T(8,128)(2,1)S(1)}, u32[]{:S(2)}, u32[]{:S(2)}) collective-permute-start(bf16[40,512]{1,0:T(8,128)(2,1)S(1)} %add_add_fusion.mine_ref), channel_id=1, source_target_pairs={{0,64},{64,0},{1,65},{65,1},{2,66},{66,2},{3,67},{67,3},{4,68},{68... | collective-permute-start | bytes 122888 | tf_op jit(solution)/shard_map/ppermute | solution.py:401
  32.2 5.0 %collective-permute-start.8 = (bf16[40,24576]{1,0:T(8,128)(2,1)S(1)}, bf16[40,24576]{1,0:T(8,128)(2,1)S(1)}, u32[]{:S(2)}, u32[]{:S(2)}) collective-permute-start(bf16[40,24576]{1,0:T(8,128)(2,1)S(1)} %get-tuple-element.37), channel_id=1, source_target_pairs={{0,64},{64,0},{1,65},{65,1},{2,66},{66,2},{3,67},{67,3},{4,68},{68... | collective-permute-start | bytes 5898248 | tf_op jit(solution)/shard_map/ppermute | solution.py:401
  36.9 2.1 %collective-permute-start.7 = (bf16[40,8192]{1,0:T(8,128)(2,1)S(1)}, bf16[40,8192]{1,0:T(8,128)(2,1)S(1)}, u32[]{:S(2)}, u32[]{:S(2)}) collective-permute-start(bf16[40,8192]{1,0:T(8,128)(2,1)S(1)} %get-tuple-element.36), channel_id=1, source_target_pairs={{0,64},{64,0},{1,65},{65,1},{2,66},{66,2},{3,67},{67,3},{4,68},{68... | collective-permute-start | bytes 1966088 | tf_op jit(solution)/shard_map/ppermute | solution.py:401

commit v8 on v7

--- a/solution.py
+++ b/solution.py
@@ -143,7 +143,9 @@
         cols_ref[b, 0] = jnp.broadcast_to(column(chosen, block), (K, LB))
         cols_ref[b, 1] = jnp.broadcast_to(jnp.maximum(column(chosen, reach), 1.0), (K, LB))
         cols_ref[b, 2] = jnp.broadcast_to(column(chosen, damping), (K, LB))
-    count_ref[0] = most
+    count_ref[0] = sp_ref[0]
+    count_ref[1] = sp_ref[1]
+    count_ref[2] = most
     distance = jnp.abs(blocks[1:2] - column(diagonal, blocks[0:1]))
     reach = column(diagonal, reaches[0:1])
     damping = column(diagonal, damp_ref[0:1, :])
@@ -168,7 +170,7 @@
             jax.ShapeDtypeStruct((B, K, K), BF16),
             jax.ShapeDtypeStruct((B, 3, K, LB), F32),
             jax.ShapeDtypeStruct((K, K), F32),
-            jax.ShapeDtypeStruct((1,), I32),
+            jax.ShapeDtypeStruct((3,), I32),
         ],
         compiler_params=pltpu.CompilerParams(vmem_limit_bytes=VMEM_LIMIT),
         cost_estimate=pl.CostEstimate(
@@ -238,7 +240,7 @@
     return pl.ds(pl.multiple_of(base + a, 256), 256)
 
 
-def update_kernel(begin, sp_ref, count_ref, cov_ref, chg_ref, cols, mine_ref, other_ref, *rest):
+def update_kernel(begin, sp_ref, cov_ref, chg_ref, cols, mine_ref, other_ref, *rest):
     own_ref, away_ref = rest[-2:]
     step = pl.program_id(0) + begin
     there = sp_ref[0] * SD + step * CHUNK
@@ -293,7 +295,7 @@
 
         lax.fori_loop(0, rounds, body, 0)
 
-    n = count_ref[0]
+    n = sp_ref[2]
 
     @pl.when(n <= 32)
     def _():
@@ -312,13 +314,13 @@
         advance(K)
 
 
-def update(begin, steps, sp, count, cov, chg, cols, x, got, out):
-    half = lambda i, s, c: (0, s[0] * STEPS + begin + i)
+def update(begin, steps, info, cov, chg, cols, x, got, out):
+    half = lambda i, s: (0, s[0] * STEPS + begin + i)
     in_specs = [pl.BlockSpec(memory_space=pltpu.VMEM)] * 3 + [
         pl.BlockSpec((HALF, CHUNK), half),
         pl.BlockSpec(memory_space=pltpu.VMEM),
     ]
-    operands = [sp, count, cov, chg, cols, x, got]
+    operands = [info, cov, chg, cols, x, got]
     aliases = {}
     if out is not None:
         in_specs.append(pl.BlockSpec(memory_space=pl.ANY))
@@ -327,7 +329,7 @@
     return pl.pallas_call(
         lambda *refs: update_kernel(begin, *refs),
         grid_spec=pltpu.PrefetchScalarGridSpec(
-            num_scalar_prefetch=2,
+            num_scalar_prefetch=1,
             grid=(steps,),
             in_specs=in_specs,
             out_specs=[
@@ -410,16 +412,16 @@
     x, picked = lax.optimization_barrier((x, picked))
     two, one, three = (along_row(picked, bits) for bits in (2, 1, 3))
     got = swapped(x)
-    picks, cols, w, count = places(sp, segment, place, damping, extent)
+    picks, cols, w, info = places(sp, segment, place, damping, extent)
     near = picked + one + two + three
-    near, picks, cols, w, count = lax.optimization_barrier((near, picks, cols, w, count))
+    near, picks, cols, w, info = lax.optimization_barrier((near, picks, cols, w, info))
     far = near + across_rows(near, 0) + across_rows(near, 1)
     cov, chg = stats(far, swapped(far), readings, spread, picks, w)
     out = None
     away = []
     begin = 0
     for steps in PARTS:
-        out, part = update(begin, steps, sp, count, cov, chg, cols, x, got, out)
+        out, part = update(begin, steps, info, cov, chg, cols, x, got, out)
         away.append((begin, swapped(part)))
         begin += steps
     for some in (away[:-1], away[-1:]):

time: 40.6 us -> 39.2 us (0.966)
  Pallas kernels: 19.5 us -> 18 us
    pallas_call x2, Pallas kernels: 11.6 us -> 10.2 us  [update(): pl.pallas_call(lambda *refs: update_kernel(begin, *refs), grid_spec=pltpu...]
  transfers between devices with their start and end apart: 9 -> 9, of which waited for: 5 -> 5; matrix products, arithmetic and copies ran while one was open for 0% -> 0% of each run, Pallas kernels for 20% -> 19%
where the time goes in v8:
time: 39.2 us; the launch traced here: 38.5 us
  Pallas kernels  18 us (46%)
  starting transfers between devices  13.1 us (33%)
  waiting for transfers between devices  6.48 us (17%)
  other arithmetic  0.85 us (2%)
    pallas_call x2, Pallas kernels, update(): pl.pallas_call(lambda *refs: update_kernel(begin, *refs), grid_spec=pltpu...  10.2 us
    ppermute x5, starting transfers between devices, sent(): lax.ppermute(array, 'state', [(i, j) for i, j in pairs if 0 <= j < CHIPS])  8.75 us
    ppermute x5, waiting for transfers between devices, sent(): lax.ppermute(array, 'state', [(i, j) for i, j in pairs if 0 <= j < CHIPS])  4.98 us
    ppermute x4, starting transfers between devices, swapped(): return lax.ppermute(array, 'mem', [(0, 1), (1, 0)])  4.34 us
    pallas_call x1, Pallas kernels, pick(): pl.pallas_call(pick_kernel, grid_spec=pltpu.PrefetchScalarGridSpec(num_sc...  3.29 us
    pallas_call x2, Pallas kernels, fill(): pl.pallas_call(kernel, in_specs=[pl.BlockSpec(memory_space=pltpu.VMEM)] *...  2.16 us
    pallas_call x1, Pallas kernels, places(): pl.pallas_call(places_kernel, grid_spec=pltpu.PrefetchScalarGridSpec(num_...  1.56 us
    ppermute x4, waiting for transfers between devices, swapped(): return lax.ppermute(array, 'mem', [(0, 1), (1, 0)])  1.5 us
  transfers between devices with their start and end apart: 9, of which 5 were waited for; matrix products, arithmetic and copies ran while one was open for 0% of the time, Pallas kernels for 19%

profile of v8, /device:TPU:9, one launch (start us, length us, event | category | flops | bytes accessed | tf_op | source)
XLA Modules:
  0.0 38.5 jit_solution(17203422648010205017)
XLA Ops:
  0.0 0.7 %multiply_add_fusion.index_ref = s32[2,256]{1,0:T(2,128)S(1)} fusion(s32[2,256]{1,0:T(2,128)} %place_ref.1, s32[2,256]{1,0:T(2,128)} %seg_ref.1), kind=kLoop, calls=%fused_computation.2 | loop fusion | flops 1024 | bytes 6144 | tf_op jit(solution)/shard_map/add | solution.py:411
  0.8 0.1 pad_add_fusion.sp_ref
  0.9 3.3 %pick.1 = bf16[40,512]{1,0:T(8,128)(2,1)S(1)} custom-call(s32[3]{0:T(128)S(1)} %pad_add_fusion.sp_ref, s32[2,256]{1,0:T(2,128)S(1)} %multiply_add_fusion.index_ref, bf16[40,65536]{1,0:T(8,128)(2,1)} %refs_4_.1), custom_call_target="tpu_custom_call" | custom-call | bytes 5242880 | tf_op jit(solution)/shard_map/pick/pallas_call | solution.py:99
  4.2 0.8 %collective-permute-start.6 = (bf16[40,65536]{1,0:T(8,128)(2,1)}, bf16[40,65536]{1,0:T(8,128)(2,1)S(1)}, u32[]{:S(2)}, u32[]{:S(2)}) collective-permute-start(bf16[40,65536]{1,0:T(8,128)(2,1)} %refs_4_.1), channel_id=1, source_target_pairs={{0,64},{64,0},{1,65},{65,1},{2,66},{66,2},{3,67},{67,3},{4,68},{68... | collective-permute-start | bytes 15728648 | tf_op jit(solution)/shard_map/ppermute | solution.py:403
  4.9 3.8 %collective-permute-start.2 = (bf16[40,512]{1,0:T(8,128)(2,1)S(1)}, bf16[40,512]{1,0:T(8,128)(2,1)S(1)}, u32[]{:S(2)}, u32[]{:S(2)}) collective-permute-start(bf16[40,512]{1,0:T(8,128)(2,1)S(1)} %pick.1), channel_id=1, source_target_pairs={{0,3},{1,2},{2,1},{3,0},{4,7},{5,6},{6,5},{7,4},{8,11},{9,10},{10,... | collective-permute-start | bytes 122888 | tf_op jit(solution)/shard_map/ppermute | solution.py:387
  8.7 0.0 collective-permute-start.1
  8.7 0.6 %collective-permute-start = (bf16[40,512]{1,0:T(8,128)(2,1)S(1)}, bf16[40,512]{1,0:T(8,128)(2,1)S(1)}, u32[]{:S(2)}, u32[]{:S(2)}) collective-permute-start(bf16[40,512]{1,0:T(8,128)(2,1)S(1)} %pick.1), channel_id=1, source_target_pairs={{0,1},{1,0},{2,3},{3,2},{4,5},{5,4},{6,7},{7,6},{8,9},{9,8},{10,11... | collective-permute-start | bytes 122888 | tf_op jit(solution)/shard_map/ppermute | solution.py:387
  9.3 1.6 %places.1 = (bf16[2,256,256]{2,1,0:T(8,128)(2,1)S(1)}, f32[2,3,256,128]{3,2,1,0:T(8,128)S(1)}, f32[256,256]{1,0:T(8,128)S(1)}, s32[3]{0:T(128)S(1)}) custom-call(s32[3]{0:T(128)S(1)} %pad_add_fusion.sp_ref, s32[2,256]{1,0:T(2,128)S(1)} %copy-done, s32[2,256]{1,0:T(2,128)S(1)} %copy-done.1, f32[2,256]{1,0:T(2,128)S(1)} %copy-done.4, s32[2,256]{1,0:T(2,128)S(1)} %copy-done.5), custom_call_target="tpu_custom_call" | custom-call | flops 1000000 | bytes 2000000 | tf_op jit(solution)/shard_map/places/pallas_call | solution.py:156
  10.8 0.0 collective-permute-done.2
  10.9 2.2 %collective-permute-done.1 = bf16[40,512]{1,0:T(8,128)(2,1)S(1)} collective-permute-done((bf16[40,512]{1,0:T(8,128)(2,1)S(1)}, bf16[40,512]{1,0:T(8,128)(2,1)S(1)}, u32[]{:S(2)}, u32[]{:S(2)}) %collective-permute-start.1) | collective-permute-done | bytes 40992 | tf_op jit(solution)/shard_map/ppermute | solution.py:387
  13.1 4.3 %collective-permute-start.4 = (bf16[40,512]{1,0:T(8,128)(2,1)S(1)}, bf16[40,512]{1,0:T(8,128)(2,1)S(1)}, u32[]{:S(2)}, u32[]{:S(2)}) collective-permute-start(bf16[40,512]{1,0:T(8,128)(2,1)S(1)} %add_add_fusion.1), channel_id=1, source_target_pairs={{4,8},{5,9},{6,10},{7,11},{8,4},{9,5},{10,6},{11,7},{12,16},{13,17... | collective-permute-start | bytes 122888 | tf_op jit(solution)/shard_map/ppermute | solution.py:387
  17.3 0.1 collective-permute-start.3
  17.5 2.4 %collective-permute-done.4 = bf16[40,512]{1,0:T(8,128)(2,1)S(1)} collective-permute-done((bf16[40,512]{1,0:T(8,128)(2,1)S(1)}, bf16[40,512]{1,0:T(8,128)(2,1)S(1)}, u32[]{:S(2)}, u32[]{:S(2)}) %collective-permute-start.4) | collective-permute-done | bytes 40992 | tf_op jit(solution)/shard_map/ppermute | solution.py:387
  19.9 0.4 collective-permute-done.3
  20.3 3.1 %collective-permute-start.5 = (bf16[40,512]{1,0:T(8,128)(2,1)S(1)}, bf16[40,512]{1,0:T(8,128)(2,1)S(1)}, u32[]{:S(2)}, u32[]{:S(2)}) collective-permute-start(bf16[40,512]{1,0:T(8,128)(2,1)S(1)} %add_add_fusion.mine_ref), channel_id=1, source_target_pairs={{0,64},{64,0},{1,65},{65,1},{2,66},{66,2},{3,67},{67,3},{4,68},{68... | collective-permute-start | bytes 122888 | tf_op jit(solution)/shard_map/ppermute | solution.py:403
  23.4 0.9 %collective-permute-done.5.other_ref = bf16[40,512]{1,0:T(8,128)(2,1)S(1)} collective-permute-done((bf16[40,512]{1,0:T(8,128)(2,1)S(1)}, bf16[40,512]{1,0:T(8,128)(2,1)S(1)}, u32[]{:S(2)}, u32[]{:S(2)}) %collective-permute-start.5) | collective-permute-done | bytes 40992 | tf_op jit(solution)/shard_map/ppermute | solution.py:403
  24.2 0.8 %stats.1 = (bf16[2,256,96]{2,1,0:T(8,128)(2,1)S(1)}, bf16[2,80,256]{2,1,0:T(8,128)(2,1)S(1)}) custom-call(bf16[40,512]{1,0:T(8,128)(2,1)S(1)} %add_add_fusion.mine_ref, bf16[40,512]{1,0:T(8,128)(2,1)S(1)} %collective-permute-done.5.other_ref, f32[2,256]{1,0:T(2,128)S(1)} %copy-done.2, f32[2,256]{1,0:T(2,128)S(1)} %copy-done.3, ...), custom_call_target="tpu_custom_call" | custom-call | tf_op jit(solution)/shard_map/stats/pallas_call | solution.py:218
  25.0 6.5 %update0.1 = (bf16[40,65536]{1,0:T(8,128)(2,1)}, bf16[40,24576]{1,0:T(8,128)(2,1)S(1)}) custom-call(s32[3]{0:T(128)S(1)} %get-tuple-element.27.refs_0_, bf16[2,256,96]{2,1,0:T(8,128)(2,1)S(1)} %get-tuple-element.31.refs_1_, bf16[2,80,256]{2,1,0:T(8,128)(2,1)S(1)} %get-tuple-element.32.refs_2_, f32[2,3,256,128]{3,2,1,0:T(8,128)S(1)} %get-tuple-element.33.refs_3_, ...), custom_call_target="tpu_custom_call" | custom-call | flops 1800000000 | bytes 7864320 | tf_op jit(solution)/shard_map/update0/pallas_call | solution.py:329
  31.5 0.3 collective-permute-start.8
  31.8 3.8 %update3.1 = (bf16[40,65536]{1,0:T(8,128)(2,1)}, bf16[40,8192]{1,0:T(8,128)(2,1)S(1)}) custom-call(s32[3]{0:T(128)S(1)} %get-tuple-element.27.refs_0_, bf16[2,256,96]{2,1,0:T(8,128)(2,1)S(1)} %get-tuple-element.31.refs_1_, bf16[2,80,256]{2,1,0:T(8,128)(2,1)S(1)} %get-tuple-element.32.refs_2_, ...), custom_call_target="tpu_custom_call", output_to_operand_aliasing={{0}: (6, {})} | custom-call | flops 600000000 | bytes 2621440 | tf_op jit(solution)/shard_map/update3/pallas_call | solution.py:329
  35.6 0.2 collective-permute-start.7
  35.8 1.3 %fill0.1.refs_1_ = bf16[40,65536]{1,0:T(8,128)(2,1)} custom-call(bf16[40,24576]{1,0:T(8,128)(2,1)S(1)} %collective-permute-done.8.refs_0_, bf16[40,65536]{1,0:T(8,128)(2,1)} %get-tuple-element.38.refs_1_), custom_call_target="tpu_custom_call", output_to_operand_aliasing={{}: (1, {})} | custom-call | tf_op jit(solution)/shard_map/fill0/pallas_call | solution.py:372
  37.1 0.6 %collective-permute-done.7.refs_0_ = bf16[40,8192]{1,0:T(8,128)(2,1)S(1)} collective-permute-done((bf16[40,8192]{1,0:T(8,128)(2,1)S(1)}, bf16[40,8192]{1,0:T(8,128)(2,1)S(1)}, u32[]{:S(2)}, u32[]{:S(2)}) %collective-permute-start.7) | collective-permute-done | bytes 655392 | tf_op jit(solution)/shard_map/ppermute | solution.py:403
  37.7 0.9 %fill3.1 = bf16[40,65536]{1,0:T(8,128)(2,1)} custom-call(bf16[40,8192]{1,0:T(8,128)(2,1)S(1)} %collective-permute-done.7.refs_0_, bf16[40,65536]{1,0:T(8,128)(2,1)} %fill0.1.refs_1_), custom_call_target="tpu_custom_call", output_to_operand_aliasing={{}: (1, {})} | custom-call | tf_op jit(solution)/shard_map/fill3/pallas_call | solution.py:372
  (17 shorter events, 0.1 us)
Async XLA Ops:
  0.0 9.3 %copy-start.1 = (s32[2,256]{1,0:T(2,128)S(1)}, s32[2,256]{1,0:T(2,128)}, u32[]{:S(2)}) copy-start(s32[2,256]{1,0:T(2,128)} %place_ref.1) | copy-start | bytes 6148
  0.0 9.3 %copy-start = (s32[2,256]{1,0:T(2,128)S(1)}, s32[2,256]{1,0:T(2,128)}, u32[]{:S(2)}) copy-start(s32[2,256]{1,0:T(2,128)} %seg_ref.1) | copy-start | bytes 6148
  0.0 9.3 %copy-start.5 = (s32[2,256]{1,0:T(2,128)S(1)}, s32[2,256]{1,0:T(2,128)}, u32[]{:S(2)}) copy-start(s32[2,256]{1,0:T(2,128)} %ext_ref.1) | copy-start | bytes 6148
  0.0 9.3 %copy-start.4 = (f32[2,256]{1,0:T(2,128)S(1)}, f32[2,256]{1,0:T(2,128)}, u32[]{:S(2)}) copy-start(f32[2,256]{1,0:T(2,128)} %damp_ref.1) | copy-start | bytes 6148
  0.0 24.2 %copy-start.3 = (f32[2,256]{1,0:T(2,128)S(1)}, f32[2,256]{1,0:T(2,128)}, u32[]{:S(2)}) copy-start(f32[2,256]{1,0:T(2,128)} %var_ref.1) | copy-start | bytes 6148
  0.0 24.2 %copy-start.2 = (f32[2,256]{1,0:T(2,128)S(1)}, f32[2,256]{1,0:T(2,128)}, u32[]{:S(2)}) copy-start(f32[2,256]{1,0:T(2,128)} %val_ref.1) | copy-start | bytes 6148
  4.2 20.8 %collective-permute-start.6 = (bf16[40,65536]{1,0:T(8,128)(2,1)}, bf16[40,65536]{1,0:T(8,128)(2,1)S(1)}, u32[]{:S(2)}, u32[]{:S(2)}) collective-permute-start(bf16[40,65536]{1,0:T(8,128)(2,1)} %refs_4_.1), channel_id=1, source_target_pairs={{0,64},{64,0},{1,65},{65,1},{2,66},{66,2},{3,67},{67,3},{4,68},{68... | collective-permute-start | bytes 15728648 | tf_op jit(solution)/shard_map/ppermute | solution.py:403
  4.9 5.9 %collective-permute-start.2 = (bf16[40,512]{1,0:T(8,128)(2,1)S(1)}, bf16[40,512]{1,0:T(8,128)(2,1)S(1)}, u32[]{:S(2)}, u32[]{:S(2)}) collective-permute-start(bf16[40,512]{1,0:T(8,128)(2,1)S(1)} %pick.1), channel_id=1, source_target_pairs={{0,3},{1,2},{2,1},{3,0},{4,7},{5,6},{6,5},{7,4},{8,11},{9,10},{10,... | collective-permute-start | bytes 122888 | tf_op jit(solution)/shard_map/ppermute | solution.py:387
  8.7 4.4 %collective-permute-start.1 = (bf16[40,512]{1,0:T(8,128)(2,1)S(1)}, bf16[40,512]{1,0:T(8,128)(2,1)S(1)}, u32[]{:S(2)}, u32[]{:S(2)}) collective-permute-start(bf16[40,512]{1,0:T(8,128)(2,1)S(1)} %pick.1), channel_id=1, source_target_pairs={{0,2},{1,3},{2,0},{3,1},{4,6},{5,7},{6,4},{7,5},{8,10},{9,11},{10,... | collective-permute-start | bytes 122888 | tf_op jit(solution)/shard_map/ppermute | solution.py:387
  8.7 4.4 %collective-permute-start = (bf16[40,512]{1,0:T(8,128)(2,1)S(1)}, bf16[40,512]{1,0:T(8,128)(2,1)S(1)}, u32[]{:S(2)}, u32[]{:S(2)}) collective-permute-start(bf16[40,512]{1,0:T(8,128)(2,1)S(1)} %pick.1), channel_id=1, source_target_pairs={{0,1},{1,0},{2,3},{3,2},{4,5},{5,4},{6,7},{7,6},{8,9},{9,8},{10,11... | collective-permute-start | bytes 122888 | tf_op jit(solution)/shard_map/ppermute | solution.py:387
  13.1 6.9 %collective-permute-start.4 = (bf16[40,512]{1,0:T(8,128)(2,1)S(1)}, bf16[40,512]{1,0:T(8,128)(2,1)S(1)}, u32[]{:S(2)}, u32[]{:S(2)}) collective-permute-start(bf16[40,512]{1,0:T(8,128)(2,1)S(1)} %add_add_fusion.1), channel_id=1, source_target_pairs={{4,8},{5,9},{6,10},{7,11},{8,4},{9,5},{10,6},{11,7},{12,16},{13,17... | collective-permute-start | bytes 122888 | tf_op jit(solution)/shard_map/ppermute | solution.py:387
  17.3 2.9 %collective-permute-start.3 = (bf16[40,512]{1,0:T(8,128)(2,1)S(1)}, bf16[40,512]{1,0:T(8,128)(2,1)S(1)}, u32[]{:S(2)}, u32[]{:S(2)}) collective-permute-start(bf16[40,512]{1,0:T(8,128)(2,1)S(1)} %add_add_fusion.1), channel_id=1, source_target_pairs={{0,4},{1,5},{2,6},{3,7},{4,0},{5,1},{6,2},{7,3},{8,12},{9,13},{10,... | collective-permute-start | bytes 122888 | tf_op jit(solution)/shard_map/ppermute | solution.py:387
  20.3 3.9 %collective-permute-start.5 = (bf16[40,512]{1,0:T(8,128)(2,1)S(1)}, bf16[40,512]{1,0:T(8,128)(2,1)S(1)}, u32[]{:S(2)}, u32[]{:S(2)}) collective-permute-start(bf16[40,512]{1,0:T(8,128)(2,1)S(1)} %add_add_fusion.mine_ref), channel_id=1, source_target_pairs={{0,64},{64,0},{1,65},{65,1},{2,66},{66,2},{3,67},{67,3},{4,68},{68... | collective-permute-start | bytes 122888 | tf_op jit(solution)/shard_map/ppermute | solution.py:403
  31.5 4.3 %collective-permute-start.8 = (bf16[40,24576]{1,0:T(8,128)(2,1)S(1)}, bf16[40,24576]{1,0:T(8,128)(2,1)S(1)}, u32[]{:S(2)}, u32[]{:S(2)}) collective-permute-start(bf16[40,24576]{1,0:T(8,128)(2,1)S(1)} %get-tuple-element.37), channel_id=1, source_target_pairs={{0,64},{64,0},{1,65},{65,1},{2,66},{66,2},{3,67},{67,3},{4,68},{68... | collective-permute-start | bytes 5898248 | tf_op jit(solution)/shard_map/ppermute | solution.py:403
  35.6 2.1 %collective-permute-start.7 = (bf16[40,8192]{1,0:T(8,128)(2,1)S(1)}, bf16[40,8192]{1,0:T(8,128)(2,1)S(1)}, u32[]{:S(2)}, u32[]{:S(2)}) collective-permute-start(bf16[40,8192]{1,0:T(8,128)(2,1)S(1)} %get-tuple-element.36), channel_id=1, source_target_pairs={{0,64},{64,0},{1,65},{65,1},{2,66},{66,2},{3,67},{67,3},{4,68},{68... | collective-permute-start | bytes 1966088 | tf_op jit(solution)/shard_map/ppermute | solution.py:403
